TPU v7x, 256 devices: a whole 4x4x8 slice. The times are simulated.
256 devices in a mesh: dp: 8 (over y_hi, x), ctx: 32 (over y_lo, z, core).
Axes of the slice: x: 4, y: 4 (y_hi: 2, y_lo: 2; y = y_hi * 2 + y_lo), z: 8, core: 2. Of those that a mesh axis runs over, the one named last changes fastest.
Arguments:
- mixed: bfloat16 [8192, 4096], P('ctx', 'dp'), may hold values from -6 to 6
- log_decay: float32 [8192, 16], P('ctx', 'dp'), may hold values from -1 to 0
- beta_logit: float32 [8192, 16], P('ctx', 'dp'), may hold values from -4 to 4
- conv_weight: float32 [4, 4096], P(None, 'dp'), may hold values from -3 to 3
- norm_gain: float32 [128], replicated, may hold values from 0.1 to 1.9
- out_weight: bfloat16 [2048, 1024], P('dp'), may hold values from -0.125 to 0.125
- out_grad: bfloat16 [8192, 1024], P(('ctx', 'dp')), may hold values from -12 to 12
Outputs:
- output: bfloat16 [8192, 1024], P(('ctx', 'dp'))
- grad_mixed: bfloat16 [8192, 4096], P('ctx', 'dp')
- grad_log_decay: float32 [8192, 16], P('ctx', 'dp')
- grad_beta_logit: float32 [8192, 16], P('ctx', 'dp')
- grad_conv_weight: float32 [4, 4096], P(None, 'dp')
- grad_norm_gain: float32 [128], replicated
- grad_out_weight: float32 [2048, 1024], P(('dp', 'ctx'))
All inputs are finite; a program needn't handle non-finite values.
Results may differ from a plain program's by a relative error of at most 0.03.
Values may be sent and summed in bfloat16 or wider, within the bound.
No kernel may reach another device: no remote copies, remote signals or barrier semaphores. Data moves between devices by JAX's collectives and lax.ppermute only.
A program may use at most 128 MiB of HBM per device.

v0:
```python
import math

import jax
import jax.numpy as jnp
from jax import lax
from jax.sharding import PartitionSpec as P

VHEADS = 16
KHEADS = 8
HEADDIM = 128
BLOCK = 64


EPS = 1e-06
HIGHEST = lax.Precision.HIGHEST


def shifted(block, axis, distance):
    devices = range(lax.axis_size(axis))
    route = [(i - distance, i) for i in devices if i - distance in devices]
    return lax.ppermute(block, axis, route)


def prefix_2(value, axis, join, neutral, backward):
    count, mine = (lax.axis_size(axis), lax.axis_index(axis))
    pieces = jax.tree.map(lambda part: lax.all_gather(part, axis), value)
    if backward:
        pieces = jax.tree.map(lambda part: part[::-1], pieces)
        mine = count - 1 - mine
    total = jax.tree.map(
        lambda part, zero: jnp.full_like(part, 0) + jnp.asarray(zero, part.dtype), value, neutral
    )

    def step(position, total):
        longer = join(total, jax.tree.map(lambda part: part[position], pieces))
        return jax.tree.map(lambda new, old: jnp.where(position < mine, new, old), longer, total)

    return lax.fori_loop(0, count - 1, step, total)


def product(pattern, left_array, right_array):
    return jnp.einsum(pattern, left_array, right_array, precision=HIGHEST)


def conv_silu(padded_rows, conv_weight):
    conv_taps = conv_weight.shape[0]
    row_count = padded_rows.shape[0] - (conv_taps - 1)
    summed = jnp.zeros((row_count, padded_rows.shape[1]), jnp.float32)
    for offset in range(conv_taps):
        summed = summed + conv_weight[offset] * padded_rows[offset : offset + row_count]
    return jax.nn.silu(summed)


def unit_rows(vectors):
    return vectors * lax.rsqrt(jnp.sum(vectors * vectors, axis=-1, keepdims=True) + EPS)


def prepare(active, decays, strengths):
    row_count = active.shape[0]
    value_heads = decays.shape[1]
    group_size = VHEADS // KHEADS
    key_heads = value_heads // group_size
    grouped = active.reshape(row_count, key_heads, (2 + group_size) * HEADDIM)
    queries = unit_rows(grouped[:, :, :HEADDIM]) * (1.0 / math.sqrt(HEADDIM))
    key_rows = unit_rows(grouped[:, :, HEADDIM : 2 * HEADDIM])
    values = grouped[:, :, 2 * HEADDIM :].reshape(row_count, value_heads, HEADDIM)
    queries = jnp.repeat(queries, group_size, axis=1)
    key_rows = jnp.repeat(key_rows, group_size, axis=1)
    blocks = row_count // BLOCK

    def arrange(tensor):
        return jnp.transpose(tensor.reshape(blocks, BLOCK, value_heads, -1), (0, 2, 1, 3))

    return (
        arrange(queries),
        arrange(key_rows),
        arrange(values),
        arrange(decays[:, :, None])[..., 0],
        arrange(jax.nn.sigmoid(strengths)[:, :, None])[..., 0],
    )


def block_terms(block_in):
    queries, key_rows, values, decays, strengths = (
        block_in[0],
        block_in[1],
        block_in[2],
        block_in[3],
        block_in[4],
    )
    length = decays.shape[-1]
    cumulative = jnp.cumsum(decays, axis=-1)
    row_index = lax.broadcasted_iota(jnp.int32, (length, length), 0)
    col_index = lax.broadcasted_iota(jnp.int32, (length, length), 1)
    causal = row_index >= col_index
    strict = row_index > col_index
    spread = cumulative[:, :, None] - cumulative[:, None, :]
    damping = jnp.where(causal, jnp.exp(jnp.where(causal, spread, 0.0)), 0.0)
    key_inner = product("hck,hsk->hcs", key_rows, key_rows)
    lower_mat = jnp.where(strict, strengths[:, :, None] * damping * key_inner, 0.0)
    growth = jnp.exp(cumulative)
    tail_keys = jnp.exp(cumulative[:, -1:] - cumulative)[..., None] * key_rows
    stacked = jnp.concatenate(
        [(strengths * growth)[..., None] * key_rows, strengths[..., None] * values], axis=-1
    )
    solved = lax.linalg.triangular_solve(
        lower_mat, stacked, left_side=True, lower=True, unit_diagonal=True
    )
    head_size = key_rows.shape[-1]
    write_keys = solved[..., :head_size]
    new_values = solved[..., head_size:]
    scores = damping * product("hck,hsk->hcs", queries, key_rows)
    return (write_keys, new_values, scores, growth, tail_keys, queries, growth[:, -1])


def rows_layout(stacked):
    return jnp.transpose(stacked, (0, 2, 1, 3)).reshape(
        stacked.shape[0] * stacked.shape[2], stacked.shape[1], stacked.shape[3]
    )


def run_blocks(carry_state, arranged):

    def run_advance(running, block_in):
        write_keys, new_values, scores, growth, tail_keys, queries, growth_end = block_terms(
            block_in
        )
        deltas = new_values - product("hck,hek->hce", write_keys, running)
        output = growth[..., None] * product("hck,hek->hce", queries, running) + product(
            "hcs,hse->hce", scores, deltas
        )
        next_state = growth_end[:, None, None] * running + product(
            "hse,hsk->hek", deltas, tail_keys
        )
        return (next_state, output)

    final_state, outputs = lax.scan(run_advance, carry_state, arranged)
    return (rows_layout(outputs), final_state)


def local_core(carry_state, active, decays, strengths):
    return run_blocks(carry_state, prepare(active, decays, strengths))


def eye_stack(value_heads):
    return jnp.broadcast_to(jnp.eye(HEADDIM, dtype=jnp.float32), (value_heads, HEADDIM, HEADDIM))


def local_pieces(active, decays, strengths):
    identity = eye_stack(decays.shape[1])
    start_carry = (identity, jnp.zeros((decays.shape[1], HEADDIM, HEADDIM), jnp.float32))

    def local_advance(running, block_in):
        through, offset_state = running
        write_keys, new_values, scores, growth, tail_keys, queries, growth_end = block_terms(
            block_in
        )
        effective = growth[..., None] * queries - product("hcs,hsk->hck", scores, write_keys)
        local_out = product("hck,hek->hce", effective, offset_state) + product(
            "hcs,hse->hce", scores, new_values
        )
        reach_rows = product("hck,hjk->hcj", effective, through)
        block_map = growth_end[:, None, None] * identity - product(
            "hsk,hsj->hkj", write_keys, tail_keys
        )
        block_add = product("hse,hsk->hek", new_values, tail_keys)
        through = product("hjk,hkl->hjl", through, block_map)
        offset_state = product("hek,hkl->hel", offset_state, block_map) + block_add
        return ((through, offset_state), (local_out, reach_rows))

    final_pair, outputs = lax.scan(local_advance, start_carry, prepare(active, decays, strengths))
    return (rows_layout(outputs[0]), rows_layout(outputs[1]), final_pair[0], final_pair[1])


def normalize(mixer_out, gain_vector):
    scaled = (
        mixer_out
        * lax.rsqrt(jnp.mean(mixer_out * mixer_out, axis=-1, keepdims=True) + EPS)
        * gain_vector
    )
    return scaled.reshape(mixer_out.shape[0], -1)


def chain_step(earlier_pair, later_pair):
    return (
        product("hjk,hkl->hjl", earlier_pair[0], later_pair[0]),
        product("hek,hkl->hel", earlier_pair[1], later_pair[0]) + later_pair[1],
    )


def local(mixed, log_decay, beta_logit, conv_weight, norm_gain, out_weight, out_grad):
    conv_taps = conv_weight.shape[0]
    row_count = mixed.shape[0]
    value_heads = log_decay.shape[1]
    rim_rows = shifted(mixed[row_count - (conv_taps - 1) :], "ctx", 1)
    padded = jnp.concatenate([rim_rows, mixed], axis=0).astype(jnp.float32)
    active_wide, conv_pull = jax.vjp(conv_silu, padded, conv_weight)
    active = lax.optimization_barrier(active_wide.astype(jnp.bfloat16)).astype(jnp.float32)
    start_pair = (eye_stack(value_heads), jnp.zeros((value_heads, HEADDIM, HEADDIM), jnp.float32))
    pieces_out = local_pieces(active, log_decay, beta_logit)
    chain_maps, chain_adds = (pieces_out[2], pieces_out[3])
    prefix = prefix_2((chain_maps, chain_adds), "ctx", chain_step, start_pair, False)
    entry_state = prefix[1]
    core_out, core_pull = jax.vjp(local_core, entry_state, active, log_decay, beta_logit)
    mixer_out, leaving = core_out
    normed_wide, norm_pull = jax.vjp(normalize, mixer_out, norm_gain)
    normed = normed_wide.astype(jnp.bfloat16)
    result = lax.psum_scatter(
        jnp.dot(normed, out_weight, preferred_element_type=jnp.float32).astype(jnp.bfloat16),
        "dp",
        scatter_dimension=0,
        tiled=True,
    )
    full_grad = lax.all_gather(out_grad, "dp", axis=0, tiled=True)
    back_rows = jnp.dot(full_grad, out_weight.T, preferred_element_type=jnp.float32)
    grad_weight = lax.psum_scatter(
        jnp.einsum("tv,td->vd", normed, full_grad, preferred_element_type=jnp.float32).astype(
            jnp.bfloat16
        ),
        "ctx",
        scatter_dimension=0,
        tiled=True,
    ).astype(jnp.float32)
    grad_mixer, grad_gain = norm_pull(back_rows)
    local_grad = core_pull((grad_mixer, jnp.zeros_like(leaving)))[0]
    suffix = prefix_2(
        (jnp.swapaxes(chain_maps, 1, 2), local_grad), "ctx", chain_step, start_pair, True
    )
    exit_grad = suffix[1]
    core_grads = core_pull((grad_mixer, exit_grad))
    grad_active, grad_decay, grad_beta = (core_grads[1], core_grads[2], core_grads[3])
    grad_padded, grad_conv = conv_pull(grad_active)
    spill_rows = shifted(grad_padded[: conv_taps - 1], "ctx", -1)
    own_rows = grad_padded[conv_taps - 1 :]
    own_rows = own_rows.at[row_count - (conv_taps - 1) :].add(spill_rows)
    grad_conv_total, gain_partial = lax.psum((grad_conv, grad_gain), "ctx")
    grad_gain_total = lax.psum(gain_partial, "dp")
    return (
        result,
        own_rows.astype(jnp.bfloat16),
        grad_decay,
        grad_beta,
        grad_conv_total,
        grad_gain_total,
        grad_weight,
    )


def solution(mesh):
    return jax.shard_map(
        local,
        mesh=mesh,
        in_specs=(
            P("ctx", "dp"),
            P("ctx", "dp"),
            P("ctx", "dp"),
            P(None, "dp"),
            P(),
            P("dp", None),
            P(("ctx", "dp"), None),
        ),
        out_specs=(
            P(("ctx", "dp"), None),
            P("ctx", "dp"),
            P("ctx", "dp"),
            P("ctx", "dp"),
            P(None, "dp"),
            P(),
            P(("dp", "ctx"), None),
        ),
        check_vma=False,
    )
```

profile of v0, /device:TPU:8, one launch (start us, length us, event | category | flops | bytes accessed | tf_op | source)
XLA Modules:
  0.0 858.3 jit_solution(8584469403035977819)
XLA Ops:
  8.0 1.9 collective-permute-start
  12.5 3.9 collective-permute-done
  20.2 52.3 %while.145 = (s32[]{:T(128)}, f32[2,128,128]{1,2,0:T(8,128)S(1)}, f32[2,128,128]{1,2,0:T(8,128)S(1)}, f32[4,2,64]{2,1,0:T(2,128)S(1)}, f32[4,2,64]{2,1,0:T(2,128...) while((s32[]{:T(128)}, f32[2,128,128]{1,2,0:T(8,128)S(1)}, ...), condition=%wide.region_3.5_spmd.clone, body=%wide.region_1.4_spmd.clone.sunk | while | flops 189067456 | bytes 2523331 | solution.py:171
  21.2 9.8 %custom-call.44 = f32[2,1,64,64]{2,3,1,0:T(8,128)S(1)} custom-call(f32[2,1,64,64]{3,2,1,0:T(8,128)S(1)} %fusion.384), custom_call_target="InvertDiagBlocksLowerTriangular" | custom-call | tf_op jit(solution)/shard_map/while/body/eval_jaxpr/triangular_solve/custom-call.1 | solution.py:106
  34.3 9.8 %custom-call.44 = f32[2,1,64,64]{2,3,1,0:T(8,128)S(1)} custom-call(f32[2,1,64,64]{3,2,1,0:T(8,128)S(1)} %fusion.384), custom_call_target="InvertDiagBlocksLowerTriangular" | custom-call | tf_op jit(solution)/shard_map/while/body/eval_jaxpr/triangular_solve/custom-call.1 | solution.py:106
  47.3 9.8 %custom-call.44 = f32[2,1,64,64]{2,3,1,0:T(8,128)S(1)} custom-call(f32[2,1,64,64]{3,2,1,0:T(8,128)S(1)} %fusion.384), custom_call_target="InvertDiagBlocksLowerTriangular" | custom-call | tf_op jit(solution)/shard_map/while/body/eval_jaxpr/triangular_solve/custom-call.1 | solution.py:106
  60.4 9.8 %custom-call.44 = f32[2,1,64,64]{2,3,1,0:T(8,128)S(1)} custom-call(f32[2,1,64,64]{3,2,1,0:T(8,128)S(1)} %fusion.384), custom_call_target="InvertDiagBlocksLowerTriangular" | custom-call | tf_op jit(solution)/shard_map/while/body/eval_jaxpr/triangular_solve/custom-call.1 | solution.py:106
  74.3 35.2 %all_gather.33 = bf16[256,1024]{1,0:T(8,128)(2,1)S(1)} all-gather(bf16[32,1024]{1,0:T(8,128)(2,1)S(1)} %copy-done.9), channel_id=1, replica_groups=mesh['dp'=8,'ctx'=32] {'dp'}, dimensions={0}, use_global_device_ids=true | all-gather | bytes 589824 | tf_op jit(solution)/shard_map/all_gather | solution.py:214
  111.7 28.6 %all-gather.9.cloned.1.call-done = f32[64,128,128]{2,1,0:T(8,128)} async-done(((f32[2,128,128]{2,1,0:T(8,128)}), f32[64,128,128]{2,1,0:T(8,128)}) %all-gather.9.cloned.1.call-update) | async-done | bytes 4194320 | tf_op jit(solution)/shard_map/all_gather | solution.py:26
  140.3 68.5 %all-gather.11.cloned.1.call-done = f32[64,128,128]{2,1,0:T(8,128)} async-done(((f32[2,128,128]{2,1,0:T(8,128)}), f32[64,128,128]{2,1,0:T(8,128)}) %all-gather.11.cloned.1.call-update) | async-done | bytes 4194320 | tf_op jit(solution)/shard_map/all_gather | solution.py:26
  208.8 73.6 %while.146 = (s32[]{:T(128)}, f32[2,128,128]{1,2,0:T(8,128)S(1)}, s32[]{:T(128)}, f32[32,2,128,128]{3,2,1,0:T(8,128)}, f32[32,2,128,128]{3,2,1,0:T(8,128)}, /*index=5*/s32[]{:T(128)}, s32[]{:T(128)}) while((s32[]{:T(128)}, f32[2,128,128]{1,2,0:T(8,128)S(1)}, s32[]{:T(128)}, f32[32,2,128,128]{3,2,1,0:T(8,128)}, ...), condition=%wide.region_5.7_spmd.clone, body=%wide.region_4.6_spmd.clone.sunk | while | flops 50462724 | bytes 1443947 | solution.py:38
  287.1 97.9 %while.143 = (s32[]{:T(128)}, f32[2,128,128]{2,1,0:T(8,128)S(1)}, f32[4,2,64,128]{3,2,1,0:T(8,128)}, f32[4,2,64,64]{3,2,1,0:T(8,128)}, f32[4,2,64,64]{3,2,1,0:T(...) while((s32[]{:T(128)}, f32[2,128,128]{2,1,0:T(8,128)S(1)}, ...), condition=%wide.region_9.11_spmd.clone.clone, body=%wide.region_7.10_spmd.clone.clone.sunk | while | flops 138834496 | bytes 3687305 | solution.py:137
  292.7 11.2 %custom-call.42 = f32[2,1,64,64]{2,3,1,0:T(8,128)} custom-call(f32[2,1,64,64]{3,2,1,0:T(8,128)} %get-tuple-element.3230), custom_call_target="InvertDiagBlocksLowerTriangular" | custom-call | tf_op jit(solution)/shard_map/jvp()/while/body/eval_jaxpr/triangular_solve/custom-call.1 | solution.py:106
  303.9 1.8 bitcast_dynamic-update-slice_fusion.19
  317.2 11.2 %custom-call.42 = f32[2,1,64,64]{2,3,1,0:T(8,128)} custom-call(f32[2,1,64,64]{3,2,1,0:T(8,128)} %get-tuple-element.3230), custom_call_target="InvertDiagBlocksLowerTriangular" | custom-call | tf_op jit(solution)/shard_map/jvp()/while/body/eval_jaxpr/triangular_solve/custom-call.1 | solution.py:106
  328.4 1.8 bitcast_dynamic-update-slice_fusion.19
  341.6 11.2 %custom-call.42 = f32[2,1,64,64]{2,3,1,0:T(8,128)} custom-call(f32[2,1,64,64]{3,2,1,0:T(8,128)} %get-tuple-element.3230), custom_call_target="InvertDiagBlocksLowerTriangular" | custom-call | tf_op jit(solution)/shard_map/jvp()/while/body/eval_jaxpr/triangular_solve/custom-call.1 | solution.py:106
  352.8 1.8 bitcast_dynamic-update-slice_fusion.19
  366.1 11.2 %custom-call.42 = f32[2,1,64,64]{2,3,1,0:T(8,128)} custom-call(f32[2,1,64,64]{3,2,1,0:T(8,128)} %get-tuple-element.3230), custom_call_target="InvertDiagBlocksLowerTriangular" | custom-call | tf_op jit(solution)/shard_map/jvp()/while/body/eval_jaxpr/triangular_solve/custom-call.1 | solution.py:106
  377.3 1.8 bitcast_dynamic-update-slice_fusion.19
  390.1 2.2 convolution_convert_fusion
  392.4 18.6 %while.147 = (s32[]{:T(128)}, f32[2,128,128]{2,1,0:T(8,128)S(1)}, f32[4,2,1,1]{1,3,2,0:T(1,128)}, f32[4,2,64,1]{2,1,3,0:T(2,128)S(1)}, f32[4,2,64,128]{3,2,1,0:T...) while((s32[]{:T(128)}, f32[2,128,128]{2,1,0:T(8,128)S(1)}, ...), condition=%wide.region_14.16_spmd.clone, body=%wide.region_13.15_spmd.clone.sunk | while | flops 88293376 | bytes 1316019 | solution.py:137
  412.0 5.6 copy.142
  417.7 4.7 rev.6
  424.0 83.7 %reduce-scatter.5.cloned.1.call-done = bf16[8,1024]{1,0:T(8,128)(2,1)} async-done(((bf16[256,1024]{1,0:T(8,128)(2,1)}), bf16[8,1024]{1,0:T(8,128)(2,1)}) %reduce-scatter.5.cloned.1.call-update) | async-done | bytes 16400 | tf_op jit(solution)/shard_map/reduce_scatter | solution.py:216
  509.0 63.3 %all-gather.15.cloned.1.call-done = f32[64,128,128]{2,1,0:T(8,128)} async-done(((f32[2,128,128]{2,1,0:T(8,128)}), f32[64,128,128]{2,1,0:T(8,128)}) %all-gather.15.cloned.1.call-update) | async-done | bytes 4194320 | tf_op jit(solution)/shard_map/all_gather | solution.py:26
  572.4 5.6 copy.145
  578.0 4.7 rev.7
  582.6 40.0 %while.148 = (s32[]{:T(128)}, f32[2,128,128]{1,2,0:T(8,128)S(1)}, s32[]{:T(128)}, f32[32,2,128,128]{2,3,1,0:T(8,128)}, f32[32,2,128,128]{2,3,1,0:T(8,128)}, /*index=5*/s32[]{:T(128)}, s32[]{:T(128)}) while((s32[]{:T(128)}, f32[2,128,128]{1,2,0:T(8,128)S(1)}, s32[]{:T(128)}, f32[32,2,128,128]{2,3,1,0:T(8,128)}, ...), condition=%wide.region_16.18_spmd.clone, body=%wide.region_15.17_spmd.clone.sunk | while | flops 50462724 | bytes 920167 | solution.py:38
  624.9 133.3 %while.144 = (s32[]{:T(128)}, f32[2,128,128]{2,1,0:T(8,128)S(1)}, f32[4,2,64,128]{3,2,1,0:T(8,128)}, f32[4,2,64,128]{3,2,1,0:T(8,128)}, f32[4,2,64,128]{3,2,1,0:...) while((s32[]{:T(128)}, f32[2,128,128]{2,1,0:T(8,128)S(1)}, ...), condition=%wide.region_28.30_spmd.clone.clone, body=%wide.region_17.29_spmd.clone.clone.sunk | while | flops 283874368 | bytes 5498349 | solution.py:137
  627.6 1.5 add_bitcast_fusion.3
  629.1 10.6 %custom-call.43 = f32[2,1,64,64]{2,3,1,0:T(8,128)S(1)} custom-call(f32[2,1,64,64]{3,2,1,0:T(8,128)} %add_bitcast_fusion.3), custom_call_target="InvertDiagBlocksLowerTriangular" | custom-call | tf_op jit(solution)/shard_map/transpose(jvp())/while/body/eval_jaxpr/triangular_solve | solution.py:106
  645.5 1.7 fusion.359
  653.3 1.7 fusion.369
  660.9 1.5 add_bitcast_fusion.3
  662.4 10.6 %custom-call.43 = f32[2,1,64,64]{2,3,1,0:T(8,128)S(1)} custom-call(f32[2,1,64,64]{3,2,1,0:T(8,128)} %add_bitcast_fusion.3), custom_call_target="InvertDiagBlocksLowerTriangular" | custom-call | tf_op jit(solution)/shard_map/transpose(jvp())/while/body/eval_jaxpr/triangular_solve | solution.py:106
  678.9 1.7 fusion.359
  686.6 1.7 fusion.369
  695.7 10.6 %custom-call.43 = f32[2,1,64,64]{2,3,1,0:T(8,128)S(1)} custom-call(f32[2,1,64,64]{3,2,1,0:T(8,128)} %add_bitcast_fusion.3), custom_call_target="InvertDiagBlocksLowerTriangular" | custom-call | tf_op jit(solution)/shard_map/transpose(jvp())/while/body/eval_jaxpr/triangular_solve | solution.py:106
  712.1 1.7 fusion.359
  719.9 1.7 fusion.369
  729.0 10.6 %custom-call.43 = f32[2,1,64,64]{2,3,1,0:T(8,128)S(1)} custom-call(f32[2,1,64,64]{3,2,1,0:T(8,128)} %add_bitcast_fusion.3), custom_call_target="InvertDiagBlocksLowerTriangular" | custom-call | tf_op jit(solution)/shard_map/transpose(jvp())/while/body/eval_jaxpr/triangular_solve | solution.py:106
  745.5 1.7 fusion.359
  753.2 1.7 fusion.369
  763.2 1.5 multiply_reduce_fusion.3
  765.4 4.1 collective-permute-start.1
  770.9 55.8 %all-reduce.15 = (f32[4,512]{1,0:T(4,128)}, f32[128]{0:T(128)S(1)}) all-reduce(f32[4,512]{1,0:T(4,128)S(1)} %pad_add_fusion.5, f32[128]{0:T(128)S(1)} %copy-done.26), channel_id=1, replica_groups=mesh['dp'=8,'ctx'=32] {'ctx'}, use_global_device_ids=true, to_apply=%region_37.39 | all-reduce | flops 2176 | bytes 17408 | tf_op jit(solution)/shard_map/psum | solution.py:236
  826.7 23.8 %psum.23 = f32[128]{0:T(128)} all-reduce(f32[128]{0:T(128)S(1)} %get-tuple-element.2610), channel_id=1, replica_groups=mesh['dp'=8,'ctx'=32] {'dp'}, use_global_device_ids=true, to_apply=%region_41.43 | all-reduce | flops 128 | bytes 1024 | tf_op jit(solution)/shard_map/psum | solution.py:237
  (653 shorter events, 296.4 us)
Async XLA Ops:
  7.2 103.3 %copy-start = (bf16[256,1024]{1,0:T(8,128)(2,1)S(1)}, bf16[256,1024]{1,0:T(8,128)(2,1)}, u32[]{:S(2)}) copy-start(bf16[256,1024]{1,0:T(8,128)(2,1)} %param.28) | copy-start | bytes 1572868
  7.2 133.1 %all-gather.9.cloned.1.call-start = ((), (), s32[]{:S(2)}) async-start(), calls=%async_computation.4 | async-start | bytes 4325376 | tf_op jit(solution)/shard_map/all_gather | solution.py:26
  8.0 8.4 collective-permute-start
  11.5 7.5 copy-start.14
  11.5 7.5 copy-start.16
  11.5 7.5 copy-start.18
  11.5 8.7 %copy-start.12 = (f32[1,512]{1,0:T(1,128)}, f32[1,512]{1,0:T(1,128)S(1)}, u32[]{:S(2)}) copy-start(f32[1,512]{1,0:T(1,128)S(1)} %get-tuple-element.2670) | copy-start | bytes 6148
  18.7 0.6 copy-start.21
  18.7 0.6 copy-start.22
  18.8 1.3 copy-start.20
  20.1 54.2 %copy-start.9 = (bf16[32,1024]{1,0:T(8,128)(2,1)S(1)}, bf16[32,1024]{1,0:T(8,128)(2,1)}, u32[]{:S(2)}) copy-start(bf16[32,1024]{1,0:T(8,128)(2,1)} %param.29) | copy-start | bytes 196612
  20.2 91.5 %copy-start.24 = (f32[128]{0:T(128)S(1)}, f32[128]{0:T(128)}, u32[]{:S(2)}) copy-start(f32[128]{0:T(128)} %param.27) | copy-start | bytes 1540
  72.5 39.2 %copy-start.2 = (f32[2,128,128]{1,2,0:T(8,128)}, f32[2,128,128]{1,2,0:T(8,128)S(1)}, u32[]{:S(2)}) copy-start(f32[2,128,128]{1,2,0:T(8,128)S(1)} %get-tuple-element.1689) | copy-start | bytes 393220
  72.5 136.3 %copy-start.8 = (f32[4,2,64]{2,1,0:T(2,128)}, f32[4,2,64]{2,1,0:T(2,128)S(1)}, u32[]{:S(2)}) copy-start(f32[4,2,64]{2,1,0:T(2,128)S(1)} %get-tuple-element.3692) | copy-start | bytes 6148
  72.5 136.3 %copy-start.10 = (f32[4,2,64]{2,1,0:T(2,128)}, f32[4,2,64]{2,1,0:T(2,128)S(1)}, u32[]{:S(2)}) copy-start(f32[4,2,64]{2,1,0:T(2,128)S(1)} %get-tuple-element.3696) | copy-start | bytes 6148
  73.3 135.5 %all-gather.11.cloned.1.call-start = ((), (), s32[]{:S(2)}) async-start(), calls=%async_computation.5 | async-start | bytes 4325376 | tf_op jit(solution)/shard_map/all_gather | solution.py:26
  74.1 337.9 %all-gather.13.cloned.1.call-start = ((), (), s32[]{:S(2)}) async-start(), calls=%async_computation.6 | async-start | bytes 4325376 | tf_op jit(solution)/shard_map/all_gather | solution.py:26
  109.6 0.8 copy-start.3
  110.8 0.8 copy-start.4
  111.7 396.0 %reduce-scatter.5.cloned.1.call-start = ((), (), s32[]{:S(2)}) async-start(), calls=%async_computation.3 | async-start | bytes 540672 | tf_op jit(solution)/shard_map/reduce_scatter | solution.py:216
  208.8 78.2 %copy-start.11 = (f32[4,2,64,1]{2,1,3,0:T(2,128)S(1)}, f32[4,2,64,1]{2,1,3,0:T(2,128)}, u32[]{:S(2)}) copy-start(f32[4,2,64,1]{2,1,3,0:T(2,128)} %custom-call.36) | copy-start | bytes 6148
  287.1 97.9 %copy-start.25 = (f32[128]{0:T(128)S(1)}, f32[128]{0:T(128)}, u32[]{:S(2)}) copy-start(f32[128]{0:T(128)} %param.27) | copy-start | bytes 1540
  390.1 2.3 copy-start.5
  392.3 180.1 %all-gather.15.cloned.1.call-start = ((), (), s32[]{:S(2)}) async-start(), calls=%async_computation.7 | async-start | bytes 4325376 | tf_op jit(solution)/shard_map/all_gather | solution.py:26
  411.0 0.7 copy-start.1
  411.7 439.1 %reduce-scatter.3.cloned.1.call-start = ((), (), s32[]{:S(2)}) async-start(), calls=%async_computation.2 | async-start | bytes 589824 | tf_op jit(solution)/shard_map/reduce_scatter | solution.py:208
  417.7 5.2 copy-start.6
  758.2 6.6 copy-start.13
  758.2 6.6 copy-start.15
  758.2 6.6 copy-start.17
  758.2 6.6 copy-start.19
  764.7 5.6 copy-start.23
  764.7 6.2 copy-start.26
  765.4 85.1 %collective-permute-start.1 = (f32[3,512]{1,0:T(4,128)S(1)}, f32[3,512]{1,0:T(4,128)S(1)}, u32[]{:S(2)}, u32[]{:S(2)}) collective-permute-start(f32[3,512]{1,0:T(4,128)S(1)} %pad_add_fusion.4), channel_id=1, source_target_pairs={{1,0},{2,1},{3,2},{4,3},{5,4},{6,5},{7,6},{8,7},{9,8},{10,9},{11,1... | collective-permute-start | bytes 18440 | tf_op jit(solution)/shard_map/ppermute | solution.py:21
  850.7 0.7 copy-start.7
Sparse Core Ops, SparseCore 0:
  73.4 66.8 all-gather.8
  142.2 66.6 all-gather.10
  210.7 66.4 all-gather.12
  392.4 115.2 reduce-scatter.4
  509.6 62.7 all-gather.14
  577.2 75.5 reduce-scatter.2
where the time goes:
time: 865 us; the launch traced here: 858 us
  waiting for transfers between devices  248 us (29%)
  matrix products  195 us (23%)
  other arithmetic  179 us (21%)
  blocking collectives  115 us (13%)
  local copies, waits for them, and re-layouts  95.8 us (11%)
  between operations  14.9 us (2%)
    dot_general x170, matrix products, product(): return jnp.einsum(pattern, left_array, right_array, precision=HIGHEST)  172 us
    all_gather x4, waiting for transfers between devices, prefix_2(): pieces = jax.tree.map(lambda part: lax.all_gather(part, axis), value)  160 us
    another operation x48, other arithmetic, block_terms(): lax.linalg.triangular_solve(lower_mat, stacked, left_side=True, lower=Tru...  133 us
    reduce_scatter x1, waiting for transfers between devices, local(): lax.psum_scatter(jnp.einsum('tv,td->vd', normed, full_grad, preferred_ele...  83.7 us
    psum x1, blocking collectives, local(): grad_conv_total, gain_partial = lax.psum((grad_conv, grad_gain), 'ctx')  55.8 us
    all_gather x1, blocking collectives, local(): full_grad = lax.all_gather(out_grad, 'dp', axis=0, tiled=True)  35.2 us
    dynamic_slice x62, local copies, waits for them, and re-layouts, step(): longer = join(total, jax.tree.map(lambda part: part[position], pieces))  31.4 us
    psum x1, blocking collectives, local(): grad_gain_total = lax.psum(gain_partial, 'dp')  23.8 us
  transfers between devices with their start and end apart: 8, of which 5 were waited for; matrix products, arithmetic and copies ran while one was open for 48% of the time, Pallas kernels for 0%

commit v1 on v0

v1 whole, which is shorter than its diff:
```python
import functools
import math

import jax
import jax.numpy as jnp
from jax import lax
from jax.experimental import pallas as pl
from jax.experimental.pallas import tpu as pltpu
from jax.sharding import Mesh
from jax.sharding import PartitionSpec as P

D = 128
ROWS = 256
NB = 4
EPS = 1e-06
SCALE = 1.0 / math.sqrt(D)
HIGHEST = lax.Precision.HIGHEST
F32 = jnp.float32
BF16 = jnp.bfloat16
PACK = 272

FORMS = {
    "nn": (((1,), (0,)), ((), ())),
    "nt": (((1,), (1,)), ((), ())),
    "tn": (((0,), (0,)), ((), ())),
}


def halves(x):
    high = x.astype(BF16)
    return high, (x - high.astype(F32)).astype(BF16)


def mm(a, b, form="nn", passes=1):
    dims = FORMS[form]
    dot = functools.partial(lax.dot_general, dimension_numbers=dims, preferred_element_type=F32)
    if passes == 6:
        return dot(a, b, precision=HIGHEST)
    if passes == 1:
        return dot(a.astype(BF16), b.astype(BF16))
    ah, al = halves(a)
    bh, bl = halves(b)
    return dot(ah, bh) + (dot(ah, bl) + dot(al, bh))


P_KK = 3
P_INV = 3
P_TY = 3
P_MAP = 1
P_OUT = 1
P_BACK = 1


def grid_index():
    return (
        lax.broadcasted_iota(jnp.int32, (D, D), 0),
        lax.broadcasted_iota(jnp.int32, (D, D), 1),
    )


def row_sum(x):
    return jnp.sum(x, axis=-1, keepdims=True)


def triangle_inverses(lowers):
    i, j = grid_index()
    eye = (i == j).astype(F32)
    small = [jnp.where((i >> 3) == (j >> 3), low, 0.0) for low in lowers]
    squares = [mm(s, s, passes=P_INV) for s in small]
    cubes = [mm(s, q, passes=P_INV) for s, q in zip(small, squares)]
    fourths = [mm(q, q, passes=P_INV) for q in squares]
    starts = [eye - s + q - c for s, q, c in zip(small, squares, cubes)]
    inverses = [t + mm(t, f, passes=P_INV) for t, f in zip(starts, fourths)]
    for level in (3, 4, 5, 6):
        joint = ((i >> (level + 1)) == (j >> (level + 1))) & ((i >> level) > (j >> level))
        inner = [
            mm(jnp.where(joint, low, 0.0), t, passes=P_INV) for low, t in zip(lowers, inverses)
        ]
        inverses = [t - mm(t, c, passes=P_INV) for t, c in zip(inverses, inner)]
    return inverses


def silu(u):
    return u / (1.0 + jnp.exp(-u))


def unit(raw):
    inverse = lax.rsqrt(row_sum(raw * raw) + EPS)
    return raw * inverse, inverse


def block(b):
    return slice(b * D, (b + 1) * D)


def value_lanes(core):
    return pl.ds(pl.multiple_of(2 * D + core * D, D), D)


def lane_groups(core):
    return (slice(0, D), slice(D, 2 * D), value_lanes(core))


def damping(cum_col, cum_row):
    i, j = grid_index()
    causal = i >= j
    return jnp.where(causal, jnp.exp(jnp.where(causal, cum_col - cum_row, 0.0)), 0.0)


def gate_columns(gates):
    return jnp.transpose(gates)


def maps_kernel(
    ids, mixed, other, tail_a, tail_b, gate_own, gate_other, conv_w,
    padded, pre, q_out, k_out, inverse_out, x_out, scores_out, maps_out, gates_out, packed,
):
    core = ids[1]
    for group, lanes in enumerate(lane_groups(core)):
        here = slice(group * D, (group + 1) * D)
        padded[0:8, here] = jnp.zeros((8, D), F32)
        padded[5:8, here] = tail_a[:, lanes].astype(F32) + tail_b[:, lanes].astype(F32)
        padded[pl.ds(8 + core * ROWS, ROWS), here] = mixed[:, lanes].astype(F32)
        padded[pl.ds(8 + (1 - core) * ROWS, ROWS), here] = other[:, lanes].astype(F32)

    gates_out[...] = jnp.zeros_like(gates_out)
    for source, own in ((gate_own, True), (gate_other, False)):
        picked = jnp.where(core == 0, source[...], pltpu.roll(source[...], 7, 0))
        at = (core if own else 1 - core) * 2
        for half in range(2):
            gates_out[pl.ds(at + half, 1), :] = picked[0:1, block(half)]
            gates_out[pl.ds(4 + at + half, 1), :] = picked[2:3, block(half)]
    i, j = grid_index()
    raw = gates_out[...]
    upto = (i <= j).astype(F32)
    cumulative = mm(raw, upto, passes=6)
    is_decay = lax.broadcasted_iota(jnp.int32, (8, D), 0) < 4
    gates = jnp.where(is_decay, cumulative, 1.0 / (1.0 + jnp.exp(-raw)))
    gates_out[...] = gates
    columns = gate_columns(gates)

    qs, ks, vs = [], [], []
    for b in range(NB):
        pieces = []
        for group, lanes in enumerate(lane_groups(core)):
            here = slice(group * D, (group + 1) * D)
            total = conv_w[0:1, lanes] * padded[5 + b * D : 5 + (b + 1) * D, here]
            for tap in range(1, 4):
                start = 5 + tap + b * D
                total = total + conv_w[tap : tap + 1, lanes] * padded[start : start + D, here]
            pre[block(b), here] = total
            pieces.append(silu(total).astype(BF16).astype(F32))
        q = unit(pieces[0])[0] * SCALE
        k = unit(pieces[1])[0]
        q_out[block(b), :] = q
        k_out[block(b), :] = k
        qs.append(q)
        ks.append(k)
        vs.append(pieces[2])

    strict = i > j
    lowers = []
    for b in range(NB):
        damp = damping(columns[:, b : b + 1], gates[b : b + 1, :])
        both = mm(jnp.concatenate([ks[b], qs[b]], axis=0), ks[b], "nt", P_KK)
        lowers.append(jnp.where(strict, columns[:, 4 + b : 5 + b] * damp * both[0:D], 0.0))
        scores_out[block(b), :] = damp * both[D:]
    inverses = triangle_inverses(lowers)
    maps, decays = [], []
    for b in range(NB):
        inverse_out[block(b), :] = inverses[b]
        cum, beta = columns[:, b : b + 1], columns[:, 4 + b : 5 + b]
        stacked = jnp.concatenate([(beta * jnp.exp(cum)) * ks[b], beta * vs[b]], axis=1)
        x = mm(inverses[b], stacked, passes=P_TY)
        x_out[block(b), :] = x
        end = gates[b : b + 1, D - 1 : D]
        tail_keys = jnp.exp(end - cum) * ks[b]
        both = mm(x, tail_keys, "tn", P_MAP)
        maps_out[2 * b * D : 2 * (b + 1) * D, :] = both
        maps.append(both)
        decays.append(jnp.exp(end))

    def compose(first, first_decay, then, then_decay):
        moved = mm(first, then[0:D], passes=P_MAP)
        through = then_decay * first[0:D] + first_decay * then[0:D] - moved[0:D]
        added = then_decay * first[D:] - moved[D:] + then[D:]
        return jnp.concatenate([through, added], axis=0), first_decay * then_decay

    early, early_decay = compose(maps[0], decays[0], maps[1], decays[1])
    late, late_decay = compose(maps[2], decays[2], maps[3], decays[3])
    whole, decay = compose(early, early_decay, late, late_decay)
    whole = whole.astype(BF16)
    row = lax.broadcasted_iota(jnp.int32, (16, D), 0)
    decay = jnp.broadcast_to(decay, (16, D))
    high = decay.astype(BF16).astype(F32)
    low = (decay - high).astype(BF16).astype(F32)
    lowest = decay - high - low
    parts = jnp.where(row == 0, high, jnp.where(row == 1, low, jnp.where(row == 2, lowest, 0.0)))
    parts = parts.astype(BF16)
    for copy in range(packed.shape[0]):
        packed[copy, 0 : 2 * D, :] = whole
        packed[copy, 2 * D : PACK, :] = parts


def readout_kernel(scores, x, q, gates, read_out, base_out):
    columns = gate_columns(gates[...])
    for b in range(NB):
        px = mm(scores[block(b), :], x[block(b), :], passes=P_TY)
        grown = jnp.exp(columns[:, b : b + 1]) * q[block(b), :]
        read_out[2 * b * D : (2 * b + 1) * D, :] = grown - px[:, 0:D]
        read_out[(2 * b + 1) * D : 2 * (b + 1) * D, :] = -x[block(b), 0:D]
        base_out[2 * b * D : (2 * b + 1) * D, :] = px[:, D:]
        base_out[(2 * b + 1) * D : 2 * (b + 1) * D, :] = x[block(b), D:]


def back_kernel(ids, full_grad, weight, back_out):
    rows = weight[pl.ds(pl.multiple_of(ids[1] * D, D), D), :]
    back_out[...] = mm(full_grad[...], rows, "nt")


def slab_decay(piece):
    return jnp.sum(piece[2 * D : PACK].astype(F32), axis=0, keepdims=True)


def outputs_kernel(
    ids, gathered, maps, read, base, gates, back, gain,
    states_out, deltas_out, grads_out, reach_out, packed_grad, normed_out, sent, gain_out,
):
    chip, core = ids[0], ids[1]

    def fold(position, state):
        piece = gathered[position]
        return slab_decay(piece) * state + (
            piece[D : 2 * D].astype(F32) - mm(state, piece[0:D], passes=P_MAP)
        )

    state = lax.fori_loop(0, chip, fold, jnp.zeros((D, D), F32))
    states, decays = [], []
    for b in range(NB):
        states.append(state)
        states_out[block(b), :] = state
        decay = jnp.exp(gates[b : b + 1, D - 1 : D])
        decays.append(decay)
        if b + 1 < NB:
            here = maps[2 * b * D : 2 * (b + 1) * D, :]
            state = decay * state - mm(state, here[0:D], passes=P_MAP) + here[D:]
    total_gain = jnp.zeros((1, D), F32)
    reaches = []
    for b in range(NB):
        both = slice(2 * b * D, 2 * (b + 1) * D)
        rows = base[both, :] + mm(read[both, :], states[b], "nt", P_OUT)
        out = rows[0:D]
        deltas_out[block(b), :] = rows[D:]
        inverse = lax.rsqrt(row_sum(out * out) * (1.0 / D) + EPS)
        unit_out = out * inverse
        normed = (unit_out * gain[...]).astype(BF16)
        normed_out[block(b), :] = normed

        @pl.when((b // 2) != core)
        def _():
            sent[block(b % 2), :] = normed

        cotangent = back[block(b), :]
        total_gain = total_gain + jnp.sum(cotangent * unit_out, axis=0, keepdims=True)
        scaled = cotangent * gain[...]
        grad = inverse * (scaled - unit_out * (row_sum(scaled * unit_out) * (1.0 / D)))
        grads_out[block(b), :] = grad
        reach = mm(grad, read[2 * b * D : (2 * b + 1) * D, :], "tn", P_OUT)
        reach_out[block(b), :] = reach
        reaches.append(reach)
    gain_out[...] = jnp.broadcast_to(total_gain, (8, D))
    state_grad = reaches[NB - 1]
    for b in range(NB - 2, -1, -1):
        through = maps[2 * b * D : (2 * b + 1) * D, :]
        state_grad = decays[b] * state_grad - mm(state_grad, through, "nt", P_MAP) + reaches[b]
    state_grad = state_grad.astype(BF16)
    for copy in range(packed_grad.shape[0]):
        packed_grad[copy] = state_grad


def local_grads_kernel(
    scores, deltas, grads, states, q, k, gates,
    dq_out, dk_out, pull_out, rows_out, sums_out,
):
    columns = gate_columns(gates[...])
    i, j = grid_index()
    sums_out[...] = jnp.zeros_like(sums_out)
    for b in range(NB):
        at = block(b)
        grad, score = grads[at, :], scores[at, :]
        damp = damping(columns[:, b : b + 1], gates[b : b + 1, :])
        d_score = jnp.where(i >= j, mm(grad, deltas[at, :], "nt", P_BACK), 0.0)
        d_inner = d_score * damp
        sums_out[b : b + 1, :] = jnp.sum(d_score * score, axis=0, keepdims=True)
        reading = mm(grad, states[at, :], passes=P_BACK)
        growth = jnp.exp(columns[:, b : b + 1])
        dq_out[at, :] = growth * reading + mm(d_inner, k[at, :], passes=P_BACK)
        dk_out[at, :] = mm(d_inner, q[at, :], "tn", P_BACK)
        pull_out[at, :] = mm(score, grad, "tn", P_BACK)
        row = row_sum(d_score * score) + row_sum(growth * q[at, :] * reading)
        rows_out[at, :] = jnp.broadcast_to(row, (D, D))


def grads_kernel(
    ids, gathered, gathered_grad, maps, reach, states, deltas, inverse, x, q, k, gates, pre, padded,
    dq, dk, pull, rows_in, sums, conv_w,
    keep_out, send_out, spill_out, gate_keep, gate_send, conv_out,
    d_pre,
):
    chip, core = ids[0], ids[1]
    count = gathered.shape[0]

    def fold(step, total):
        position = count - 1 - step
        piece = gathered[position]
        return slab_decay(piece) * total + (
            gathered_grad[position].astype(F32) - mm(total, piece[0:D], "nt", P_MAP)
        )

    exit_grad = lax.fori_loop(0, count - 1 - chip, fold, jnp.zeros((D, D), F32))
    columns = gate_columns(gates[...])
    i, j = grid_index()
    strict = i > j
    exits = [None] * NB
    decays = [jnp.exp(gates[b : b + 1, D - 1 : D]) for b in range(NB)]
    for b in range(NB - 1, -1, -1):
        exits[b] = exit_grad
        if b:
            through = maps[2 * b * D : (2 * b + 1) * D, :]
            exit_grad = (
                decays[b] * exit_grad - mm(exit_grad, through, "nt", P_MAP) + reach[block(b), :]
            )
    d_pre[NB * D : NB * D + 8, :] = jnp.zeros((8, 3 * D), F32)
    lane = lax.broadcasted_iota(jnp.int32, (D, D), 1)
    row_terms = jnp.zeros((D, D), F32)
    beta_terms = jnp.zeros((D, D), F32)
    col_rows, end_rows = [], []
    for b in range(NB):
        at = block(b)
        key, query = k[at, :], q[at, :]
        cum, beta = columns[:, b : b + 1], columns[:, 4 + b : 5 + b]
        growth = jnp.exp(cum)
        remain = jnp.exp(gates[b : b + 1, D - 1 : D] - cum)
        damp = damping(cum, gates[b : b + 1, :])
        tail_keys = remain * key
        d_delta = pull[at, :] + mm(tail_keys, exits[b], "nt", P_BACK)
        d_x = jnp.concatenate([-mm(d_delta, states[at, :], passes=P_BACK), d_delta], axis=1)
        d_y = mm(inverse[at, :], d_x, "tn", P_BACK)
        both = x[at, :]
        d_lower = jnp.where(strict, -mm(d_y, both, "nt", P_BACK), 0.0)
        d_inner = d_lower * (beta * damp)
        inner = mm(key, key, "nt", P_KK)
        elementwise = d_inner * inner
        d_tail = mm(deltas[at, :], exits[b], passes=P_BACK)
        symmetric = d_inner + jnp.transpose(d_inner)
        d_key = (
            dk[at, :]
            + mm(symmetric, key, passes=P_BACK)
            + (beta * growth) * d_y[:, 0:D]
            + remain * d_tail
        )
        d_query = dq[at, :]
        tail_dot = row_sum(d_tail * tail_keys)
        written = row_sum((beta * growth) * key * d_y[:, 0:D])
        row = rows_in[at, :] + (row_sum(elementwise) + written - tail_dot)
        row_terms = jnp.where(lane == b, row, row_terms)
        beta_terms = jnp.where(lane == b, (1.0 - beta) * row_sum(d_y * both), beta_terms)
        col_rows.append(sums[b : b + 1, :] + jnp.sum(elementwise, axis=0, keepdims=True))
        end = jnp.sum(tail_dot, axis=0, keepdims=True) + decays[b] * jnp.sum(
            row_sum(exits[b] * states[at, :]), axis=0, keepdims=True
        )
        end_rows.append(jnp.broadcast_to(end, (1, D)))

        u_q, u_k, u_v = pre[at, 0:D], pre[at, D : 2 * D], pre[at, 2 * D :]
        sigmoids = [1.0 / (1.0 + jnp.exp(-u)) for u in (u_q, u_k, u_v)]
        raw_q = (u_q * sigmoids[0]).astype(BF16).astype(F32)
        raw_k = (u_k * sigmoids[1]).astype(BF16).astype(F32)
        unit_q, inverse_q = unit(raw_q)
        inverse_k = unit(raw_k)[1]
        d_unit = d_query * SCALE
        d_raw_q = inverse_q * (d_unit - unit_q * row_sum(unit_q * d_unit))
        d_raw_k = inverse_k * (d_key - key * row_sum(key * d_key))
        d_raw_v = beta * d_y[:, D:]
        for group, (d_raw, u, s) in enumerate(
            zip((d_raw_q, d_raw_k, d_raw_v), (u_q, u_k, u_v), sigmoids)
        ):
            d_pre[at, group * D : (group + 1) * D] = d_raw * (s * (1.0 + u * (1.0 - s)))

    rows = jnp.transpose(row_terms)[0:8, :] - jnp.concatenate(
        col_rows + [jnp.zeros((4, D), F32)], axis=0
    )
    d_decay = mm(rows, (i >= j).astype(F32), passes=6) + jnp.concatenate(
        end_rows + [jnp.zeros((4, D), F32)], axis=0
    )
    d_logit = jnp.transpose(beta_terms)[0:8, :]
    for target, own in ((gate_keep, True), (gate_send, False)):
        target[...] = jnp.zeros_like(target)
        for head in range(2):

            @pl.when(core == head)
            def _():
                first = 2 * (head if own else 1 - head)
                for half in range(2):
                    b = first + half
                    target[head : head + 1, block(half)] = d_decay[b : b + 1, :]
                    target[2 + head : 3 + head, block(half)] = d_logit[b : b + 1, :]

    keep_out[...] = jnp.zeros_like(keep_out)
    send_out[...] = jnp.zeros_like(send_out)
    spill_out[...] = jnp.zeros_like(spill_out)
    conv_out[...] = jnp.zeros_like(conv_out)
    for group, lanes in enumerate(lane_groups(core)):
        here = slice(group * D, (group + 1) * D)
        taps = [conv_w[tap : tap + 1, lanes] for tap in range(4)]
        sums_of = [jnp.zeros((1, D), F32) for _ in range(4)]
        for b in range(NB):
            total = taps[3] * d_pre[b * D : (b + 1) * D, here]
            for tap in range(3):
                start = b * D + 3 - tap
                total = total + taps[tap] * d_pre[start : start + D, here]
            mine = (b // 2) == core
            at = slice((b % 2) * D, (b % 2 + 1) * D)

            @pl.when(mine)
            def _():
                keep_out[at, lanes] = total

            @pl.when(jnp.logical_not(mine))
            def _():
                send_out[at, lanes] = total.astype(BF16)

            for tap in range(4):
                start = 5 + tap + b * D
                sums_of[tap] = sums_of[tap] + jnp.sum(
                    d_pre[b * D : (b + 1) * D, here] * padded[start : start + D, here],
                    axis=0,
                    keepdims=True,
                )
        for tap in range(4):
            conv_out[tap : tap + 1, lanes] = sums_of[tap]
        for back in range(1, 4):
            total = jnp.zeros((1, D), F32)
            for tap in range(0, 4 - back):
                at = 3 - back - tap
                total = total + taps[tap] * d_pre[at : at + 1, here]
            spill_out[3 - back : 4 - back, lanes] = total


def project_kernel(ids, normed, received, weight, gain_part, out):
    core = ids[1]
    kept = normed[pl.ds(pl.multiple_of(core * ROWS, ROWS), ROWS), :]
    mine = weight[pl.ds(pl.multiple_of(core * D, D), D), :]
    others = weight[pl.ds(pl.multiple_of((1 - core) * D, D), D), :]
    share = (mm(kept, mine) + mm(received[...], others)).astype(BF16)
    count, height = out.shape[0], out.shape[1] - 16
    row = lax.broadcasted_iota(jnp.int32, (16, D), 0)
    gain = jnp.broadcast_to(gain_part[0:1, :], (16, D))
    high = gain.astype(BF16).astype(F32)
    extra = jnp.where(row == 0, high, jnp.where(row == 1, gain - high, 0.0)).astype(BF16)
    for owner in range(count):
        out[owner, 0:height, :] = share[owner * height : (owner + 1) * height]
        out[owner, height:, :] = jnp.zeros((16, out.shape[2]), BF16)
        out[owner, height:, 0:D] = extra


def call(kernel, shapes, args, name, flops, moved, scratch=(), smem=True):
    specs = [pl.BlockSpec(memory_space=pltpu.VMEM) for _ in args]
    if smem:
        specs[0] = pl.BlockSpec(memory_space=pltpu.SMEM)
    return pl.pallas_call(
        kernel,
        out_shape=[jax.ShapeDtypeStruct(shape, dtype) for shape, dtype in shapes],
        in_specs=specs,
        out_specs=[pl.BlockSpec(memory_space=pltpu.VMEM) for _ in shapes],
        scratch_shapes=list(scratch),
        name=name,
        cost_estimate=pl.CostEstimate(flops=flops, bytes_accessed=moved, transcendentals=0),
        compiler_params=pltpu.CompilerParams(vmem_limit_bytes=40 * 2**20),
    )(*args)


def everyone(x, axes):
    return lax.all_to_all(x, axes, 0, 0, tiled=True)


def local(mixed, log_decay, beta_logit, conv_weight, norm_gain, out_weight, out_grad):
    chips, groups = lax.axis_size("chip"), lax.axis_size("dp")
    ids = jnp.stack([lax.axis_index("chip"), lax.axis_index("core")]).astype(jnp.int32)
    line = ("chip", "core")
    swap = [(0, 1), (1, 0)]
    width = out_weight.shape[1]

    gates_own = jnp.concatenate([log_decay.T, beta_logit.T, jnp.zeros((4, ROWS), F32)], axis=0)
    other = lax.ppermute(mixed, "core", swap)
    tail = mixed[ROWS - 3 :]
    tail_a = lax.ppermute(tail, line, [(2 * c + 1, 2 * c + 2) for c in range(chips - 1)])
    tail_b = lax.ppermute(tail, line, [(2 * c + 1, 2 * c + 3) for c in range(chips - 1)])
    gates_other = lax.ppermute(gates_own, "core", swap)
    full_grad = lax.all_gather(out_grad, ("core", "dp"), axis=0, tiled=True)

    rows = NB * D
    (padded, pre, q, k, inverse, x, scores, maps, gates, packed) = call(
        maps_kernel,
        [
            ((rows + 8, 3 * D), F32),
            ((rows, 3 * D), F32),
            ((rows, D), F32),
            ((rows, D), F32),
            ((rows, D), F32),
            ((rows, 2 * D), F32),
            ((rows, D), F32),
            ((2 * rows, D), F32),
            ((8, D), F32),
            ((chips, PACK, D), BF16),
        ],
        [ids, mixed, other, tail_a, tail_b, gates_own, gates_other, conv_weight],
        "maps", 10**9, 6 * 10**6,
    )
    gathered = everyone(packed, "chip")
    read, base = call(
        readout_kernel,
        [((2 * rows, D), F32), ((2 * rows, D), F32)],
        [scores, x, q, gates],
        "readout", 10**8, 2 * 10**6, smem=False,
    )
    (back,) = call(
        back_kernel,
        [((rows, D), F32)],
        [ids, full_grad, out_weight],
        "back", 10**8, 2 * 10**6,
    )
    gain = norm_gain.reshape(1, D)
    (states, deltas, grads, reach, packed_grad, normed, sent, gain_part) = call(
        outputs_kernel,
        [
            ((rows, D), F32),
            ((rows, D), F32),
            ((rows, D), F32),
            ((rows, D), F32),
            ((chips, D, D), BF16),
            ((rows, D), BF16),
            ((ROWS, D), BF16),
            ((8, D), F32),
        ],
        [ids, gathered, maps, read, base, gates, back, gain],
        "outputs", 10**9, 6 * 10**6,
    )
    gathered_grad = everyone(packed_grad, "chip")
    received = lax.ppermute(sent, "core", swap)
    dq, dk, pull, row_terms, sums = call(
        local_grads_kernel,
        [
            ((rows, D), F32),
            ((rows, D), F32),
            ((rows, D), F32),
            ((rows, D), F32),
            ((8, D), F32),
        ],
        [scores, deltas, grads, states, q, k, gates],
        "local_grads", 10**9, 4 * 10**6, smem=False,
    )

    height = ROWS // groups
    (share,) = call(
        project_kernel,
        [((groups, height + 16, width), BF16)],
        [ids, normed, received, out_weight, gain_part],
        "project", 10**8, 2 * 10**6,
    )
    shares = everyone(share, "dp").astype(F32)
    result = jnp.sum(shares[:, :height], axis=0).astype(BF16)
    gain_rows = jnp.sum(shares[:, height : height + 2, :D], axis=0)

    weight_part = jnp.einsum("tv,td->vd", normed, full_grad, preferred_element_type=F32)
    weight_parts = everyone(weight_part.astype(BF16).reshape(chips, D // chips, width), "chip")
    weight_sum = jnp.sum(weight_parts.astype(F32), axis=0)
    grad_weight = lax.ppermute(
        weight_sum, line, [(2 * c + h, h * chips + c) for c in range(chips) for h in range(2)]
    )

    keep, send, spill, gate_keep, gate_send, conv_part = call(
        grads_kernel,
        [
            ((ROWS, 4 * D), F32),
            ((ROWS, 4 * D), BF16),
            ((8, 4 * D), F32),
            ((8, ROWS), F32),
            ((8, ROWS), F32),
            ((8, 4 * D), F32),
        ],
        [
            ids, gathered, gathered_grad, maps, reach, states, deltas, inverse, x, q, k, gates,
            pre, padded, dq, dk, pull, row_terms, sums, conv_weight,
        ],
        "grads", 10**9, 8 * 10**6,
        scratch=[pltpu.VMEM((rows + 8, 3 * D), F32)],
    )
    taken = lax.ppermute(send, "core", swap)
    gate_taken = lax.ppermute(gate_send, "core", swap)
    spill_a = lax.ppermute(spill, line, [(2 * c, 2 * c - 1) for c in range(1, chips)])
    spill_b = lax.ppermute(spill, line, [(2 * c + 1, 2 * c - 1) for c in range(1, chips)])

    high = gain_rows[0:1] + gain_rows[1:2]
    gain_high = high.astype(BF16).astype(F32)
    extra = jnp.pad(jnp.concatenate([gain_high, high - gain_high]), ((4, 2), (0, 3 * D)))
    small = (conv_part + extra).astype(BF16)
    smalls = everyone(jnp.broadcast_to(small, (2 * chips, 8, 4 * D)), line)
    totals = jnp.sum(smalls.astype(F32), axis=0)

    spilled = jnp.pad((spill_a + spill_b)[0:3], ((ROWS - 3, 0), (0, 0)))
    grad_mixed = (keep + taken.astype(F32) + spilled).astype(BF16)
    gate_grads = gate_keep + gate_taken
    return (
        result,
        grad_mixed,
        gate_grads[0:2].T,
        gate_grads[2:4].T,
        totals[0:4],
        totals[4, :D] + totals[5, :D],
        grad_weight,
    )


def solution(mesh):
    groups, line = mesh.shape["dp"], mesh.shape["ctx"]
    fine = Mesh(mesh.devices.reshape(groups, line // 2, 2), ("dp", "chip", "core"))
    ctx = ("chip", "core")
    return jax.shard_map(
        local,
        mesh=fine,
        in_specs=(
            P(ctx, "dp"),
            P(ctx, "dp"),
            P(ctx, "dp"),
            P(None, "dp"),
            P(),
            P("dp", None),
            P((*ctx, "dp"), None),
        ),
        out_specs=(
            P((*ctx, "dp"), None),
            P(ctx, "dp"),
            P(ctx, "dp"),
            P(ctx, "dp"),
            P(None, "dp"),
            P(),
            P(("dp", *ctx), None),
        ),
        check_vma=False,
    )
```

time: 865 us -> 220 us (0.25)
  matrix products: 195 us -> 1.05 us
  waiting for transfers between devices: 248 us -> 73.6 us
  other arithmetic: 179 us -> 5.12 us
  blocking collectives: 115 us -> 16.7 us
  local copies, waits for them, and re-layouts: 95.8 us -> 35.7 us
  starting transfers between devices: 6.46 us -> 50.6 us
  Pallas kernels: 0 us -> 20.1 us
    dot_general x177 -> x1, matrix products: 180 us -> 1.05 us  [local(): jnp.einsum('tv,td->vd', normed, full_grad, preferred_element_type=F32)]
    another operation x76 -> x1, other arithmetic: 140 us -> 0.07 us  [local(): jnp.stack([lax.axis_index('chip'), lax.axis_index('core')])]
    all_gather x4 -> x1, waiting for transfers between devices: 160 us -> 50.9 us  [local(): full_grad = lax.all_gather(out_grad, ('core', 'dp'), axis=0, tiled=True)]
    reduce_scatter x2 -> x0, waiting for transfers between devices: 83.7 us -> none  [the longest x1 83.7 us: local(): lax.psum_scatter(jnp.einsum('tv,td->vd', normed, full_grad, preferred_ele...]
    psum x2 -> x0, blocking collectives: 79.6 us -> none  [the longest x1 55.8 us: local(): grad_conv_total, gain_partial = lax.psum((grad_conv, grad_gain), 'ctx')]
    all_gather x1 -> x0, blocking collectives: 35.2 us -> none  [local(): full_grad = lax.all_gather(out_grad, 'dp', axis=0, tiled=True)]
    all_to_all x0 -> x4, starting transfers between devices: none -> 31.7 us  [everyone(): return lax.all_to_all(x, axes, 0, 0, tiled=True)]
    dynamic_slice x62 -> x0, local copies, waits for them, and re-layouts: 31.4 us -> none  [step(): longer = join(total, jax.tree.map(lambda part: part[position], pieces))]
  transfers between devices with their start and end apart: 8 -> 15, of which waited for: 5 -> 6; matrix products, arithmetic and copies ran while one was open for 48% -> 3% of each run, Pallas kernels for 0% -> 2%
where the time goes in v1:
time: 220 us; the launch traced here: 217 us
  waiting for transfers between devices  73.6 us (33%)
  starting transfers between devices  50.6 us (23%)
  local copies, waits for them, and re-layouts  35.7 us (16%)
  Pallas kernels  20.1 us (9%)
  blocking collectives  16.7 us (8%)
  between operations  14.4 us (7%)
  other arithmetic  5.12 us (2%)
    all_gather x1, waiting for transfers between devices, local(): full_grad = lax.all_gather(out_grad, ('core', 'dp'), axis=0, tiled=True)  50.9 us
    unnamed x99, local copies, waits for them, and re-layouts  33 us
    all_to_all x4, starting transfers between devices, everyone(): return lax.all_to_all(x, axes, 0, 0, tiled=True)  31.7 us
    pallas_call x7, Pallas kernels, call(): pl.pallas_call(kernel, out_shape=[jax.ShapeDtypeStruct(shape, dtype) for...  20.1 us
    all_to_all x1, blocking collectives, everyone(): return lax.all_to_all(x, axes, 0, 0, tiled=True)  16.7 us
    all_to_all x4, waiting for transfers between devices, everyone(): return lax.all_to_all(x, axes, 0, 0, tiled=True)  15.8 us
    ppermute x1, starting transfers between devices, local(): lax.ppermute(weight_sum, line, [(2 * c + h, h * chips + c) for c in range...  7.28 us
    ppermute x1, starting transfers between devices, local(): lax.ppermute(spill, line, [(2 * c, 2 * c - 1) for c in range(1, chips)])  5.78 us
  transfers between devices with their start and end apart: 15, of which 6 were waited for; matrix products, arithmetic and copies ran while one was open for 3% of the time, Pallas kernels for 2%

profile of v1, /device:TPU:8, one launch (start us, length us, event | category | flops | bytes accessed | tf_op | source)
XLA Modules:
  0.0 217.1 jit_solution(14356557868876812811)
XLA Ops:
  8.5 1.3 collective-permute-start.1
  9.8 2.8 %collective-permute-start = (bf16[256,512]{1,0:T(8,128)(2,1)}, bf16[256,512]{1,0:T(8,128)(2,1)S(1)}, u32[]{:S(2)}, u32[]{:S(2)}) collective-permute-start(bf16[256,512]{1,0:T(8,128)(2,1)} %mixed.1), channel_id=1, source_target_pairs={{0,1},{1,0},{2,3},{3,2},{4,5},{5,4},{6,7},{7,6},{8,9},{9,8},{10,11... | collective-permute-start | bytes 786440 | tf_op jit(solution)/shard_map/ppermute | solution.py:494
  13.6 3.9 %collective-permute-done.1.tail_a = bf16[3,512]{1,0:T(4,128)(2,1)S(1)} collective-permute-done((bf16[3,512]{1,0:T(4,128)(2,1)S(1)}, bf16[3,512]{1,0:T(4,128)(2,1)S(1)}, u32[]{:S(2)}, u32[]{:S(2)}) %collective-permute-start.1) | collective-permute-done | bytes 3104 | tf_op jit(solution)/shard_map/ppermute | solution.py:496
  18.9 0.9 copy-done.37
  19.9 0.9 copy-done.44
  20.8 6.3 %maps.1 = (f32[520,384]{1,0:T(8,128)S(1)}, f32[512,384]{1,0:T(8,128)S(1)}, f32[512,128]{1,0:T(8,128)S(1)}, f32[512,128]{1,0:T(8,128)S(1)}, f32[512,128]{1,0:T(8,...) custom-call(s32[2]{0:T(128)S(1)} %pad_add_fusion.ids, ...), custom_call_target="tpu_custom_call" | custom-call | flops 1000000000 | bytes 6000000 | tf_op jit(solution)/shard_map/maps/pallas_call | solution.py:470
  27.1 0.9 copy-done.3
  28.0 0.9 copy-done.5
  30.3 7.3 %all-to-all-start = ((bf16[16,272,128]{2,1,0:T(8,128)(2,1)}), bf16[16,272,128]{2,1,0:T(8,128)(2,1)S(1)}, u32[]{:S(2)}, u32[]{:S(2)}) async-start(bf16[16,272,128]{2,1,0:T(8,128)(2,1)} %get-tuple-element.38), calls=%async_computation | async-start | bytes 2228224 | tf_op jit(solution)/shard_map/all_to_all | solution.py:483
  40.4 50.9 %all-gather.2.cloned.1.call-done.full_grad = bf16[512,1024]{1,0:T(8,128)(2,1)} async-done(((bf16[32,1024]{1,0:T(8,128)(2,1)}), bf16[512,1024]{1,0:T(8,128)(2,1)}) %all-gather.2.cloned.1.call-update) | async-done | bytes 1048592 | tf_op jit(solution)/shard_map/all_gather | solution.py:499
  91.3 1.2 copy-done
  92.5 1.0 back.1
  94.2 0.9 copy-done.34
  95.2 1.0 copy-done.39
  96.2 1.0 copy-done.41
  97.2 3.8 %outputs.1 = (f32[512,128]{1,0:T(8,128)S(1)}, f32[512,128]{1,0:T(8,128)S(1)}, f32[512,128]{1,0:T(8,128)S(1)}, f32[512,128]{1,0:T(8,128)S(1)}, bf16[16,128,128]{2...) custom-call(s32[2]{0:T(128)S(1)} %pad_add_fusion.ids, ...), custom_call_target="tpu_custom_call" | custom-call | flops 1000000000 | bytes 6000000 | tf_op jit(solution)/shard_map/outputs/pallas_call | solution.py:470
  104.0 1.1 fusion
  105.0 9.1 %all-to-all-start.4 = ((bf16[16,8,1024]{2,1,0:T(8,128)(2,1)}), bf16[16,8,1024]{2,1,0:T(8,128)(2,1)}, u32[]{:S(2)}, u32[]{:S(2)}) async-start(bf16[16,8,1024]{2,1,0:T(8,128)(2,1)} %fusion), calls=%async_computation.4 | async-start | bytes 524288 | tf_op jit(solution)/shard_map/all_to_all | solution.py:483
  114.1 1.2 collective-permute-done.4.received
  115.3 1.0 project.1
  116.3 7.7 %all-to-all-done.4 = bf16[16,8,1024]{2,1,0:T(8,128)(2,1)} async-done(((bf16[16,8,1024]{2,1,0:T(8,128)(2,1)}), bf16[16,8,1024]{2,1,0:T(8,128)(2,1)}, u32[]{:S(2)}, u32[]{:S(2)}) %all-to-all-start.4) | async-done | bytes 262176 | tf_op jit(solution)/shard_map/all_to_all | solution.py:483
  124.0 16.7 %all_to_all.25 = bf16[8,48,1024]{2,1,0:T(8,128)(2,1)} all-to-all(bf16[8,48,1024]{2,1,0:T(8,128)(2,1)S(1)} %project.1), channel_id=1, replica_groups=mesh['dp'=8,'chip'=16,'core'=2] {'dp'}, dimensions={0} | all-to-all | bytes 1572864 | tf_op jit(solution)/shard_map/all_to_all | solution.py:483
  140.7 7.1 %all-to-all-start.2 = ((bf16[16,128,128]{2,1,0:T(8,128)(2,1)}), bf16[16,128,128]{2,1,0:T(8,128)(2,1)S(1)}, u32[]{:S(2)}, u32[]{:S(2)}) async-start(bf16[16,128,128]{2,1,0:T(8,128)(2,1)} %copy-done.10), calls=%async_computation.2 | async-start | bytes 1048576 | tf_op jit(solution)/shard_map/all_to_all | solution.py:483
  147.8 1.0 convert_reduce_fusion
  148.8 7.3 %collective-permute-start.9 = (f32[8,1024]{1,0:T(8,128)S(1)}, f32[8,1024]{1,0:T(8,128)}, u32[]{:S(2)}, u32[]{:S(2)}) collective-permute-start(f32[8,1024]{1,0:T(8,128)S(1)} %convert_reduce_fusion), channel_id=1, source_target_pairs={{0,0},{1,16},{2,1},{3,17},{4,2},{5,18},{6,3},{7,19},{8,4},{9,20},{... | collective-permute-start | bytes 98312 | tf_op jit(solution)/shard_map/ppermute | solution.py:577
  156.1 0.9 copy-done.16
  157.1 0.9 copy-done.19
  158.0 0.9 copy-done.32
  159.0 0.9 copy-done.47
  159.9 1.1 local_grads.1
  162.5 1.1 copy-done.4
  163.7 1.0 copy-done.8
  164.7 0.9 copy-done.14
  165.7 0.9 copy-done.17
  166.6 0.9 copy-done.20
  167.6 0.9 copy-done.22
  168.5 0.9 copy-done.24
  169.5 0.9 copy-done.26
  170.4 0.9 copy-done.28
  171.4 0.9 copy-done.30
  172.3 6.6 %grads.1 = (f32[256,512]{1,0:T(8,128)S(1)}, bf16[256,512]{1,0:T(8,128)(2,1)S(1)}, f32[8,512]{1,0:T(8,128)S(1)}, f32[8,256]{1,0:T(8,128)S(1)}, f32[8,256]{1,0:T(8,128)S(1)}, /*index=5*/f32[8,512]{1,0:T(8,128)S(1)}) custom-call(s32[2]{0:T(128)S(1)} %pad_add_fusion.ids, bf16[16,272,128]{2,1,0:T(8,128)(2,1)S(1)} %all-to-all-done.gathered, ...), custom_call_target="tpu_custom_call" | custom-call | flops 1000000000 | bytes 8000000 | tf_op jit(solution)/shard_map/grads/pallas_call | solution.py:470
  178.9 0.8 copy-done.9
  181.0 5.8 %collective-permute-start.6 = (f32[8,512]{1,0:T(8,128)S(1)}, f32[8,512]{1,0:T(8,128)S(1)}, u32[]{:S(2)}, u32[]{:S(2)}) collective-permute-start(f32[8,512]{1,0:T(8,128)S(1)} %get-tuple-element.65), channel_id=1, source_target_pairs={{2,1},{4,3},{6,5},{8,7},{10,9},{12,11},{14,13},{16,15},{18,17},{20... | collective-permute-start | bytes 49160 | tf_op jit(solution)/shard_map/ppermute | solution.py:600
  187.7 8.3 %all-to-all-start.3 = ((bf16[32,8,512]{2,1,0:T(8,128)(2,1)}), bf16[32,8,512]{2,1,0:T(8,128)(2,1)S(1)}, u32[]{:S(2)}, u32[]{:S(2)}) async-start(bf16[32,8,512]{2,1,0:T(8,128)(2,1)} %broadcast_in_dim.7), calls=%async_computation.3 | async-start | bytes 524288 | tf_op jit(solution)/shard_map/all_to_all | solution.py:483
  196.8 1.0 collective-permute-done.5
  197.8 1.8 add_convert_fusion
  199.6 8.2 %all-to-all-done.3 = bf16[32,8,512]{2,1,0:T(8,128)(2,1)S(1)} async-done(((bf16[32,8,512]{2,1,0:T(8,128)(2,1)}), bf16[32,8,512]{2,1,0:T(8,128)(2,1)S(1)}, u32[]{:S(2)}, u32[]{:S(2)}) %all-to-all-start.3) | async-done | bytes 262176 | tf_op jit(solution)/shard_map/all_to_all | solution.py:483
  208.9 1.4 copy.15
  (110 shorter events, 17.2 us)
Async XLA Ops:
  7.9 5.7 %collective-permute-start.2 = (bf16[3,512]{1,0:T(4,128)(2,1)S(1)}, bf16[3,512]{1,0:T(4,128)(2,1)S(1)}, u32[]{:S(2)}, u32[]{:S(2)}) collective-permute-start(bf16[3,512]{1,0:T(4,128)(2,1)S(1)} %slice.33), channel_id=1, source_target_pairs={{1,3},{3,5},{5,7},{7,9},{9,11},{11,13},{13,15},{15,17},{17,19},{19... | collective-permute-start | bytes 9224 | tf_op jit(solution)/shard_map/ppermute | solution.py:497
  8.5 9.0 %collective-permute-start.1 = (bf16[3,512]{1,0:T(4,128)(2,1)S(1)}, bf16[3,512]{1,0:T(4,128)(2,1)S(1)}, u32[]{:S(2)}, u32[]{:S(2)}) collective-permute-start(bf16[3,512]{1,0:T(4,128)(2,1)S(1)} %slice.33), channel_id=1, source_target_pairs={{1,2},{3,4},{5,6},{7,8},{9,10},{11,12},{13,14},{15,16},{17,18},{19... | collective-permute-start | bytes 9224 | tf_op jit(solution)/shard_map/ppermute | solution.py:496
  9.8 7.7 %collective-permute-start = (bf16[256,512]{1,0:T(8,128)(2,1)}, bf16[256,512]{1,0:T(8,128)(2,1)S(1)}, u32[]{:S(2)}, u32[]{:S(2)}) collective-permute-start(bf16[256,512]{1,0:T(8,128)(2,1)} %mixed.1), channel_id=1, source_target_pairs={{0,1},{1,0},{2,3},{3,2},{4,5},{5,4},{6,7},{7,6},{8,9},{9,8},{10,11... | collective-permute-start | bytes 786440 | tf_op jit(solution)/shard_map/ppermute | solution.py:494
  13.5 4.1 %collective-permute-start.3 = (f32[8,256]{1,0:T(8,128)S(1)}, f32[8,256]{1,0:T(8,128)S(1)}, u32[]{:S(2)}, u32[]{:S(2)}) collective-permute-start(f32[8,256]{1,0:T(8,128)S(1)} %maximum_maximum_fusion.gate_own), channel_id=1, source_target_pairs={{0,1},{1,0},{2,3},{3,2},{4,5},{5,4},{6,7},{7,6},{8,9},{9,8},{10,11... | collective-permute-start | bytes 24584 | tf_op jit(solution)/shard_map/ppermute | solution.py:498
  18.9 0.9 copy-start.37
  19.9 0.9 copy-start.44
  30.3 8.5 %copy-start.31 = (f32[512,128]{1,0:T(8,128)}, f32[512,128]{1,0:T(8,128)S(1)}, u32[]{:S(2)}) copy-start(f32[512,128]{1,0:T(8,128)S(1)} %get-tuple-element.40.scores) | copy-start | bytes 786436
  30.3 63.9 %copy-start.7 = (f32[1024,128]{1,0:T(8,128)}, f32[1024,128]{1,0:T(8,128)S(1)}, u32[]{:S(2)}) copy-start(f32[1024,128]{1,0:T(8,128)S(1)} %get-tuple-element.39.maps) | copy-start | bytes 1572868
  30.3 61.0 %copy-start.2 = (bf16[256,1024]{1,0:T(8,128)(2,1)S(1)}, bf16[256,1024]{1,0:T(8,128)(2,1)}, u32[]{:S(2)}) copy-start(bf16[256,1024]{1,0:T(8,128)(2,1)} %weight.3) | copy-start | bytes 1572868
  30.3 63.9 %all-to-all-start = ((bf16[16,272,128]{2,1,0:T(8,128)(2,1)}), bf16[16,272,128]{2,1,0:T(8,128)(2,1)S(1)}, u32[]{:S(2)}, u32[]{:S(2)}) async-start(bf16[16,272,128]{2,1,0:T(8,128)(2,1)} %get-tuple-element.38), calls=%async_computation | async-start | bytes 2228224 | tf_op jit(solution)/shard_map/all_to_all | solution.py:483
  37.6 56.6 %copy-start.45 = (f32[128]{0:T(128)S(1)}, f32[128]{0:T(128)}, u32[]{:S(2)}) copy-start(f32[128]{0:T(128)} %param.11) | copy-start | bytes 1540
  37.6 53.7 %all-gather.2.cloned.1.call-start = ((), (), s32[]{:S(2)}) async-start(), calls=%async_computation.5 | async-start | bytes 1114112 | tf_op jit(solution)/shard_map/all_gather | solution.py:499
  91.3 1.2 copy-start
  94.2 1.0 copy-start.34
  95.2 1.0 copy-start.39
  96.2 1.0 copy-start.41
  97.2 6.7 %copy-start.1 = (bf16[512,1024]{1,0:T(8,128)(2,1)S(1)}, bf16[512,1024]{1,0:T(8,128)(2,1)}, u32[]{:S(2)}) copy-start(bf16[512,1024]{1,0:T(8,128)(2,1)} %all-gather.2.cloned.1.call-done.full_grad) | copy-start | bytes 3145732
  104.0 11.4 %copy-start.21 = (f32[512,128]{1,0:T(8,128)}, f32[512,128]{1,0:T(8,128)S(1)}, u32[]{:S(2)}) copy-start(f32[512,128]{1,0:T(8,128)S(1)} %get-tuple-element.50.reach) | copy-start | bytes 786436
  105.0 19.0 %all-to-all-start.4 = ((bf16[16,8,1024]{2,1,0:T(8,128)(2,1)}), bf16[16,8,1024]{2,1,0:T(8,128)(2,1)}, u32[]{:S(2)}, u32[]{:S(2)}) async-start(bf16[16,8,1024]{2,1,0:T(8,128)(2,1)} %fusion), calls=%async_computation.4 | async-start | bytes 524288 | tf_op jit(solution)/shard_map/all_to_all | solution.py:483
  114.1 1.3 collective-permute-start.4
  116.3 39.8 %copy-start.12 = (f32[512,128]{1,0:T(8,128)S(1)}, f32[512,128]{1,0:T(8,128)}, u32[]{:S(2)}) copy-start(f32[512,128]{1,0:T(8,128)} %copy-done.11) | copy-start | bytes 786436
  140.7 21.3 %all-to-all-start.2 = ((bf16[16,128,128]{2,1,0:T(8,128)(2,1)}), bf16[16,128,128]{2,1,0:T(8,128)(2,1)S(1)}, u32[]{:S(2)}, u32[]{:S(2)}) async-start(bf16[16,128,128]{2,1,0:T(8,128)(2,1)} %copy-done.10), calls=%async_computation.2 | async-start | bytes 1048576 | tf_op jit(solution)/shard_map/all_to_all | solution.py:483
  148.8 12.2 %collective-permute-start.9 = (f32[8,1024]{1,0:T(8,128)S(1)}, f32[8,1024]{1,0:T(8,128)}, u32[]{:S(2)}, u32[]{:S(2)}) collective-permute-start(f32[8,1024]{1,0:T(8,128)S(1)} %convert_reduce_fusion), channel_id=1, source_target_pairs={{0,0},{1,16},{2,1},{3,17},{4,2},{5,18},{6,3},{7,19},{8,4},{9,20},{... | collective-permute-start | bytes 98312 | tf_op jit(solution)/shard_map/ppermute | solution.py:577
  156.1 1.0 copy-start.16
  157.0 0.9 copy-start.19
  158.0 0.9 copy-start.32
  158.9 0.9 copy-start.47
  159.9 1.1 copy-start.48
  161.0 1.0 copy-start.23
  161.0 1.0 copy-start.25
  161.0 1.0 copy-start.27
  161.0 1.0 copy-start.29
  161.0 1.5 copy-start.6
  161.0 1.5 copy-start.36
  162.5 1.1 copy-start.4
  163.7 1.0 copy-start.8
  164.7 0.9 copy-start.14
  165.7 0.9 copy-start.17
  166.6 0.9 copy-start.20
  167.6 0.9 copy-start.22
  168.5 0.9 copy-start.24
  169.5 0.9 copy-start.26
  170.4 0.9 copy-start.28
  180.4 16.4 %collective-permute-start.7 = (f32[8,512]{1,0:T(8,128)S(1)}, f32[8,512]{1,0:T(8,128)S(1)}, u32[]{:S(2)}, u32[]{:S(2)}) collective-permute-start(f32[8,512]{1,0:T(8,128)S(1)} %get-tuple-element.65), channel_id=1, source_target_pairs={{3,1},{5,3},{7,5},{9,7},{11,9},{13,11},{15,13},{17,15},{19,17},{21... | collective-permute-start | bytes 49160 | tf_op jit(solution)/shard_map/ppermute | solution.py:601
  181.0 15.7 %collective-permute-start.6 = (f32[8,512]{1,0:T(8,128)S(1)}, f32[8,512]{1,0:T(8,128)S(1)}, u32[]{:S(2)}, u32[]{:S(2)}) collective-permute-start(f32[8,512]{1,0:T(8,128)S(1)} %get-tuple-element.65), channel_id=1, source_target_pairs={{2,1},{4,3},{6,5},{8,7},{10,9},{12,11},{14,13},{16,15},{18,17},{20... | collective-permute-start | bytes 49160 | tf_op jit(solution)/shard_map/ppermute | solution.py:600
  186.8 9.3 %collective-permute-start.8 = (f32[8,256]{1,0:T(8,128)S(1)}, f32[8,256]{1,0:T(8,128)S(1)}, u32[]{:S(2)}, u32[]{:S(2)}) collective-permute-start(f32[8,256]{1,0:T(8,128)S(1)} %get-tuple-element.67), channel_id=1, source_target_pairs={{0,1},{1,0},{2,3},{3,2},{4,5},{5,4},{6,7},{7,6},{8,9},{9,8},{10,11... | collective-permute-start | bytes 24584 | tf_op jit(solution)/shard_map/ppermute | solution.py:599
  187.7 20.1 %all-to-all-start.3 = ((bf16[32,8,512]{2,1,0:T(8,128)(2,1)}), bf16[32,8,512]{2,1,0:T(8,128)(2,1)S(1)}, u32[]{:S(2)}, u32[]{:S(2)}) async-start(bf16[32,8,512]{2,1,0:T(8,128)(2,1)} %broadcast_in_dim.7), calls=%async_computation.3 | async-start | bytes 524288 | tf_op jit(solution)/shard_map/all_to_all | solution.py:483
  195.9 1.8 collective-permute-start.5
  (16 other events, 12.2 us)
Sparse Core Ops, SparseCore 0:
  41.1 50.0 all-gather.1

commit v2 on v1

--- a/solution.py
+++ b/solution.py
@@ -49,6 +49,63 @@
 P_MAP = 1
 P_OUT = 1
 P_BACK = 1
+
+
+class Taken:
+    def __init__(self, source, buffer, sem):
+        self.buffer, self.shape, self.waiting = buffer, buffer.shape, True
+        self.copy = pltpu.make_async_copy(source, buffer, sem)
+        self.copy.start()
+
+    def ready(self):
+        if self.waiting:
+            self.copy.wait()
+            self.waiting = False
+        return self
+
+    def __getitem__(self, at):
+        return self.ready().buffer[at]
+
+
+class Given:
+    def __init__(self, target, buffer, sem):
+        self.buffer, self.shape, self.waiting = buffer, buffer.shape, False
+        self.copy = pltpu.make_async_copy(buffer, target, sem)
+
+    def __getitem__(self, at):
+        return self.buffer[at]
+
+    def __setitem__(self, at, value):
+        self.buffer[at] = value
+
+    def clear(self):
+        self.buffer[...] = jnp.zeros_like(self.buffer)
+
+    def whole(self):
+        self.copy.start()
+        self.waiting = True
+
+
+def staged(kernel, taken, unread, given, with_ids):
+    def body(*refs):
+        ids, refs = (refs[:1], refs[1:]) if with_ids else ((), refs)
+        sources, refs = refs[:taken], refs[taken + unread :]
+        targets, refs = refs[:given], refs[given:]
+        in_buffers, refs = refs[:taken], refs[taken:]
+        out_buffers, refs = refs[:given], refs[given:]
+        in_sems, out_sems, *rest = refs
+        ins = [Taken(s, b, in_sems.at[n]) for n, (s, b) in enumerate(zip(sources, in_buffers))]
+        outs = [Given(t, b, out_sems.at[n]) for n, (t, b) in enumerate(zip(targets, out_buffers))]
+        kernel(*ids, *ins, *outs, *rest)
+        for each in ins:
+            each.ready()
+        for each in outs:
+            if not each.waiting:
+                each.whole()
+        for each in outs:
+            each.copy.wait()
+
+    return body
 
 
 def grid_index():
@@ -119,11 +176,12 @@
     for group, lanes in enumerate(lane_groups(core)):
         here = slice(group * D, (group + 1) * D)
         padded[0:8, here] = jnp.zeros((8, D), F32)
-        padded[5:8, here] = tail_a[:, lanes].astype(F32) + tail_b[:, lanes].astype(F32)
+        tail = tail_a[:, lanes].astype(F32) + tail_b[:, lanes].astype(F32)
+        padded[5:8, here] = tail[13:16]
         padded[pl.ds(8 + core * ROWS, ROWS), here] = mixed[:, lanes].astype(F32)
         padded[pl.ds(8 + (1 - core) * ROWS, ROWS), here] = other[:, lanes].astype(F32)
 
-    gates_out[...] = jnp.zeros_like(gates_out)
+    gates_out.clear()
     for source, own in ((gate_own, True), (gate_other, False)):
         picked = jnp.where(core == 0, source[...], pltpu.roll(source[...], 7, 0))
         at = (core if own else 1 - core) * 2
@@ -157,6 +215,8 @@
         qs.append(q)
         ks.append(k)
         vs.append(pieces[2])
+    for each in (padded, pre, q_out, k_out, gates_out):
+        each.whole()
 
     strict = i > j
     lowers = []
@@ -165,6 +225,7 @@
         both = mm(jnp.concatenate([ks[b], qs[b]], axis=0), ks[b], "nt", P_KK)
         lowers.append(jnp.where(strict, columns[:, 4 + b : 5 + b] * damp * both[0:D], 0.0))
         scores_out[block(b), :] = damp * both[D:]
+    scores_out.whole()
     inverses = triangle_inverses(lowers)
     maps, decays = [], []
     for b in range(NB):
@@ -179,6 +240,8 @@
         maps_out[2 * b * D : 2 * (b + 1) * D, :] = both
         maps.append(both)
         decays.append(jnp.exp(end))
+    for each in (inverse_out, x_out, maps_out):
+        each.whole()
 
     def compose(first, first_decay, then, then_decay):
         moved = mm(first, then[0:D], passes=P_MAP)
@@ -213,28 +276,60 @@
         base_out[(2 * b + 1) * D : 2 * (b + 1) * D, :] = x[block(b), D:]
 
 
-def back_kernel(ids, full_grad, weight, back_out):
-    rows = weight[pl.ds(pl.multiple_of(ids[1] * D, D), D), :]
-    back_out[...] = mm(full_grad[...], rows, "nt")
+def back_kernel(ids, grad_own, grad_other, weight, back_out):
+    core = ids[1]
+    weight.ready()
+    head = weight[pl.ds(pl.multiple_of(core * D, D), D), :]
+    back_out[pl.ds(pl.multiple_of(core * ROWS, ROWS), ROWS), :] = mm(grad_own[...], head, "nt")
+    back_out[pl.ds(pl.multiple_of((1 - core) * ROWS, ROWS), ROWS), :] = mm(
+        grad_other[...], head, "nt"
+    )
 
 
 def slab_decay(piece):
     return jnp.sum(piece[2 * D : PACK].astype(F32), axis=0, keepdims=True)
 
 
-def outputs_kernel(
-    ids, gathered, maps, read, base, gates, back, gain,
-    states_out, deltas_out, grads_out, reach_out, packed_grad, normed_out, sent, gain_out,
-):
-    chip, core = ids[0], ids[1]
-
-    def fold(position, state):
+def forward_fold(gathered, first, last, state):
+    def step(position, state):
         piece = gathered[position]
         return slab_decay(piece) * state + (
             piece[D : 2 * D].astype(F32) - mm(state, piece[0:D], passes=P_MAP)
         )
 
-    state = lax.fori_loop(0, chip, fold, jnp.zeros((D, D), F32))
+    return lax.fori_loop(first, last, step, state)
+
+
+def backward_fold(gathered, gathered_grad, first, last, total):
+    def step(count, total):
+        position = last - 1 - count
+        piece = gathered[position]
+        return slab_decay(piece) * total + (
+            gathered_grad[position].astype(F32) - mm(total, piece[0:D], "nt", P_MAP)
+        )
+
+    return lax.fori_loop(0, last - first, step, total)
+
+
+def forward_total_kernel(gathered, out):
+    gathered.ready()
+    out[...] = forward_fold(gathered, 0, gathered.shape[0], jnp.zeros((D, D), F32))
+
+
+def backward_total_kernel(gathered, gathered_grad, out):
+    gathered.ready()
+    gathered_grad.ready()
+    count = gathered.shape[0]
+    out[...] = backward_fold(gathered, gathered_grad, 0, count, jnp.zeros((D, D), F32))
+
+
+def outputs_kernel(
+    ids, gathered, entry, maps, read, base, gates, back, gain,
+    states_out, deltas_out, grads_out, reach_out, packed_grad, normed_out, sent, gain_out,
+):
+    chip, core = ids[0], ids[1]
+    gathered.ready()
+    state = forward_fold(gathered, 0, chip, entry[...])
     states, decays = [], []
     for b in range(NB):
         states.append(state)
@@ -253,7 +348,7 @@
         deltas_out[block(b), :] = rows[D:]
         inverse = lax.rsqrt(row_sum(out * out) * (1.0 / D) + EPS)
         unit_out = out * inverse
-        normed = (unit_out * gain[...]).astype(BF16)
+        normed = (unit_out * gain[0:1, :]).astype(BF16)
         normed_out[block(b), :] = normed
 
         @pl.when((b // 2) != core)
@@ -262,12 +357,14 @@
 
         cotangent = back[block(b), :]
         total_gain = total_gain + jnp.sum(cotangent * unit_out, axis=0, keepdims=True)
-        scaled = cotangent * gain[...]
+        scaled = cotangent * gain[0:1, :]
         grad = inverse * (scaled - unit_out * (row_sum(scaled * unit_out) * (1.0 / D)))
         grads_out[block(b), :] = grad
         reach = mm(grad, read[2 * b * D : (2 * b + 1) * D, :], "tn", P_OUT)
         reach_out[block(b), :] = reach
         reaches.append(reach)
+    for each in (states_out, deltas_out, grads_out, reach_out, normed_out, sent):
+        each.whole()
     gain_out[...] = jnp.broadcast_to(total_gain, (8, D))
     state_grad = reaches[NB - 1]
     for b in range(NB - 2, -1, -1):
@@ -284,7 +381,7 @@
 ):
     columns = gate_columns(gates[...])
     i, j = grid_index()
-    sums_out[...] = jnp.zeros_like(sums_out)
+    sums_out.clear()
     for b in range(NB):
         at = block(b)
         grad, score = grads[at, :], scores[at, :]
@@ -302,22 +399,17 @@
 
 
 def grads_kernel(
-    ids, gathered, gathered_grad, maps, reach, states, deltas, inverse, x, q, k, gates, pre, padded,
+    ids, gathered, gathered_grad, leaving, maps, reach, states, deltas, inverse, x, q, k, gates, pre, padded,
     dq, dk, pull, rows_in, sums, conv_w,
     keep_out, send_out, spill_out, gate_keep, gate_send, conv_out,
     d_pre,
 ):
     chip, core = ids[0], ids[1]
-    count = gathered.shape[0]
-
-    def fold(step, total):
-        position = count - 1 - step
-        piece = gathered[position]
-        return slab_decay(piece) * total + (
-            gathered_grad[position].astype(F32) - mm(total, piece[0:D], "nt", P_MAP)
-        )
-
-    exit_grad = lax.fori_loop(0, count - 1 - chip, fold, jnp.zeros((D, D), F32))
+    gathered.ready()
+    gathered_grad.ready()
+    exit_grad = backward_fold(
+        gathered, gathered_grad, chip + 1, gathered.shape[0], leaving[...]
+    )
     columns = gate_columns(gates[...])
     i, j = grid_index()
     strict = i > j
@@ -394,7 +486,7 @@
     )
     d_logit = jnp.transpose(beta_terms)[0:8, :]
     for target, own in ((gate_keep, True), (gate_send, False)):
-        target[...] = jnp.zeros_like(target)
+        target.clear()
         for head in range(2):
 
             @pl.when(core == head)
@@ -405,10 +497,10 @@
                     target[head : head + 1, block(half)] = d_decay[b : b + 1, :]
                     target[2 + head : 3 + head, block(half)] = d_logit[b : b + 1, :]
 
-    keep_out[...] = jnp.zeros_like(keep_out)
-    send_out[...] = jnp.zeros_like(send_out)
-    spill_out[...] = jnp.zeros_like(spill_out)
-    conv_out[...] = jnp.zeros_like(conv_out)
+    keep_out.clear()
+    send_out.clear()
+    spill_out.clear()
+    conv_out.clear()
     for group, lanes in enumerate(lane_groups(core)):
         here = slice(group * D, (group + 1) * D)
         taps = [conv_w[tap : tap + 1, lanes] for tap in range(4)]
@@ -446,9 +538,12 @@
             spill_out[3 - back : 4 - back, lanes] = total
 
 
-def project_kernel(ids, normed, received, weight, gain_part, out):
+def shares_kernel(ids, normed, received, weight, gain_part, grad_own, grad_other, out, weight_out):
     core = ids[1]
+    normed.ready()
+    weight.ready()
     kept = normed[pl.ds(pl.multiple_of(core * ROWS, ROWS), ROWS), :]
+    given = normed[pl.ds(pl.multiple_of((1 - core) * ROWS, ROWS), ROWS), :]
     mine = weight[pl.ds(pl.multiple_of(core * D, D), D), :]
     others = weight[pl.ds(pl.multiple_of((1 - core) * D, D), D), :]
     share = (mm(kept, mine) + mm(received[...], others)).astype(BF16)
@@ -461,22 +556,30 @@
         out[owner, 0:height, :] = share[owner * height : (owner + 1) * height]
         out[owner, height:, :] = jnp.zeros((16, out.shape[2]), BF16)
         out[owner, height:, 0:D] = extra
-
-
-def call(kernel, shapes, args, name, flops, moved, scratch=(), smem=True):
-    specs = [pl.BlockSpec(memory_space=pltpu.VMEM) for _ in args]
-    if smem:
-        specs[0] = pl.BlockSpec(memory_space=pltpu.SMEM)
+    out.whole()
+    weight_out[...] = (mm(kept, grad_own[...], "tn") + mm(given, grad_other[...], "tn")).astype(BF16)
+
+
+def call(kernel, shapes, args, name, flops, scratch=(), with_ids=True, after=()):
+    arrays = args[1:] if with_ids else args
+    outs = [jax.ShapeDtypeStruct(shape, dtype) for shape, dtype in shapes]
+    anywhere = pl.BlockSpec(memory_space=pl.ANY)
+    moved = sum(x.size * x.dtype.itemsize for x in [*arrays, *outs])
     return pl.pallas_call(
-        kernel,
-        out_shape=[jax.ShapeDtypeStruct(shape, dtype) for shape, dtype in shapes],
-        in_specs=specs,
-        out_specs=[pl.BlockSpec(memory_space=pltpu.VMEM) for _ in shapes],
-        scratch_shapes=list(scratch),
+        staged(kernel, len(arrays), len(after), len(outs), with_ids),
+        out_shape=outs,
+        in_specs=[pl.BlockSpec(memory_space=pltpu.SMEM)] * with_ids
+        + [anywhere] * (len(arrays) + len(after)),
+        out_specs=[anywhere] * len(outs),
+        scratch_shapes=[
+            *[pltpu.VMEM(x.shape, x.dtype) for x in [*arrays, *outs]],
+            pltpu.SemaphoreType.DMA((len(arrays),)),
+            pltpu.SemaphoreType.DMA((len(outs),)),
+            *scratch,
+        ],
         name=name,
         cost_estimate=pl.CostEstimate(flops=flops, bytes_accessed=moved, transcendentals=0),
-        compiler_params=pltpu.CompilerParams(vmem_limit_bytes=40 * 2**20),
-    )(*args)
+    )(*args, *after)
 
 
 def everyone(x, axes):
@@ -484,21 +587,26 @@
 
 
 def local(mixed, log_decay, beta_logit, conv_weight, norm_gain, out_weight, out_grad):
-    chips, groups = lax.axis_size("chip"), lax.axis_size("dp")
-    ids = jnp.stack([lax.axis_index("chip"), lax.axis_index("core")]).astype(jnp.int32)
-    line = ("chip", "core")
+    near, groups = lax.axis_size("near"), lax.axis_size("dp")
+    chips = lax.axis_size("far") * near
+    ids = jnp.stack([lax.axis_index(axis) for axis in ("near", "core")]).astype(jnp.int32)
+    chip_line, line = ("far", "near"), ("far", "near", "core")
     swap = [(0, 1), (1, 0)]
     width = out_weight.shape[1]
+    rows = NB * D
+    height = ROWS // groups
 
     gates_own = jnp.concatenate([log_decay.T, beta_logit.T, jnp.zeros((4, ROWS), F32)], axis=0)
-    other = lax.ppermute(mixed, "core", swap)
-    tail = mixed[ROWS - 3 :]
+    tail = mixed[ROWS - 16 :]
     tail_a = lax.ppermute(tail, line, [(2 * c + 1, 2 * c + 2) for c in range(chips - 1)])
     tail_b = lax.ppermute(tail, line, [(2 * c + 1, 2 * c + 3) for c in range(chips - 1)])
+    other = lax.ppermute(mixed, "core", swap)
     gates_other = lax.ppermute(gates_own, "core", swap)
-    full_grad = lax.all_gather(out_grad, ("core", "dp"), axis=0, tiled=True)
-
-    rows = NB * D
+    out_grad, gates_other, tail_a, tail_b, other = lax.optimization_barrier(
+        (out_grad, gates_other, tail_a, tail_b, other)
+    )
+    grad_own = everyone(jnp.broadcast_to(out_grad[None], (groups, height, width)), "dp")
+    grad_own = grad_own.reshape(ROWS, width)
     (padded, pre, q, k, inverse, x, scores, maps, gates, packed) = call(
         maps_kernel,
         [
@@ -511,25 +619,34 @@
             ((rows, D), F32),
             ((2 * rows, D), F32),
             ((8, D), F32),
-            ((chips, PACK, D), BF16),
+            ((near, PACK, D), BF16),
         ],
         [ids, mixed, other, tail_a, tail_b, gates_own, gates_other, conv_weight],
-        "maps", 10**9, 6 * 10**6,
-    )
-    gathered = everyone(packed, "chip")
+        "maps", 10**9,
+    )
+    gathered = everyone(packed, "near")
+
+    grad_other = lax.ppermute(grad_own, "core", swap)
     read, base = call(
         readout_kernel,
         [((2 * rows, D), F32), ((2 * rows, D), F32)],
         [scores, x, q, gates],
-        "readout", 10**8, 2 * 10**6, smem=False,
+        "readout", 10**8, with_ids=False,
     )
     (back,) = call(
         back_kernel,
         [((rows, D), F32)],
-        [ids, full_grad, out_weight],
-        "back", 10**8, 2 * 10**6,
-    )
-    gain = norm_gain.reshape(1, D)
+        [ids, grad_own, grad_other, out_weight],
+        "back", 10**8,
+    )
+    (total,) = call(
+        forward_total_kernel,
+        [((D, D), F32)],
+        [gathered],
+        "forward_total", 10**8, with_ids=False, after=[read, back],
+    )
+    entry = lax.ppermute(total, "far", [(0, 1)])
+    gain = jnp.broadcast_to(norm_gain.reshape(1, D), (8, D))
     (states, deltas, grads, reach, packed_grad, normed, sent, gain_part) = call(
         outputs_kernel,
         [
@@ -537,15 +654,15 @@
             ((rows, D), F32),
             ((rows, D), F32),
             ((rows, D), F32),
-            ((chips, D, D), BF16),
+            ((near, D, D), BF16),
             ((rows, D), BF16),
             ((ROWS, D), BF16),
             ((8, D), F32),
         ],
-        [ids, gathered, maps, read, base, gates, back, gain],
-        "outputs", 10**9, 6 * 10**6,
-    )
-    gathered_grad = everyone(packed_grad, "chip")
+        [ids, gathered, entry, maps, read, base, gates, back, gain],
+        "outputs", 10**9,
+    )
+    gathered_grad = everyone(packed_grad, "near")
     received = lax.ppermute(sent, "core", swap)
     dq, dk, pull, row_terms, sums = call(
         local_grads_kernel,
@@ -557,27 +674,23 @@
             ((8, D), F32),
         ],
         [scores, deltas, grads, states, q, k, gates],
-        "local_grads", 10**9, 4 * 10**6, smem=False,
-    )
-
-    height = ROWS // groups
-    (share,) = call(
-        project_kernel,
-        [((groups, height + 16, width), BF16)],
-        [ids, normed, received, out_weight, gain_part],
-        "project", 10**8, 2 * 10**6,
-    )
-    shares = everyone(share, "dp").astype(F32)
-    result = jnp.sum(shares[:, :height], axis=0).astype(BF16)
-    gain_rows = jnp.sum(shares[:, height : height + 2, :D], axis=0)
-
-    weight_part = jnp.einsum("tv,td->vd", normed, full_grad, preferred_element_type=F32)
-    weight_parts = everyone(weight_part.astype(BF16).reshape(chips, D // chips, width), "chip")
-    weight_sum = jnp.sum(weight_parts.astype(F32), axis=0)
-    grad_weight = lax.ppermute(
-        weight_sum, line, [(2 * c + h, h * chips + c) for c in range(chips) for h in range(2)]
-    )
-
+        "local_grads", 10**9, with_ids=False,
+    )
+    share, weight_part = call(
+        shares_kernel,
+        [((groups, height + 16, width), BF16), ((D, width), BF16)],
+        [ids, normed, received, out_weight, gain_part, grad_own, grad_other],
+        "shares", 10**8, after=[sums],
+    )
+
+    (total,) = call(
+        backward_total_kernel,
+        [((D, D), F32)],
+        [gathered, gathered_grad],
+        "backward_total", 10**8, with_ids=False,
+    )
+    total, share = lax.optimization_barrier((total, share))
+    leaving = lax.ppermute(total, "far", [(1, 0)])
     keep, send, spill, gate_keep, gate_send, conv_part = call(
         grads_kernel,
         [
@@ -589,23 +702,42 @@
             ((8, 4 * D), F32),
         ],
         [
-            ids, gathered, gathered_grad, maps, reach, states, deltas, inverse, x, q, k, gates,
+            ids, gathered, gathered_grad, leaving, maps, reach, states, deltas, inverse, x, q, k, gates,
             pre, padded, dq, dk, pull, row_terms, sums, conv_weight,
         ],
-        "grads", 10**9, 8 * 10**6,
+        "grads", 10**9,
         scratch=[pltpu.VMEM((rows + 8, 3 * D), F32)],
+    )
+    shares = everyone(share, "dp").astype(F32)
+    result = jnp.sum(shares[:, :height], axis=0).astype(BF16)
+    gain_rows = jnp.sum(shares[:, height : height + 2, :D], axis=0)
+
+    gain_row = gain_rows[0:1] + gain_rows[1:2]
+    totals = conv_part + jnp.pad(gain_row, ((4, 3), (0, 3 * D)))
+    totals = totals + lax.ppermute(totals, "core", swap)
+    totals, send, spill, gate_send, weight_part = lax.optimization_barrier(
+        (totals, send, spill, gate_send, weight_part)
     )
     taken = lax.ppermute(send, "core", swap)
     gate_taken = lax.ppermute(gate_send, "core", swap)
     spill_a = lax.ppermute(spill, line, [(2 * c, 2 * c - 1) for c in range(1, chips)])
     spill_b = lax.ppermute(spill, line, [(2 * c + 1, 2 * c - 1) for c in range(1, chips)])
-
-    high = gain_rows[0:1] + gain_rows[1:2]
-    gain_high = high.astype(BF16).astype(F32)
-    extra = jnp.pad(jnp.concatenate([gain_high, high - gain_high]), ((4, 2), (0, 3 * D)))
-    small = (conv_part + extra).astype(BF16)
-    smalls = everyone(jnp.broadcast_to(small, (2 * chips, 8, 4 * D)), line)
-    totals = jnp.sum(smalls.astype(F32), axis=0)
+    distance = 1
+    while distance < chips:
+        pairs = [(c, c ^ distance) for c in range(chips)]
+        seen = lax.ppermute(totals, chip_line, pairs)
+        last = distance * 2 == chips
+        if not last:
+            totals = totals + seen
+        distance *= 2
+    grad_taps = totals[0:4] + seen[0:4]
+    grad_gain = totals[4, :D] + seen[4, :D]
+
+    weight_parts = everyone(weight_part.reshape(chips, D // chips, width), chip_line)
+    weight_sum = jnp.sum(weight_parts.astype(F32), axis=0)
+    grad_weight = lax.ppermute(
+        weight_sum, line, [(2 * c + h, h * chips + c) for c in range(chips) for h in range(2)]
+    )
 
     spilled = jnp.pad((spill_a + spill_b)[0:3], ((ROWS - 3, 0), (0, 0)))
     grad_mixed = (keep + taken.astype(F32) + spilled).astype(BF16)
@@ -615,16 +747,16 @@
         grad_mixed,
         gate_grads[0:2].T,
         gate_grads[2:4].T,
-        totals[0:4],
-        totals[4, :D] + totals[5, :D],
+        grad_taps,
+        grad_gain,
         grad_weight,
     )
 
 
 def solution(mesh):
     groups, line = mesh.shape["dp"], mesh.shape["ctx"]
-    fine = Mesh(mesh.devices.reshape(groups, line // 2, 2), ("dp", "chip", "core"))
-    ctx = ("chip", "core")
+    ctx = ("far", "near", "core")
+    fine = Mesh(mesh.devices.reshape(groups, 2, line // 4, 2), ("dp", *ctx))
     return jax.shard_map(
         local,
         mesh=fine,

time: 220 us -> 157 us (0.71)
  waiting for transfers between devices: 73.6 us -> 45 us
  local copies, waits for them, and re-layouts: 35.7 us -> 8.48 us
  Pallas kernels: 20.1 us -> 42.6 us
  blocking collectives: 16.7 us -> 0 us
  between operations: 14.4 us -> 1.08 us
    all_gather x1 -> x0, waiting for transfers between devices: 50.9 us -> none  [local(): full_grad = lax.all_gather(out_grad, ('core', 'dp'), axis=0, tiled=True)]
    unnamed x99 -> x41, local copies, waits for them, and re-layouts: 33 us -> 4.71 us
    ppermute x0 -> x8, waiting for transfers between devices: none -> 24.2 us  [the longest x4 12.8 us: local(): seen = lax.ppermute(totals, chip_line, pairs)]
    pallas_call x7 -> x9, Pallas kernels: 20.1 us -> 42.6 us  [call(): pl.pallas_call(staged(kernel, len(arrays), len(after), len(outs), with_id...]
    all_to_all x1 -> x0, blocking collectives: 16.7 us -> none  [everyone(): return lax.all_to_all(x, axes, 0, 0, tiled=True)]
    ppermute x0 -> x8, starting transfers between devices: none -> 9.99 us  [the longest x4 6.11 us: local(): seen = lax.ppermute(totals, chip_line, pairs)]
    all_to_all x4 -> x5, starting transfers between devices: 31.7 us -> 25.6 us  [everyone(): return lax.all_to_all(x, axes, 0, 0, tiled=True)]
    ppermute x1, starting transfers between devices: 0.03 us -> 5.56 us  [local(): gates_other = lax.ppermute(gates_own, 'core', swap)]
  transfers between devices with their start and end apart: 15 -> 23, of which waited for: 6 -> 11; matrix products, arithmetic and copies ran while one was open for 3% -> 3% of each run, Pallas kernels for 2% -> 20%
where the time goes in v2:
time: 157 us; the launch traced here: 154 us
  starting transfers between devices  52.8 us (34%)
  waiting for transfers between devices  45 us (29%)
  Pallas kernels  42.6 us (27%)
  local copies, waits for them, and re-layouts  8.48 us (5%)
  other arithmetic  4.2 us (3%)
    pallas_call x9, Pallas kernels, call(): pl.pallas_call(staged(kernel, len(arrays), len(after), len(outs), with_id...  42.6 us
    all_to_all x5, starting transfers between devices, everyone(): return lax.all_to_all(x, axes, 0, 0, tiled=True)  25.6 us
    all_to_all x5, waiting for transfers between devices, everyone(): return lax.all_to_all(x, axes, 0, 0, tiled=True)  18.5 us
    ppermute x4, waiting for transfers between devices, local(): seen = lax.ppermute(totals, chip_line, pairs)  12.8 us
    ppermute x4, starting transfers between devices, local(): seen = lax.ppermute(totals, chip_line, pairs)  6.11 us
    ppermute x1, starting transfers between devices, local(): gates_other = lax.ppermute(gates_own, 'core', swap)  5.56 us
    ppermute x1, waiting for transfers between devices, local(): leaving = lax.ppermute(total, 'far', [(1, 0)])  5.2 us
    ppermute x1, waiting for transfers between devices, local(): entry = lax.ppermute(total, 'far', [(0, 1)])  5.07 us
  transfers between devices with their start and end apart: 23, of which 11 were waited for; matrix products, arithmetic and copies ran while one was open for 3% of the time, Pallas kernels for 20%

profile of v2, /device:TPU:8, one launch (start us, length us, event | category | flops | bytes accessed | tf_op | source)
XLA Modules:
  0.0 154.2 jit_solution(4513000481592421512)
XLA Ops:
  0.7 0.7 slice.36
  1.5 1.3 collective-permute-start.1
  2.7 0.7 collective-permute-start.2
  3.5 0.8 maximum_maximum_fusion.refs_5_
  4.3 5.6 %collective-permute-start = (f32[8,256]{1,0:T(8,128)S(1)}, f32[8,256]{1,0:T(8,128)S(1)}, u32[]{:S(2)}, u32[]{:S(2)}) collective-permute-start(f32[8,256]{1,0:T(8,128)S(1)} %maximum_maximum_fusion.refs_5_), channel_id=1, source_target_pairs={{0,1},{1,0},{2,3},{3,2},{4,5},{5,4},{6,7},{7,6},{8,9},{9,8},{10,11... | collective-permute-start | bytes 24584 | tf_op jit(solution)/shard_map/ppermute | solution.py:604
  9.8 0.8 collective-permute-done.refs_6_
  10.7 1.8 %broadcast_in_dim.7 = bf16[8,32,1024]{2,1,0:T(8,128)(2,1)} broadcast(bf16[32,1024]{1,0:T(8,128)(2,1)} %param.13), dimensions={1,2} | broadcast | bytes 589824 | tf_op jit(solution)/shard_map/broadcast_in_dim | solution.py:608
  12.5 6.0 %all-to-all-start.1 = ((bf16[8,32,1024]{2,1,0:T(8,128)(2,1)}), bf16[8,32,1024]{2,1,0:T(8,128)(2,1)S(1)}, u32[]{:S(2)}, u32[]{:S(2)}) async-start(bf16[8,32,1024]{2,1,0:T(8,128)(2,1)} %broadcast_in_dim.7), calls=%async_computation.1 | async-start | bytes 1048576 | tf_op jit(solution)/shard_map/all_to_all | solution.py:586
  19.1 8.2 %maps.1 = (f32[520,384]{1,0:T(8,128)}, f32[512,384]{1,0:T(8,128)}, f32[512,128]{1,0:T(8,128)}, f32[512,128]{1,0:T(8,128)}, f32[512,128]{1,0:T(8,128)}, /*index=5...) custom-call(s32[2]{0:T(128)} %pad_add_fusion.1.refs_0_, ...), custom_call_target="tpu_custom_call" | custom-call | flops 1000000000 | bytes 4825088 | tf_op jit(solution)/shard_map/maps/pallas_call | solution.py:568
  27.3 4.2 %all-to-all-done.1 = bf16[8,32,1024]{2,1,0:T(8,128)(2,1)S(1)} async-done(((bf16[8,32,1024]{2,1,0:T(8,128)(2,1)}), bf16[8,32,1024]{2,1,0:T(8,128)(2,1)S(1)}, u32[]{:S(2)}, u32[]{:S(2)}) %all-to-all-start.1) | async-done | bytes 524320 | tf_op jit(solution)/shard_map/all_to_all | solution.py:586
  31.4 6.7 %all-to-all-start = ((bf16[8,272,128]{2,1,0:T(8,128)(2,1)}), bf16[8,272,128]{2,1,0:T(8,128)(2,1)S(1)}, u32[]{:S(2)}, u32[]{:S(2)}) async-start(bf16[8,272,128]{2,1,0:T(8,128)(2,1)} %get-tuple-element.56), calls=%async_computation | async-start | bytes 1114112 | tf_op jit(solution)/shard_map/all_to_all | solution.py:586
  38.2 2.8 %readout.1 = (f32[1024,128]{1,0:T(8,128)}, f32[1024,128]{1,0:T(8,128)}) custom-call(f32[512,128]{1,0:T(8,128)} %get-tuple-element.57.refs_0_, f32[512,256]{1,0:T(8,128)} %get-tuple-element.58.refs_1_.refs_9_, f32[512,128]{1,0:T(8,128)} %get-tuple-element.59.refs_2_.refs_4_.refs_10_, f32[8,128]{1,0:T(8,128)} %get-tuple-element.60.refs_3_.refs_6_.refs_12_), custom_call_target="tpu_custom_call" | custom-call | flops 100000000 | bytes 2101248 | tf_op jit(solution)/shard_map/readout/pallas_call | solution.py:568
  41.0 0.8 copy-done.3
  41.8 3.6 %back.1.refs_2_.refs_7_ = f32[512,128]{1,0:T(8,128)} custom-call(s32[2]{0:T(128)} %pad_add_fusion.1.refs_0_, bf16[256,1024]{1,0:T(8,128)(2,1)} %bitcast.13, bf16[256,1024]{1,0:T(8,128)(2,1)} %copy-done.3, bf16[256,1024]{1,0:T(8,128)(2,1)} %refs_3_.3), custom_call_target="tpu_custom_call" | custom-call | flops 100000000 | bytes 1835008 | tf_op jit(solution)/shard_map/back/pallas_call | solution.py:568
  45.4 11.2 %all-to-all-done.refs_0_.refs_1_ = bf16[8,272,128]{2,1,0:T(8,128)(2,1)S(1)} async-done(((bf16[8,272,128]{2,1,0:T(8,128)(2,1)}), bf16[8,272,128]{2,1,0:T(8,128)(2,1)S(1)}, u32[]{:S(2)}, u32[]{:S(2)}) %all-to-all-start) | async-done | bytes 557088 | tf_op jit(solution)/shard_map/all_to_all | solution.py:586
  56.6 0.8 copy-done
  57.4 2.8 %forward_total.1 = f32[128,128]{1,0:T(8,128)} custom-call(bf16[8,272,128]{2,1,0:T(8,128)(2,1)} %copy-done, f32[1024,128]{1,0:T(8,128)} %get-tuple-element.61.refs_1_.refs_4_, f32[512,128]{1,0:T(8,128)} %back.1.refs_2_.refs_7_), custom_call_target="tpu_custom_call" | custom-call | flops 100000000 | bytes 622592 | tf_op jit(solution)/shard_map/forward_total/pallas_call | solution.py:568
  60.3 1.3 collective-permute-start.5
  61.6 5.1 %collective-permute-done.5.refs_2_ = f32[128,128]{1,0:T(8,128)S(1)} collective-permute-done((f32[128,128]{1,0:T(8,128)}, f32[128,128]{1,0:T(8,128)S(1)}, u32[]{:S(2)}, u32[]{:S(2)}) %collective-permute-start.5) | collective-permute-done | bytes 65568 | tf_op jit(solution)/shard_map/ppermute | solution.py:648
  66.6 0.6 broadcast_in_dim.16.refs_8_
  67.3 5.2 %outputs.1 = (f32[512,128]{1,0:T(8,128)}, f32[512,128]{1,0:T(8,128)}, f32[512,128]{1,0:T(8,128)}, f32[512,128]{1,0:T(8,128)}, bf16[8,128,128]{2,1,0:T(8,128)(2,1...) custom-call(s32[2]{0:T(128)} %pad_add_fusion.1.refs_0_, bf16[8,272,128]{2,1,0:T(8,128)(2,1)} %copy-done, ...), custom_call_target="tpu_custom_call" | custom-call | flops 1000000000 | bytes 3977216 | tf_op jit(solution)/shard_map/outputs/pallas_call | solution.py:568
  72.5 3.4 %all-to-all-start.2 = ((bf16[8,128,128]{2,1,0:T(8,128)(2,1)}), bf16[8,128,128]{2,1,0:T(8,128)(2,1)S(1)}, u32[]{:S(2)}, u32[]{:S(2)}) async-start(bf16[8,128,128]{2,1,0:T(8,128)(2,1)} %get-tuple-element.65), calls=%async_computation.2 | async-start | bytes 524288 | tf_op jit(solution)/shard_map/all_to_all | solution.py:586
  76.0 3.7 %local_grads.1 = (f32[512,128]{1,0:T(8,128)}, f32[512,128]{1,0:T(8,128)}, f32[512,128]{1,0:T(8,128)}, f32[512,128]{1,0:T(8,128)}, f32[8,128]{1,0:T(8,128)}) custom-call(f32[512,128]{1,0:T(8,128)} %get-tuple-element.57.refs_0_, f32[512,128]{1,0:T(8,128)} %get-tuple-element.69.refs_1_.refs_7_, f32[512,128]{1,0:T(8,128)} %get-tuple-element.70.refs_2_, ...), custom_call_target="tpu_custom_call" | custom-call | flops 1000000000 | bytes 2629632 | tf_op jit(solution)/shard_map/local_grads/pallas_call | solution.py:568
  79.7 0.6 copy-done.8
  80.4 3.5 %shares.1 = (bf16[8,48,1024]{2,1,0:T(8,128)(2,1)}, bf16[128,1024]{1,0:T(8,128)(2,1)}) custom-call(s32[2]{0:T(128)} %pad_add_fusion.1.refs_0_, bf16[512,128]{1,0:T(8,128)(2,1)} %get-tuple-element.66.refs_1_, bf16[256,128]{1,0:T(8,128)(2,1)} %copy-done.8, bf16[256,1024]{1,0:T(8,128)(2,1)} %refs_3_.3, f32[8,128]{1,0:T(8,128)} %get-tuple-element.68.refs_4_, ...), custom_call_target="tpu_custom_call" | custom-call | flops 100000000 | bytes 2822144 | tf_op jit(solution)/shard_map/shares/pallas_call | solution.py:568
  83.9 3.1 %all-to-all-done.2.refs_1_.refs_2_ = bf16[8,128,128]{2,1,0:T(8,128)(2,1)S(1)} async-done(((bf16[8,128,128]{2,1,0:T(8,128)(2,1)}), bf16[8,128,128]{2,1,0:T(8,128)(2,1)S(1)}, u32[]{:S(2)}, u32[]{:S(2)}) %all-to-all-start.2) | async-done | bytes 262176 | tf_op jit(solution)/shard_map/all_to_all | solution.py:586
  87.0 0.7 copy-done.2
  87.7 3.0 %backward_total.1 = f32[128,128]{1,0:T(8,128)} custom-call(bf16[8,272,128]{2,1,0:T(8,128)(2,1)} %copy-done, bf16[8,128,128]{2,1,0:T(8,128)(2,1)} %copy-done.2), custom_call_target="tpu_custom_call" | custom-call | flops 100000000 | bytes 884736 | tf_op jit(solution)/shard_map/backward_total/pallas_call | solution.py:568
  90.8 3.9 %all-to-all-start.3 = ((bf16[8,48,1024]{2,1,0:T(8,128)(2,1)}), bf16[8,48,1024]{2,1,0:T(8,128)(2,1)S(1)}, u32[]{:S(2)}, u32[]{:S(2)}) async-start(bf16[8,48,1024]{2,1,0:T(8,128)(2,1)} %get-tuple-element.75), calls=%async_computation.3 | async-start | bytes 1572864 | tf_op jit(solution)/shard_map/all_to_all | solution.py:586
  94.7 2.6 %collective-permute-start.7 = (f32[128,128]{1,0:T(8,128)S(1)}, f32[128,128]{1,0:T(8,128)S(1)}, u32[]{:S(2)}, u32[]{:S(2)}) collective-permute-start(f32[128,128]{1,0:T(8,128)S(1)} %copy-done.6), channel_id=1, source_target_pairs={{16,0},{17,1},{18,2},{19,3},{20,4},{21,5},{22,6},{23,7},{24,8},{25... | collective-permute-start | bytes 196616 | tf_op jit(solution)/shard_map/ppermute | solution.py:693
  97.3 5.2 %collective-permute-done.7.refs_3_ = f32[128,128]{1,0:T(8,128)S(1)} collective-permute-done((f32[128,128]{1,0:T(8,128)S(1)}, f32[128,128]{1,0:T(8,128)S(1)}, u32[]{:S(2)}, u32[]{:S(2)}) %collective-permute-start.7) | collective-permute-done | bytes 65568 | tf_op jit(solution)/shard_map/ppermute | solution.py:693
  102.5 0.6 copy-done.5
  103.1 9.8 %grads.1 = (f32[256,512]{1,0:T(8,128)}, bf16[256,512]{1,0:T(8,128)(2,1)}, f32[8,512]{1,0:T(8,128)}, f32[8,256]{1,0:T(8,128)}, f32[8,256]{1,0:T(8,128)}, /*index=5*/f32[8,512]{1,0:T(8,128)}) custom-call(s32[2]{0:T(128)} %pad_add_fusion.1.refs_0_, bf16[8,272,128]{2,1,0:T(8,128)(2,1)} %copy-done, bf16[8,128,128]{2,1,0:T(8,128)(2,1)} %copy-done.2, ...), custom_call_target="tpu_custom_call" | custom-call | flops 1000000000 | bytes 6991872 | tf_op jit(solution)/shard_map/grads/pallas_call | solution.py:568
  113.7 1.2 collective-permute-done.8
  115.2 3.5 %collective-permute-done.13 = f32[8,512]{1,0:T(8,128)S(1)} collective-permute-done((f32[8,512]{1,0:T(8,128)S(1)}, f32[8,512]{1,0:T(8,128)S(1)}, u32[]{:S(2)}, u32[]{:S(2)}) %collective-permute-start.13) | collective-permute-done | bytes 16416 | tf_op jit(solution)/shard_map/ppermute | solution.py:728
  118.7 0.7 slice_reduce_fusion
  119.4 4.7 %collective-permute-start.10 = (f32[8,512]{1,0:T(8,128)S(1)}, f32[8,512]{1,0:T(8,128)S(1)}, u32[]{:S(2)}, u32[]{:S(2)}) collective-permute-start(f32[8,512]{1,0:T(8,128)S(1)} %copy-done.15), channel_id=1, source_target_pairs={{2,1},{4,3},{6,5},{8,7},{10,9},{12,11},{14,13},{16,15},{18,17},{20... | collective-permute-start | bytes 49160 | tf_op jit(solution)/shard_map/ppermute | solution.py:723
  124.1 0.7 collective-permute-start.11
  124.8 0.8 collective-permute-start.9
  125.6 5.6 %all-to-all-start.4 = ((bf16[16,8,1024]{2,1,0:T(8,128)(2,1)}), bf16[16,8,1024]{2,1,0:T(8,128)(2,1)S(1)}, u32[]{:S(2)}, u32[]{:S(2)}) async-start(bf16[16,8,1024]{2,1,0:T(8,128)(2,1)} %bitcast.8), calls=%async_computation.4 | async-start | bytes 524288 | tf_op jit(solution)/shard_map/all_to_all | solution.py:586
  131.2 5.5 %collective-permute-start.15 = (f32[8,512]{1,0:T(8,128)S(1)}, f32[8,512]{1,0:T(8,128)S(1)}, u32[]{:S(2)}, u32[]{:S(2)}) collective-permute-start(f32[8,512]{1,0:T(8,128)S(1)} %add.51), channel_id=1, source_target_pairs={{0,8},{2,10},{4,12},{6,14},{8,0},{10,2},{12,4},{14,6},{16,24},{18,... | collective-permute-start | bytes 49160 | tf_op jit(solution)/shard_map/ppermute | solution.py:728
  137.3 6.1 %collective-permute-done.15 = f32[8,512]{1,0:T(8,128)S(1)} collective-permute-done((f32[8,512]{1,0:T(8,128)S(1)}, f32[8,512]{1,0:T(8,128)S(1)}, u32[]{:S(2)}, u32[]{:S(2)}) %collective-permute-start.15) | collective-permute-done | bytes 16416 | tf_op jit(solution)/shard_map/ppermute | solution.py:728
  144.0 3.2 %collective-permute-done.16 = f32[8,512]{1,0:T(8,128)S(1)} collective-permute-done((f32[8,512]{1,0:T(8,128)S(1)}, f32[8,512]{1,0:T(8,128)S(1)}, u32[]{:S(2)}, u32[]{:S(2)}) %collective-permute-start.16) | collective-permute-done | bytes 16416 | tf_op jit(solution)/shard_map/ppermute | solution.py:728
  147.1 0.6 slice_add_fusion
  148.3 3.1 %collective-permute-start.17 = (f32[8,1024]{1,0:T(8,128)S(1)}, f32[8,1024]{1,0:T(8,128)S(1)}, u32[]{:S(2)}, u32[]{:S(2)}) collective-permute-start(f32[8,1024]{1,0:T(8,128)S(1)} %convert_reduce_fusion), channel_id=1, source_target_pairs={{0,0},{1,16},{2,1},{3,17},{4,2},{5,18},{6,3},{7,19},{8,4},{9,20},{... | collective-permute-start | bytes 98312 | tf_op jit(solution)/shard_map/ppermute | solution.py:738
  151.4 0.8 add_convert_fusion
  152.2 1.4 collective-permute-done.17
  153.5 0.6 copy.15
  (71 shorter events, 3.6 us)
Async XLA Ops:
  0.6 10.1 %collective-permute-start.3 = (bf16[256,512]{1,0:T(8,128)(2,1)}, bf16[256,512]{1,0:T(8,128)(2,1)S(1)}, u32[]{:S(2)}, u32[]{:S(2)}) collective-permute-start(bf16[256,512]{1,0:T(8,128)(2,1)} %refs_1_.1), channel_id=1, source_target_pairs={{0,1},{1,0},{2,3},{3,2},{4,5},{5,4},{6,7},{7,6},{8,9},{9,8},{10,11... | collective-permute-start | bytes 786440 | tf_op jit(solution)/shard_map/ppermute | solution.py:603
  1.5 9.2 %collective-permute-start.1 = (bf16[16,512]{1,0:T(8,128)(2,1)S(1)}, bf16[16,512]{1,0:T(8,128)(2,1)S(1)}, u32[]{:S(2)}, u32[]{:S(2)}) collective-permute-start(bf16[16,512]{1,0:T(8,128)(2,1)S(1)} %slice.36), channel_id=1, source_target_pairs={{1,2},{3,4},{5,6},{7,8},{9,10},{11,12},{13,14},{15,16},{17,18},{19... | collective-permute-start | bytes 49160 | tf_op jit(solution)/shard_map/ppermute | solution.py:601
  2.7 7.9 %collective-permute-start.2 = (bf16[16,512]{1,0:T(8,128)(2,1)S(1)}, bf16[16,512]{1,0:T(8,128)(2,1)S(1)}, u32[]{:S(2)}, u32[]{:S(2)}) collective-permute-start(bf16[16,512]{1,0:T(8,128)(2,1)S(1)} %slice.36), channel_id=1, source_target_pairs={{1,3},{3,5},{5,7},{7,9},{9,11},{11,13},{13,15},{15,17},{17,19},{19... | collective-permute-start | bytes 49160 | tf_op jit(solution)/shard_map/ppermute | solution.py:602
  4.3 14.8 %copy-start.10 = (f32[8,256]{1,0:T(8,128)}, f32[8,256]{1,0:T(8,128)S(1)}, u32[]{:S(2)}) copy-start(f32[8,256]{1,0:T(8,128)S(1)} %maximum_maximum_fusion.refs_5_) | copy-start | bytes 24580
  4.3 6.4 %collective-permute-start = (f32[8,256]{1,0:T(8,128)S(1)}, f32[8,256]{1,0:T(8,128)S(1)}, u32[]{:S(2)}, u32[]{:S(2)}) collective-permute-start(f32[8,256]{1,0:T(8,128)S(1)} %maximum_maximum_fusion.refs_5_), channel_id=1, source_target_pairs={{0,1},{1,0},{2,3},{3,2},{4,5},{5,4},{6,7},{7,6},{8,9},{9,8},{10,11... | collective-permute-start | bytes 24584 | tf_op jit(solution)/shard_map/ppermute | solution.py:604
  10.7 8.4 %copy-start.19 = (f32[8,256]{1,0:T(8,128)}, f32[8,256]{1,0:T(8,128)S(1)}, u32[]{:S(2)}) copy-start(f32[8,256]{1,0:T(8,128)S(1)} %collective-permute-done.refs_6_) | copy-start | bytes 24580
  10.7 8.4 %copy-start.16 = (bf16[16,512]{1,0:T(8,128)(2,1)}, bf16[16,512]{1,0:T(8,128)(2,1)S(1)}, u32[]{:S(2)}) copy-start(bf16[16,512]{1,0:T(8,128)(2,1)S(1)} %collective-permute-done.1.refs_3_) | copy-start | bytes 49156
  10.7 8.4 %copy-start.17 = (bf16[16,512]{1,0:T(8,128)(2,1)}, bf16[16,512]{1,0:T(8,128)(2,1)S(1)}, u32[]{:S(2)}) copy-start(bf16[16,512]{1,0:T(8,128)(2,1)S(1)} %collective-permute-done.2.refs_4_) | copy-start | bytes 49156
  10.7 8.4 %copy-start.13 = (bf16[256,512]{1,0:T(8,128)(2,1)}, bf16[256,512]{1,0:T(8,128)(2,1)S(1)}, u32[]{:S(2)}) copy-start(bf16[256,512]{1,0:T(8,128)(2,1)S(1)} %collective-permute-done.3.refs_2_) | copy-start | bytes 786436
  12.5 19.0 %all-to-all-start.1 = ((bf16[8,32,1024]{2,1,0:T(8,128)(2,1)}), bf16[8,32,1024]{2,1,0:T(8,128)(2,1)S(1)}, u32[]{:S(2)}, u32[]{:S(2)}) async-start(bf16[8,32,1024]{2,1,0:T(8,128)(2,1)} %broadcast_in_dim.7), calls=%async_computation.1 | async-start | bytes 1048576 | tf_op jit(solution)/shard_map/all_to_all | solution.py:586
  31.4 9.5 %copy-start.1 = (bf16[8,32,1024]{2,1,0:T(8,128)(2,1)}, bf16[8,32,1024]{2,1,0:T(8,128)(2,1)S(1)}, u32[]{:S(2)}) copy-start(bf16[8,32,1024]{2,1,0:T(8,128)(2,1)S(1)} %all-to-all-done.1) | copy-start | bytes 1572868
  31.4 25.2 %all-to-all-start = ((bf16[8,272,128]{2,1,0:T(8,128)(2,1)}), bf16[8,272,128]{2,1,0:T(8,128)(2,1)S(1)}, u32[]{:S(2)}, u32[]{:S(2)}) async-start(bf16[8,272,128]{2,1,0:T(8,128)(2,1)} %get-tuple-element.56), calls=%async_computation | async-start | bytes 1114112 | tf_op jit(solution)/shard_map/all_to_all | solution.py:586
  38.2 2.8 %collective-permute-start.4 = (bf16[256,1024]{1,0:T(8,128)(2,1)S(1)}, bf16[256,1024]{1,0:T(8,128)(2,1)S(1)}, u32[]{:S(2)}, u32[]{:S(2)}) collective-permute-start(bf16[256,1024]{1,0:T(8,128)(2,1)S(1)} %bitcast.12), channel_id=1, source_target_pairs={{0,1},{1,0},{2,3},{3,2},{4,5},{5,4},{6,7},{7,6},{8,9},{9,8},{10,11... | collective-permute-start | bytes 1572872 | tf_op jit(solution)/shard_map/ppermute | solution.py:629
  41.0 25.7 %copy-start.11 = (f32[128]{0:T(128)S(1)}, f32[128]{0:T(128)}, u32[]{:S(2)}) copy-start(f32[128]{0:T(128)} %param.11) | copy-start | bytes 1540
  41.0 0.8 copy-start.3
  56.6 0.8 copy-start
  60.3 6.4 %collective-permute-start.5 = (f32[128,128]{1,0:T(8,128)}, f32[128,128]{1,0:T(8,128)S(1)}, u32[]{:S(2)}, u32[]{:S(2)}) collective-permute-start(f32[128,128]{1,0:T(8,128)} %forward_total.1), channel_id=1, source_target_pairs={{0,16},{1,17},{2,18},{3,19},{4,20},{5,21},{6,22},{7,23},{8,24},{9,... | collective-permute-start | bytes 196616 | tf_op jit(solution)/shard_map/ppermute | solution.py:648
  66.6 0.6 copy-start.14
  72.5 14.5 %all-to-all-start.2 = ((bf16[8,128,128]{2,1,0:T(8,128)(2,1)}), bf16[8,128,128]{2,1,0:T(8,128)(2,1)S(1)}, u32[]{:S(2)}, u32[]{:S(2)}) async-start(bf16[8,128,128]{2,1,0:T(8,128)(2,1)} %get-tuple-element.65), calls=%async_computation.2 | async-start | bytes 524288 | tf_op jit(solution)/shard_map/all_to_all | solution.py:586
  75.9 3.8 %collective-permute-start.6 = (bf16[256,128]{1,0:T(8,128)(2,1)}, bf16[256,128]{1,0:T(8,128)(2,1)S(1)}, u32[]{:S(2)}, u32[]{:S(2)}) collective-permute-start(bf16[256,128]{1,0:T(8,128)(2,1)} %get-tuple-element.67), channel_id=1, source_target_pairs={{0,1},{1,0},{2,3},{3,2},{4,5},{5,4},{6,7},{7,6},{8,9},{9,8},{10,11... | collective-permute-start | bytes 196616 | tf_op jit(solution)/shard_map/ppermute | solution.py:666
  79.7 0.6 copy-start.8
  87.0 0.7 copy-start.2
  90.8 3.9 %copy-start.6 = (f32[128,128]{1,0:T(8,128)S(1)}, f32[128,128]{1,0:T(8,128)}, u32[]{:S(2)}) copy-start(f32[128,128]{1,0:T(8,128)} %backward_total.1) | copy-start | bytes 196612
  90.8 22.2 %all-to-all-start.3 = ((bf16[8,48,1024]{2,1,0:T(8,128)(2,1)}), bf16[8,48,1024]{2,1,0:T(8,128)(2,1)S(1)}, u32[]{:S(2)}, u32[]{:S(2)}) async-start(bf16[8,48,1024]{2,1,0:T(8,128)(2,1)} %get-tuple-element.75), calls=%async_computation.3 | async-start | bytes 1572864 | tf_op jit(solution)/shard_map/all_to_all | solution.py:586
  94.7 7.8 %collective-permute-start.7 = (f32[128,128]{1,0:T(8,128)S(1)}, f32[128,128]{1,0:T(8,128)S(1)}, u32[]{:S(2)}, u32[]{:S(2)}) collective-permute-start(f32[128,128]{1,0:T(8,128)S(1)} %copy-done.6), channel_id=1, source_target_pairs={{16,0},{17,1},{18,2},{19,3},{20,4},{21,5},{22,6},{23,7},{24,8},{25... | collective-permute-start | bytes 196616 | tf_op jit(solution)/shard_map/ppermute | solution.py:693
  102.5 0.6 copy-start.5
  112.9 0.7 copy-start.7
  112.9 2.0 %copy-start.18 = (f32[8,256]{1,0:T(8,128)S(1)}, f32[8,256]{1,0:T(8,128)}, u32[]{:S(2)}) copy-start(f32[8,256]{1,0:T(8,128)} %get-tuple-element.94) | copy-start | bytes 24580
  113.0 6.4 %copy-start.15 = (f32[8,512]{1,0:T(8,128)S(1)}, f32[8,512]{1,0:T(8,128)}, u32[]{:S(2)}) copy-start(f32[8,512]{1,0:T(8,128)} %get-tuple-element.92) | copy-start | bytes 49156
  113.0 11.8 %copy-start.12 = (bf16[256,512]{1,0:T(8,128)(2,1)S(1)}, bf16[256,512]{1,0:T(8,128)(2,1)}, u32[]{:S(2)}) copy-start(bf16[256,512]{1,0:T(8,128)(2,1)} %get-tuple-element.91) | copy-start | bytes 786436
  113.0 18.2 %copy-start.9 = (f32[8,256]{1,0:T(8,128)S(1)}, f32[8,256]{1,0:T(8,128)}, u32[]{:S(2)}) copy-start(f32[8,256]{1,0:T(8,128)} %get-tuple-element.93) | copy-start | bytes 24580
  113.2 38.2 %copy-start.4 = (f32[256,512]{1,0:T(8,128)S(1)}, f32[256,512]{1,0:T(8,128)}, u32[]{:S(2)}) copy-start(f32[256,512]{1,0:T(8,128)} %get-tuple-element.85) | copy-start | bytes 1572868
  113.7 1.2 collective-permute-start.8
  114.9 3.8 %collective-permute-start.13 = (f32[8,512]{1,0:T(8,128)S(1)}, f32[8,512]{1,0:T(8,128)S(1)}, u32[]{:S(2)}, u32[]{:S(2)}) collective-permute-start(f32[8,512]{1,0:T(8,128)S(1)} %fusion.1), channel_id=1, source_target_pairs={{0,2},{2,0},{4,6},{6,4},{8,10},{10,8},{12,14},{14,12},{16,18},{18,... | collective-permute-start | bytes 49160 | tf_op jit(solution)/shard_map/ppermute | solution.py:728
  115.0 16.2 %collective-permute-start.12 = (f32[8,256]{1,0:T(8,128)S(1)}, f32[8,256]{1,0:T(8,128)S(1)}, u32[]{:S(2)}, u32[]{:S(2)}) collective-permute-start(f32[8,256]{1,0:T(8,128)S(1)} %copy-done.18), channel_id=1, source_target_pairs={{0,1},{1,0},{2,3},{3,2},{4,5},{5,4},{6,7},{7,6},{8,9},{9,8},{10,11... | collective-permute-start | bytes 24584 | tf_op jit(solution)/shard_map/ppermute | solution.py:722
  118.7 12.5 %collective-permute-start.14 = (f32[8,512]{1,0:T(8,128)S(1)}, f32[8,512]{1,0:T(8,128)S(1)}, u32[]{:S(2)}, u32[]{:S(2)}) collective-permute-start(f32[8,512]{1,0:T(8,128)S(1)} %add.50), channel_id=1, source_target_pairs={{0,4},{2,6},{4,0},{6,2},{8,12},{10,14},{12,8},{14,10},{16,20},{18,... | collective-permute-start | bytes 49160 | tf_op jit(solution)/shard_map/ppermute | solution.py:728
  119.4 24.6 %collective-permute-start.10 = (f32[8,512]{1,0:T(8,128)S(1)}, f32[8,512]{1,0:T(8,128)S(1)}, u32[]{:S(2)}, u32[]{:S(2)}) collective-permute-start(f32[8,512]{1,0:T(8,128)S(1)} %copy-done.15), channel_id=1, source_target_pairs={{2,1},{4,3},{6,5},{8,7},{10,9},{12,11},{14,13},{16,15},{18,17},{20... | collective-permute-start | bytes 49160 | tf_op jit(solution)/shard_map/ppermute | solution.py:723
  124.1 19.9 %collective-permute-start.11 = (f32[8,512]{1,0:T(8,128)S(1)}, f32[8,512]{1,0:T(8,128)S(1)}, u32[]{:S(2)}, u32[]{:S(2)}) collective-permute-start(f32[8,512]{1,0:T(8,128)S(1)} %copy-done.15), channel_id=1, source_target_pairs={{3,1},{5,3},{7,5},{9,7},{11,9},{13,11},{15,13},{17,15},{19,17},{21... | collective-permute-start | bytes 49160 | tf_op jit(solution)/shard_map/ppermute | solution.py:724
  124.8 26.6 %collective-permute-start.9 = (bf16[256,512]{1,0:T(8,128)(2,1)S(1)}, bf16[256,512]{1,0:T(8,128)(2,1)S(1)}, u32[]{:S(2)}, u32[]{:S(2)}) collective-permute-start(bf16[256,512]{1,0:T(8,128)(2,1)S(1)} %copy-done.12), channel_id=1, source_target_pairs={{0,1},{1,0},{2,3},{3,2},{4,5},{5,4},{6,7},{7,6},{8,9},{9,8},{10,11... | collective-permute-start | bytes 786440 | tf_op jit(solution)/shard_map/ppermute | solution.py:721
  125.6 22.6 %all-to-all-start.4 = ((bf16[16,8,1024]{2,1,0:T(8,128)(2,1)}), bf16[16,8,1024]{2,1,0:T(8,128)(2,1)S(1)}, u32[]{:S(2)}, u32[]{:S(2)}) async-start(bf16[16,8,1024]{2,1,0:T(8,128)(2,1)} %bitcast.8), calls=%async_computation.4 | async-start | bytes 524288 | tf_op jit(solution)/shard_map/all_to_all | solution.py:586
  131.2 12.2 %collective-permute-start.15 = (f32[8,512]{1,0:T(8,128)S(1)}, f32[8,512]{1,0:T(8,128)S(1)}, u32[]{:S(2)}, u32[]{:S(2)}) collective-permute-start(f32[8,512]{1,0:T(8,128)S(1)} %add.51), channel_id=1, source_target_pairs={{0,8},{2,10},{4,12},{6,14},{8,0},{10,2},{12,4},{14,6},{16,24},{18,... | collective-permute-start | bytes 49160 | tf_op jit(solution)/shard_map/ppermute | solution.py:728
  143.4 3.7 %collective-permute-start.16 = (f32[8,512]{1,0:T(8,128)S(1)}, f32[8,512]{1,0:T(8,128)S(1)}, u32[]{:S(2)}, u32[]{:S(2)}) collective-permute-start(f32[8,512]{1,0:T(8,128)S(1)} %add.52), channel_id=1, source_target_pairs={{0,16},{2,18},{4,20},{6,22},{8,24},{10,26},{12,28},{14,30},{16,0},... | collective-permute-start | bytes 49160 | tf_op jit(solution)/shard_map/ppermute | solution.py:728
  148.3 5.2 %collective-permute-start.17 = (f32[8,1024]{1,0:T(8,128)S(1)}, f32[8,1024]{1,0:T(8,128)S(1)}, u32[]{:S(2)}, u32[]{:S(2)}) collective-permute-start(f32[8,1024]{1,0:T(8,128)S(1)} %convert_reduce_fusion), channel_id=1, source_target_pairs={{0,0},{1,16},{2,1},{3,17},{4,2},{5,18},{6,3},{7,19},{8,4},{9,20},{... | collective-permute-start | bytes 98312 | tf_op jit(solution)/shard_map/ppermute | solution.py:738

commit v3 on v2

--- a/solution.py
+++ b/solution.py
@@ -86,23 +86,53 @@
         self.waiting = True
 
 
-def staged(kernel, taken, unread, given, with_ids):
+class Resident:
+    def __init__(self, buffer):
+        self.buffer, self.shape = buffer, buffer.shape
+
+    def ready(self):
+        return self
+
+    def __getitem__(self, at):
+        return self.buffer[at]
+
+    def __setitem__(self, at, value):
+        self.buffer[at] = value
+
+    def clear(self):
+        self.buffer[...] = jnp.zeros_like(self.buffer)
+
+    def whole(self):
+        pass
+
+
+def staged(kernel, inputs, unread, outputs, with_ids):
     def body(*refs):
         ids, refs = (refs[:1], refs[1:]) if with_ids else ((), refs)
-        sources, refs = refs[:taken], refs[taken + unread :]
-        targets, refs = refs[:given], refs[given:]
-        in_buffers, refs = refs[:taken], refs[taken:]
-        out_buffers, refs = refs[:given], refs[given:]
+        sources, refs = refs[: len(inputs)], refs[len(inputs) + unread :]
+        targets, refs = refs[: len(outputs)], refs[len(outputs) :]
+        moved_in, moved_out = inputs.count(False), outputs.count(False)
+        in_buffers, refs = list(refs[:moved_in]), refs[moved_in:]
+        out_buffers, refs = list(refs[:moved_out]), refs[moved_out:]
         in_sems, out_sems, *rest = refs
-        ins = [Taken(s, b, in_sems.at[n]) for n, (s, b) in enumerate(zip(sources, in_buffers))]
-        outs = [Given(t, b, out_sems.at[n]) for n, (t, b) in enumerate(zip(targets, out_buffers))]
+        ins, outs, waits = [], [], []
+        for source, resident in zip(sources, inputs):
+            sem = in_sems.at[moved_in - len(in_buffers)]
+            ins.append(Resident(source) if resident else Taken(source, in_buffers.pop(0), sem))
+        for target, resident in zip(targets, outputs):
+            if resident:
+                outs.append(Resident(target))
+            else:
+                sem = out_sems.at[moved_out - len(out_buffers)]
+                outs.append(Given(target, out_buffers.pop(0), sem))
+                waits.append(outs[-1])
         kernel(*ids, *ins, *outs, *rest)
         for each in ins:
             each.ready()
-        for each in outs:
+        for each in waits:
             if not each.waiting:
                 each.whole()
-        for each in outs:
+        for each in waits:
             each.copy.wait()
 
     return body
@@ -276,8 +306,9 @@
         base_out[(2 * b + 1) * D : 2 * (b + 1) * D, :] = x[block(b), D:]
 
 
-def back_kernel(ids, grad_own, grad_other, weight, back_out):
+def back_kernel(ids, grad_own, grad_other, weight, back_out, mark):
     core = ids[1]
+    mark.clear()
     weight.ready()
     head = weight[pl.ds(pl.multiple_of(core * D, D), D), :]
     back_out[pl.ds(pl.multiple_of(core * ROWS, ROWS), ROWS), :] = mm(grad_own[...], head, "nt")
@@ -305,7 +336,7 @@
         position = last - 1 - count
         piece = gathered[position]
         return slab_decay(piece) * total + (
-            gathered_grad[position].astype(F32) - mm(total, piece[0:D], "nt", P_MAP)
+            gathered_grad[position, 0:D].astype(F32) - mm(total, piece[0:D], "nt", P_MAP)
         )
 
     return lax.fori_loop(0, last - first, step, total)
@@ -316,15 +347,22 @@
     out[...] = forward_fold(gathered, 0, gathered.shape[0], jnp.zeros((D, D), F32))
 
 
-def backward_total_kernel(gathered, gathered_grad, out):
-    gathered.ready()
-    gathered_grad.ready()
+def backward_total_kernel(ids, gathered, gathered_grad, out, weight_here, weight_there):
     count = gathered.shape[0]
     out[...] = backward_fold(gathered, gathered_grad, 0, count, jnp.zeros((D, D), F32))
+    height = weight_here.shape[0]
+    total = gathered_grad[0, D:].astype(F32)
+    for chip in range(1, count):
+        total = total + gathered_grad[chip, D:].astype(F32)
+    for part in range(weight_here.shape[1] // D):
+        at = 2 * height * part
+        first, second = total[at : at + height], total[at + height : at + 2 * height]
+        weight_here[:, block(part)] = jnp.where(ids[2] == 0, first, second)
+        weight_there[:, block(part)] = jnp.where(ids[2] == 0, second, first)
 
 
 def outputs_kernel(
-    ids, gathered, entry, maps, read, base, gates, back, gain,
+    ids, gathered, entry, maps, read, base, gates, back, gain, grad_own, grad_other,
     states_out, deltas_out, grads_out, reach_out, packed_grad, normed_out, sent, gain_out,
 ):
     chip, core = ids[0], ids[1]
@@ -371,8 +409,18 @@
         through = maps[2 * b * D : (2 * b + 1) * D, :]
         state_grad = decays[b] * state_grad - mm(state_grad, through, "nt", P_MAP) + reaches[b]
     state_grad = state_grad.astype(BF16)
-    for copy in range(packed_grad.shape[0]):
-        packed_grad[copy] = state_grad
+    own, others = (pl.ds(pl.multiple_of(c * ROWS, ROWS), ROWS) for c in (core, 1 - core))
+    share = mm(normed_out[own, :], grad_own[...], "tn")
+    share = (share + mm(normed_out[others, :], grad_other[...], "tn")).astype(BF16)
+    count = packed_grad.shape[0]
+    height = D // (2 * count)
+    for chip in range(count):
+        packed_grad[chip, 0:D, :] = state_grad
+        both = [share[height * c : height * (c + 1)] for c in (chip, count + chip)]
+        rows = jnp.concatenate(both, axis=0)
+        for part in range(share.shape[1] // D):
+            at = D + 2 * height * part
+            packed_grad[chip, at : at + 2 * height, :] = rows[:, block(part)]
 
 
 def local_grads_kernel(
@@ -401,7 +449,7 @@
 def grads_kernel(
     ids, gathered, gathered_grad, leaving, maps, reach, states, deltas, inverse, x, q, k, gates, pre, padded,
     dq, dk, pull, rows_in, sums, conv_w,
-    keep_out, send_out, spill_out, gate_keep, gate_send, conv_out,
+    keep_out, send_out, small_out, gate_keep,
     d_pre,
 ):
     chip, core = ids[0], ids[1]
@@ -485,8 +533,9 @@
         end_rows + [jnp.zeros((4, D), F32)], axis=0
     )
     d_logit = jnp.transpose(beta_terms)[0:8, :]
-    for target, own in ((gate_keep, True), (gate_send, False)):
-        target.clear()
+    gate_keep.clear()
+    small_out.clear()
+    for target, top, own in ((gate_keep, 0, True), (small_out, 16, False)):
         for head in range(2):
 
             @pl.when(core == head)
@@ -494,13 +543,12 @@
                 first = 2 * (head if own else 1 - head)
                 for half in range(2):
                     b = first + half
-                    target[head : head + 1, block(half)] = d_decay[b : b + 1, :]
-                    target[2 + head : 3 + head, block(half)] = d_logit[b : b + 1, :]
+                    at = top + head
+                    target[at : at + 1, block(half)] = d_decay[b : b + 1, :]
+                    target[at + 2 : at + 3, block(half)] = d_logit[b : b + 1, :]
 
     keep_out.clear()
     send_out.clear()
-    spill_out.clear()
-    conv_out.clear()
     for group, lanes in enumerate(lane_groups(core)):
         here = slice(group * D, (group + 1) * D)
         taps = [conv_w[tap : tap + 1, lanes] for tap in range(4)]
@@ -529,21 +577,21 @@
                     keepdims=True,
                 )
         for tap in range(4):
-            conv_out[tap : tap + 1, lanes] = sums_of[tap]
+            small_out[tap : tap + 1, lanes] = sums_of[tap]
         for back in range(1, 4):
             total = jnp.zeros((1, D), F32)
             for tap in range(0, 4 - back):
                 at = 3 - back - tap
                 total = total + taps[tap] * d_pre[at : at + 1, here]
-            spill_out[3 - back : 4 - back, lanes] = total
-
-
-def shares_kernel(ids, normed, received, weight, gain_part, grad_own, grad_other, out, weight_out):
+            small_out[11 - back : 12 - back, lanes] = total
+
+
+def shares_kernel(ids, normed, received, weight, gain_part, out, mark):
     core = ids[1]
+    mark.clear()
     normed.ready()
     weight.ready()
     kept = normed[pl.ds(pl.multiple_of(core * ROWS, ROWS), ROWS), :]
-    given = normed[pl.ds(pl.multiple_of((1 - core) * ROWS, ROWS), ROWS), :]
     mine = weight[pl.ds(pl.multiple_of(core * D, D), D), :]
     others = weight[pl.ds(pl.multiple_of((1 - core) * D, D), D), :]
     share = (mm(kept, mine) + mm(received[...], others)).astype(BF16)
@@ -556,29 +604,32 @@
         out[owner, 0:height, :] = share[owner * height : (owner + 1) * height]
         out[owner, height:, :] = jnp.zeros((16, out.shape[2]), BF16)
         out[owner, height:, 0:D] = extra
-    out.whole()
-    weight_out[...] = (mm(kept, grad_own[...], "tn") + mm(given, grad_other[...], "tn")).astype(BF16)
-
-
-def call(kernel, shapes, args, name, flops, scratch=(), with_ids=True, after=()):
+
+
+def call(kernel, shapes, args, name, flops, scratch=(), with_ids=True, after=(), near=(), limit=None):
     arrays = args[1:] if with_ids else args
-    outs = [jax.ShapeDtypeStruct(shape, dtype) for shape, dtype in shapes]
-    anywhere = pl.BlockSpec(memory_space=pl.ANY)
+    inputs = [any(x is other for other in near) for x in arrays]
+    outputs = [len(each) > 2 for each in shapes]
+    outs = [jax.ShapeDtypeStruct(each[0], each[1]) for each in shapes]
+    anywhere, inside = (pl.BlockSpec(memory_space=space) for space in (pl.ANY, pltpu.VMEM))
     moved = sum(x.size * x.dtype.itemsize for x in [*arrays, *outs])
+    buffers = [x for x, resident in zip([*arrays, *outs], inputs + outputs) if not resident]
     return pl.pallas_call(
-        staged(kernel, len(arrays), len(after), len(outs), with_ids),
+        staged(kernel, inputs, len(after), outputs, with_ids),
         out_shape=outs,
         in_specs=[pl.BlockSpec(memory_space=pltpu.SMEM)] * with_ids
-        + [anywhere] * (len(arrays) + len(after)),
-        out_specs=[anywhere] * len(outs),
+        + [inside if resident else anywhere for resident in inputs]
+        + [anywhere] * len(after),
+        out_specs=[inside if resident else anywhere for resident in outputs],
         scratch_shapes=[
-            *[pltpu.VMEM(x.shape, x.dtype) for x in [*arrays, *outs]],
-            pltpu.SemaphoreType.DMA((len(arrays),)),
-            pltpu.SemaphoreType.DMA((len(outs),)),
+            *[pltpu.VMEM(x.shape, x.dtype) for x in buffers],
+            pltpu.SemaphoreType.DMA((max(1, inputs.count(False)),)),
+            pltpu.SemaphoreType.DMA((max(1, outputs.count(False)),)),
             *scratch,
         ],
         name=name,
         cost_estimate=pl.CostEstimate(flops=flops, bytes_accessed=moved, transcendentals=0),
+        compiler_params=pltpu.CompilerParams(vmem_limit_bytes=limit),
     )(*args, *after)
 
 
@@ -589,7 +640,7 @@
 def local(mixed, log_decay, beta_logit, conv_weight, norm_gain, out_weight, out_grad):
     near, groups = lax.axis_size("near"), lax.axis_size("dp")
     chips = lax.axis_size("far") * near
-    ids = jnp.stack([lax.axis_index(axis) for axis in ("near", "core")]).astype(jnp.int32)
+    ids = jnp.stack([lax.axis_index(axis) for axis in ("near", "core", "far")]).astype(jnp.int32)
     chip_line, line = ("far", "near"), ("far", "near", "core")
     swap = [(0, 1), (1, 0)]
     width = out_weight.shape[1]
@@ -602,9 +653,6 @@
     tail_b = lax.ppermute(tail, line, [(2 * c + 1, 2 * c + 3) for c in range(chips - 1)])
     other = lax.ppermute(mixed, "core", swap)
     gates_other = lax.ppermute(gates_own, "core", swap)
-    out_grad, gates_other, tail_a, tail_b, other = lax.optimization_barrier(
-        (out_grad, gates_other, tail_a, tail_b, other)
-    )
     grad_own = everyone(jnp.broadcast_to(out_grad[None], (groups, height, width)), "dp")
     grad_own = grad_own.reshape(ROWS, width)
     (padded, pre, q, k, inverse, x, scores, maps, gates, packed) = call(
@@ -622,7 +670,7 @@
             ((near, PACK, D), BF16),
         ],
         [ids, mixed, other, tail_a, tail_b, gates_own, gates_other, conv_weight],
-        "maps", 10**9,
+        "maps", 10**9, near=[other, tail_a, tail_b, gates_own, gates_other],
     )
     gathered = everyone(packed, "near")
 
@@ -633,17 +681,17 @@
         [scores, x, q, gates],
         "readout", 10**8, with_ids=False,
     )
-    (back,) = call(
+    back, mark = call(
         back_kernel,
-        [((rows, D), F32)],
+        [((rows, D), F32), ((8, D), F32)],
         [ids, grad_own, grad_other, out_weight],
-        "back", 10**8,
+        "back", 10**8, after=[read],
     )
     (total,) = call(
         forward_total_kernel,
-        [((D, D), F32)],
+        [((D, D), F32, "near")],
         [gathered],
-        "forward_total", 10**8, with_ids=False, after=[read, back],
+        "forward_total", 10**8, with_ids=False, after=[mark], near=[gathered], limit=2**23,
     )
     entry = lax.ppermute(total, "far", [(0, 1)])
     gain = jnp.broadcast_to(norm_gain.reshape(1, D), (8, D))
@@ -654,13 +702,13 @@
             ((rows, D), F32),
             ((rows, D), F32),
             ((rows, D), F32),
-            ((near, D, D), BF16),
+            ((near, D + D // near * (width // D), D), BF16),
             ((rows, D), BF16),
             ((ROWS, D), BF16),
             ((8, D), F32),
         ],
-        [ids, gathered, entry, maps, read, base, gates, back, gain],
-        "outputs", 10**9,
+        [ids, gathered, entry, maps, read, base, gates, back, gain, grad_own, grad_other],
+        "outputs", 10**9, near=[gathered, entry, gain],
     )
     gathered_grad = everyone(packed_grad, "near")
     received = lax.ppermute(sent, "core", swap)
@@ -676,36 +724,53 @@
         [scores, deltas, grads, states, q, k, gates],
         "local_grads", 10**9, with_ids=False,
     )
-    share, weight_part = call(
+    share, mark = call(
         shares_kernel,
-        [((groups, height + 16, width), BF16), ((D, width), BF16)],
-        [ids, normed, received, out_weight, gain_part, grad_own, grad_other],
-        "shares", 10**8, after=[sums],
-    )
-
-    (total,) = call(
+        [((groups, height + 16, width), BF16), ((8, D), F32)],
+        [ids, normed, received, out_weight, gain_part],
+        "shares", 10**8, after=[sums], near=[received],
+    )
+
+    height_w = D // chips
+    total, weight_here, weight_there = call(
         backward_total_kernel,
-        [((D, D), F32)],
-        [gathered, gathered_grad],
-        "backward_total", 10**8, with_ids=False,
-    )
-    total, share = lax.optimization_barrier((total, share))
+        [
+            ((D, D), F32, "near"),
+            ((height_w, width), F32, "near"),
+            ((height_w, width), F32, "near"),
+        ],
+        [ids, gathered, gathered_grad],
+        "backward_total", 10**8, near=[gathered, gathered_grad], after=[mark], limit=2**23,
+    )
     leaving = lax.ppermute(total, "far", [(1, 0)])
-    keep, send, spill, gate_keep, gate_send, conv_part = call(
+    def owners(of_run):
+        return [
+            (2 * (f * near + n) + h, h * chips + of_run(f) * near + n)
+            for f in range(2)
+            for n in range(near)
+            for h in range(2)
+        ]
+
+    weight_here = lax.ppermute(weight_here, line, owners(lambda f: f))
+    weight_there = lax.ppermute(weight_there, line, owners(lambda f: 1 - f))
+    leaving, share, weight_here, weight_there = lax.optimization_barrier(
+        (leaving, share, weight_here, weight_there)
+    )
+    grad_weight = weight_here + weight_there
+
+    keep, send, small, gate_keep = call(
         grads_kernel,
         [
             ((ROWS, 4 * D), F32),
             ((ROWS, 4 * D), BF16),
-            ((8, 4 * D), F32),
-            ((8, ROWS), F32),
-            ((8, ROWS), F32),
-            ((8, 4 * D), F32),
+            ((24, 4 * D), F32, "near"),
+            ((8, ROWS), F32, "near"),
         ],
         [
             ids, gathered, gathered_grad, leaving, maps, reach, states, deltas, inverse, x, q, k, gates,
             pre, padded, dq, dk, pull, row_terms, sums, conv_weight,
         ],
-        "grads", 10**9,
+        "grads", 10**9, near=[gathered, gathered_grad, leaving],
         scratch=[pltpu.VMEM((rows + 8, 3 * D), F32)],
     )
     shares = everyone(share, "dp").astype(F32)
@@ -713,15 +778,14 @@
     gain_rows = jnp.sum(shares[:, height : height + 2, :D], axis=0)
 
     gain_row = gain_rows[0:1] + gain_rows[1:2]
-    totals = conv_part + jnp.pad(gain_row, ((4, 3), (0, 3 * D)))
-    totals = totals + lax.ppermute(totals, "core", swap)
-    totals, send, spill, gate_send, weight_part = lax.optimization_barrier(
-        (totals, send, spill, gate_send, weight_part)
-    )
+    small = small + jnp.pad(gain_row, ((4, 19), (0, 3 * D)))
+    small_other = lax.ppermute(small, "core", swap)
+    gate_taken = small_other[16:24, :ROWS]
+    spill = small[8:16] + small_other[8:16]
+    totals = small[0:8] + small_other[0:8]
+    totals, spill, send = lax.optimization_barrier((totals, spill, send))
     taken = lax.ppermute(send, "core", swap)
-    gate_taken = lax.ppermute(gate_send, "core", swap)
-    spill_a = lax.ppermute(spill, line, [(2 * c, 2 * c - 1) for c in range(1, chips)])
-    spill_b = lax.ppermute(spill, line, [(2 * c + 1, 2 * c - 1) for c in range(1, chips)])
+    spilled = lax.ppermute(spill, line, [(2 * c + 1, 2 * c - 1) for c in range(1, chips)])
     distance = 1
     while distance < chips:
         pairs = [(c, c ^ distance) for c in range(chips)]
@@ -733,13 +797,7 @@
     grad_taps = totals[0:4] + seen[0:4]
     grad_gain = totals[4, :D] + seen[4, :D]
 
-    weight_parts = everyone(weight_part.reshape(chips, D // chips, width), chip_line)
-    weight_sum = jnp.sum(weight_parts.astype(F32), axis=0)
-    grad_weight = lax.ppermute(
-        weight_sum, line, [(2 * c + h, h * chips + c) for c in range(chips) for h in range(2)]
-    )
-
-    spilled = jnp.pad((spill_a + spill_b)[0:3], ((ROWS - 3, 0), (0, 0)))
+    spilled = jnp.pad(spilled[0:3], ((ROWS - 3, 0), (0, 0)))
     grad_mixed = (keep + taken.astype(F32) + spilled).astype(BF16)
     gate_grads = gate_keep + gate_taken
     return (

time: 157 us -> 142 us (0.904)
  starting transfers between devices: 52.8 us -> 45.5 us
  waiting for transfers between devices: 45 us -> 41.3 us
  Pallas kernels: 42.6 us -> 40.9 us
    ppermute x4, starting transfers between devices: 6.11 us -> 13.4 us  [local(): seen = lax.ppermute(totals, chip_line, pairs)]
    ppermute x4, waiting for transfers between devices: 12.8 us -> 6.4 us  [local(): seen = lax.ppermute(totals, chip_line, pairs)]
    ppermute x4 -> x3, starting transfers between devices: 8 us -> 2.1 us  [the longest x1 1.92 us: local(): weight_here = lax.ppermute(weight_here, line, owners(lambda f: f))]
    ppermute x1, starting transfers between devices: 5.56 us -> 0.06 us  [local(): gates_other = lax.ppermute(gates_own, 'core', swap)]
    ppermute x1, waiting for transfers between devices: 5.2 us -> 0.01 us  [local(): leaving = lax.ppermute(total, 'far', [(1, 0)])]
    ppermute x1, waiting for transfers between devices: 0.01 us -> 4.35 us  [local(): lax.ppermute(tail, line, [(2 * c + 1, 2 * c + 2) for c in range(chips - 1)])]
    all_to_all x5 -> x4, starting transfers between devices: 25.6 us -> 21.3 us  [everyone(): return lax.all_to_all(x, axes, 0, 0, tiled=True)]
    ppermute x1, starting transfers between devices: 0.09 us -> 2.73 us  [local(): other = lax.ppermute(mixed, 'core', swap)]
  transfers between devices with their start and end apart: 23 -> 21, of which waited for: 11 -> 12; matrix products, arithmetic and copies ran while one was open for 3% -> 3% of each run, Pallas kernels for 20% -> 23%
where the time goes in v3:
time: 142 us; the launch traced here: 140 us
  starting transfers between devices  45.5 us (32%)
  waiting for transfers between devices  41.3 us (29%)
  Pallas kernels  40.9 us (29%)
  local copies, waits for them, and re-layouts  7.17 us (5%)
  other arithmetic  4.15 us (3%)
    pallas_call x9, Pallas kernels, call(): pl.pallas_call(staged(kernel, inputs, len(after), outputs, with_ids), out...  40.9 us
    all_to_all x4, starting transfers between devices, everyone(): return lax.all_to_all(x, axes, 0, 0, tiled=True)  21.3 us
    all_to_all x4, waiting for transfers between devices, everyone(): return lax.all_to_all(x, axes, 0, 0, tiled=True)  20.7 us
    ppermute x4, starting transfers between devices, local(): seen = lax.ppermute(totals, chip_line, pairs)  13.4 us
    ppermute x4, waiting for transfers between devices, local(): seen = lax.ppermute(totals, chip_line, pairs)  6.4 us
    ppermute x1, waiting for transfers between devices, local(): entry = lax.ppermute(total, 'far', [(0, 1)])  4.86 us
    ppermute x1, waiting for transfers between devices, local(): lax.ppermute(tail, line, [(2 * c + 1, 2 * c + 2) for c in range(chips - 1)])  4.35 us
    unnamed x48, local copies, waits for them, and re-layouts  4.15 us
  transfers between devices with their start and end apart: 21, of which 12 were waited for; matrix products, arithmetic and copies ran while one was open for 3% of the time, Pallas kernels for 23%

profile of v3, /device:TPU:8, one launch (start us, length us, event | category | flops | bytes accessed | tf_op | source)
XLA Modules:
  0.0 140.0 jit_solution(6956424662169508337)
XLA Ops:
  0.7 1.7 %broadcast_in_dim.7 = bf16[8,32,1024]{2,1,0:T(8,128)(2,1)} broadcast(bf16[32,1024]{1,0:T(8,128)(2,1)} %param.13), dimensions={1,2} | broadcast | bytes 589824 | tf_op jit(solution)/shard_map/broadcast_in_dim | solution.py:656
  2.4 6.0 %all-to-all-start.1 = ((bf16[8,32,1024]{2,1,0:T(8,128)(2,1)}), bf16[8,32,1024]{2,1,0:T(8,128)(2,1)S(1)}, u32[]{:S(2)}, u32[]{:S(2)}) async-start(bf16[8,32,1024]{2,1,0:T(8,128)(2,1)} %broadcast_in_dim.7), calls=%async_computation.1 | async-start | bytes 1048576 | tf_op jit(solution)/shard_map/all_to_all | solution.py:637
  8.4 0.7 collective-permute-start.2
  9.1 1.3 collective-permute-start.1
  10.4 2.7 %collective-permute-start = (bf16[256,512]{1,0:T(8,128)(2,1)S(1)}, bf16[256,512]{1,0:T(8,128)(2,1)S(1)}, u32[]{:S(2)}, u32[]{:S(2)}) collective-permute-start(bf16[256,512]{1,0:T(8,128)(2,1)S(1)} %copy-done.16), channel_id=1, source_target_pairs={{0,1},{1,0},{2,3},{3,2},{4,5},{5,4},{6,7},{7,6},{8,9},{9,8},{10,11... | collective-permute-start | bytes 786440 | tf_op jit(solution)/shard_map/ppermute | solution.py:654
  13.4 0.7 pad_add_fusion.1.refs_0_
  14.5 4.3 %collective-permute-done.1.refs_3_ = bf16[16,512]{1,0:T(8,128)(2,1)S(1)} collective-permute-done((bf16[16,512]{1,0:T(8,128)(2,1)S(1)}, bf16[16,512]{1,0:T(8,128)(2,1)S(1)}, u32[]{:S(2)}, u32[]{:S(2)}) %collective-permute-start.1) | collective-permute-done | bytes 16416 | tf_op jit(solution)/shard_map/ppermute | solution.py:652
  18.9 0.6 copy-done.22
  19.5 0.7 copy-done.19
  20.2 8.2 %maps.1 = (f32[520,384]{1,0:T(8,128)}, f32[512,384]{1,0:T(8,128)}, f32[512,128]{1,0:T(8,128)}, f32[512,128]{1,0:T(8,128)}, f32[512,128]{1,0:T(8,128)}, /*index=5...) custom-call(s32[3]{0:T(128)} %pad_add_fusion.1.refs_0_, ...), custom_call_target="tpu_custom_call" | custom-call | flops 1000000000 | bytes 4825088 | tf_op jit(solution)/shard_map/maps/pallas_call | solution.py:617
  28.4 5.0 %all-to-all-start = ((bf16[8,272,128]{2,1,0:T(8,128)(2,1)}), bf16[8,272,128]{2,1,0:T(8,128)(2,1)S(1)}, u32[]{:S(2)}, u32[]{:S(2)}) async-start(bf16[8,272,128]{2,1,0:T(8,128)(2,1)} %get-tuple-element.50), calls=%async_computation | async-start | bytes 1114112 | tf_op jit(solution)/shard_map/all_to_all | solution.py:637
  33.4 2.8 %readout.1 = (f32[1024,128]{1,0:T(8,128)}, f32[1024,128]{1,0:T(8,128)}) custom-call(f32[512,128]{1,0:T(8,128)} %get-tuple-element.51.refs_0_, f32[512,256]{1,0:T(8,128)} %get-tuple-element.52.refs_1_.refs_9_, f32[512,128]{1,0:T(8,128)} %get-tuple-element.53.refs_2_.refs_4_.refs_10_, f32[8,128]{1,0:T(8,128)} %get-tuple-element.54.refs_3_.refs_6_.refs_12_), custom_call_target="tpu_custom_call" | custom-call | flops 100000000 | bytes 2101248 | tf_op jit(solution)/shard_map/readout/pallas_call | solution.py:617
  36.2 0.8 copy-done.7
  36.9 3.6 %back.1 = (f32[512,128]{1,0:T(8,128)}, f32[8,128]{1,0:T(8,128)}) custom-call(s32[3]{0:T(128)} %pad_add_fusion.1.refs_0_, bf16[256,1024]{1,0:T(8,128)(2,1)} %bitcast.13, bf16[256,1024]{1,0:T(8,128)(2,1)} %copy-done.7, bf16[256,1024]{1,0:T(8,128)(2,1)} %refs_3_.3, f32[1024,128]{1,0:T(8,128)} %get-tuple-element.55.refs_4_), custom_call_target="tpu_custom_call" | custom-call | flops 100000000 | bytes 1839104 | tf_op jit(solution)/shard_map/back/pallas_call | solution.py:617
  40.5 9.8 %all-to-all-done.refs_0_.refs_1_ = bf16[8,272,128]{2,1,0:T(8,128)(2,1)S(1)} async-done(((bf16[8,272,128]{2,1,0:T(8,128)(2,1)}), bf16[8,272,128]{2,1,0:T(8,128)(2,1)S(1)}, u32[]{:S(2)}, u32[]{:S(2)}) %all-to-all-start) | async-done | bytes 557088 | tf_op jit(solution)/shard_map/all_to_all | solution.py:637
  50.3 0.7 copy-done.5
  51.0 1.1 forward_total.1
  52.2 1.3 collective-permute-start.5
  53.5 4.9 %collective-permute-done.5.refs_2_ = f32[128,128]{1,0:T(8,128)S(1)} collective-permute-done((f32[128,128]{1,0:T(8,128)S(1)}, f32[128,128]{1,0:T(8,128)S(1)}, u32[]{:S(2)}, u32[]{:S(2)}) %collective-permute-start.5) | collective-permute-done | bytes 65568 | tf_op jit(solution)/shard_map/ppermute | solution.py:696
  58.3 0.6 broadcast_in_dim.16.refs_8_
  59.0 6.0 %outputs.1 = (f32[512,128]{1,0:T(8,128)}, f32[512,128]{1,0:T(8,128)}, f32[512,128]{1,0:T(8,128)}, f32[512,128]{1,0:T(8,128)}, bf16[8,256,128]{2,1,0:T(8,128)(2,1...) custom-call(s32[3]{0:T(128)} %pad_add_fusion.1.refs_0_, bf16[8,272,128]{2,1,0:T(8,128)(2,1)} %copy-done, ...), custom_call_target="tpu_custom_call" | custom-call | flops 1000000000 | bytes 5287936 | tf_op jit(solution)/shard_map/outputs/pallas_call | solution.py:617
  65.0 3.5 %all-to-all-start.2 = ((bf16[8,256,128]{2,1,0:T(8,128)(2,1)}), bf16[8,256,128]{2,1,0:T(8,128)(2,1)S(1)}, u32[]{:S(2)}, u32[]{:S(2)}) async-start(bf16[8,256,128]{2,1,0:T(8,128)(2,1)} %get-tuple-element.60), calls=%async_computation.2 | async-start | bytes 1048576 | tf_op jit(solution)/shard_map/all_to_all | solution.py:637
  68.6 3.7 %local_grads.1 = (f32[512,128]{1,0:T(8,128)}, f32[512,128]{1,0:T(8,128)}, f32[512,128]{1,0:T(8,128)}, f32[512,128]{1,0:T(8,128)}, f32[8,128]{1,0:T(8,128)}) custom-call(f32[512,128]{1,0:T(8,128)} %get-tuple-element.51.refs_0_, f32[512,128]{1,0:T(8,128)} %get-tuple-element.64.refs_1_.refs_7_, f32[512,128]{1,0:T(8,128)} %get-tuple-element.65.refs_2_, ...), custom_call_target="tpu_custom_call" | custom-call | flops 1000000000 | bytes 2629632 | tf_op jit(solution)/shard_map/local_grads/pallas_call | solution.py:617
  72.4 0.6 copy-done.10
  73.0 3.4 %shares.1 = (bf16[8,48,1024]{2,1,0:T(8,128)(2,1)}, f32[8,128]{1,0:T(8,128)}) custom-call(s32[3]{0:T(128)} %pad_add_fusion.1.refs_0_, bf16[512,128]{1,0:T(8,128)(2,1)} %get-tuple-element.61.refs_1_, bf16[256,128]{1,0:T(8,128)(2,1)} %copy-done.10, bf16[256,1024]{1,0:T(8,128)(2,1)} %refs_3_.3, f32[8,128]{1,0:T(8,128)} %get-tuple-element.63.refs_4_, ...), custom_call_target="tpu_custom_call" | custom-call | flops 100000000 | bytes 1515520 | tf_op jit(solution)/shard_map/shares/pallas_call | solution.py:617
  76.4 6.5 %all-to-all-done.2.refs_2_ = bf16[8,256,128]{2,1,0:T(8,128)(2,1)S(1)} async-done(((bf16[8,256,128]{2,1,0:T(8,128)(2,1)}), bf16[8,256,128]{2,1,0:T(8,128)(2,1)S(1)}, u32[]{:S(2)}, u32[]{:S(2)}) %all-to-all-start.2) | async-done | bytes 524320 | tf_op jit(solution)/shard_map/all_to_all | solution.py:637
  82.9 0.7 copy-done.4
  83.6 1.9 %backward_total.1 = (f32[128,128]{1,0:T(8,128)S(1)}, f32[8,1024]{1,0:T(8,128)S(1)}, f32[8,1024]{1,0:T(8,128)S(1)}) custom-call(s32[3]{0:T(128)S(1)} %copy-done.3, bf16[8,272,128]{2,1,0:T(8,128)(2,1)S(1)} %copy-done.1, bf16[8,256,128]{2,1,0:T(8,128)(2,1)S(1)} %all-to-all-done.2.refs_2_, f32[8,128]{1,0:T(8,128)S(1)} %copy-done.4), custom_call_target="tpu_custom_call" | custom-call | flops 100000000 | bytes 1212416 | tf_op jit(solution)/shard_map/backward_total/pallas_call | solution.py:617
  85.5 1.9 %collective-permute-start.7 = (f32[128,128]{1,0:T(8,128)S(1)}, f32[128,128]{1,0:T(8,128)S(1)}, u32[]{:S(2)}, u32[]{:S(2)}) collective-permute-start(f32[128,128]{1,0:T(8,128)S(1)} %get-tuple-element.70), channel_id=1, source_target_pairs={{16,0},{17,1},{18,2},{19,3},{20,4},{21,5},{22,6},{23,7},{24,8},{25... | collective-permute-start | bytes 196616 | tf_op jit(solution)/shard_map/ppermute | solution.py:745
  87.4 1.9 %collective-permute-start.8 = (f32[8,1024]{1,0:T(8,128)S(1)}, f32[8,1024]{1,0:T(8,128)S(1)}, u32[]{:S(2)}, u32[]{:S(2)}) collective-permute-start(f32[8,1024]{1,0:T(8,128)S(1)} %get-tuple-element.72), channel_id=1, source_target_pairs={{0,0},{1,16},{2,1},{3,17},{4,2},{5,18},{6,3},{7,19},{8,4},{9,20},{... | collective-permute-start | bytes 98312 | tf_op jit(solution)/shard_map/ppermute | solution.py:754
  89.4 3.2 %collective-permute-done.8 = f32[8,1024]{1,0:T(8,128)S(1)} collective-permute-done((f32[8,1024]{1,0:T(8,128)S(1)}, f32[8,1024]{1,0:T(8,128)S(1)}, u32[]{:S(2)}, u32[]{:S(2)}) %collective-permute-start.8) | collective-permute-done | bytes 32800 | tf_op jit(solution)/shard_map/ppermute | solution.py:754
  92.6 6.8 %all-to-all-start.3 = ((bf16[8,48,1024]{2,1,0:T(8,128)(2,1)}), bf16[8,48,1024]{2,1,0:T(8,128)(2,1)S(1)}, u32[]{:S(2)}, u32[]{:S(2)}) async-start(bf16[8,48,1024]{2,1,0:T(8,128)(2,1)} %get-tuple-element.74), calls=%async_computation.3 | async-start | bytes 1572864 | tf_op jit(solution)/shard_map/all_to_all | solution.py:637
  99.4 10.3 %grads.1 = (f32[256,512]{1,0:T(8,128)}, bf16[256,512]{1,0:T(8,128)(2,1)}, f32[24,512]{1,0:T(8,128)}, f32[8,256]{1,0:T(8,128)}) custom-call(s32[3]{0:T(128)} %pad_add_fusion.1.refs_0_, bf16[8,272,128]{2,1,0:T(8,128)(2,1)} %copy-done, bf16[8,256,128]{2,1,0:T(8,128)(2,1)} %copy-done.2, f32[128,128]{1,0:T(8,128)} %copy-done.9, ...), custom_call_target="tpu_custom_call" | custom-call | flops 1000000000 | bytes 7262208 | tf_op jit(solution)/shard_map/grads/pallas_call | solution.py:617
  109.7 4.4 %all-to-all-done.3 = bf16[8,48,1024]{2,1,0:T(8,128)(2,1)S(1)} async-done(((bf16[8,48,1024]{2,1,0:T(8,128)(2,1)}), bf16[8,48,1024]{2,1,0:T(8,128)(2,1)S(1)}, u32[]{:S(2)}, u32[]{:S(2)}) %all-to-all-start.3) | async-done | bytes 786464 | tf_op jit(solution)/shard_map/all_to_all | solution.py:637
  114.5 1.2 collective-permute-done.10
  115.7 0.6 add.59
  116.3 3.1 %collective-permute-done.13 = f32[8,512]{1,0:T(8,128)S(1)} collective-permute-done((f32[8,512]{1,0:T(8,128)S(1)}, f32[8,512]{1,0:T(8,128)S(1)}, u32[]{:S(2)}, u32[]{:S(2)}) %collective-permute-start.13) | collective-permute-done | bytes 16416 | tf_op jit(solution)/shard_map/ppermute | solution.py:792
  119.5 3.9 %collective-permute-start.14 = (f32[8,512]{1,0:T(8,128)S(1)}, f32[8,512]{1,0:T(8,128)S(1)}, u32[]{:S(2)}, u32[]{:S(2)}) collective-permute-start(f32[8,512]{1,0:T(8,128)S(1)} %add.53), channel_id=1, source_target_pairs={{0,4},{2,6},{4,0},{6,2},{8,12},{10,14},{12,8},{14,10},{16,20},{18,... | collective-permute-start | bytes 49160 | tf_op jit(solution)/shard_map/ppermute | solution.py:792
  123.4 0.7 slice_reduce_fusion
  124.1 0.7 collective-permute-start.12
  125.1 5.8 %collective-permute-start.15 = (f32[8,512]{1,0:T(8,128)S(1)}, f32[8,512]{1,0:T(8,128)S(1)}, u32[]{:S(2)}, u32[]{:S(2)}) collective-permute-start(f32[8,512]{1,0:T(8,128)S(1)} %add.54), channel_id=1, source_target_pairs={{0,8},{2,10},{4,12},{6,14},{8,0},{10,2},{12,4},{14,6},{16,24},{18,... | collective-permute-start | bytes 49160 | tf_op jit(solution)/shard_map/ppermute | solution.py:792
  131.0 1.8 %collective-permute-done.15 = f32[8,512]{1,0:T(8,128)S(1)} collective-permute-done((f32[8,512]{1,0:T(8,128)S(1)}, f32[8,512]{1,0:T(8,128)S(1)}, u32[]{:S(2)}, u32[]{:S(2)}) %collective-permute-start.15) | collective-permute-done | bytes 16416 | tf_op jit(solution)/shard_map/ppermute | solution.py:792
  132.8 3.6 %collective-permute-start.16 = (f32[8,512]{1,0:T(8,128)S(1)}, f32[8,512]{1,0:T(8,128)S(1)}, u32[]{:S(2)}, u32[]{:S(2)}) collective-permute-start(f32[8,512]{1,0:T(8,128)S(1)} %add.55), channel_id=1, source_target_pairs={{0,16},{2,18},{4,20},{6,22},{8,24},{10,26},{12,28},{14,30},{16,0},... | collective-permute-start | bytes 49160 | tf_op jit(solution)/shard_map/ppermute | solution.py:792
  136.4 0.6 slice_bitcast_fusion
  137.0 1.1 collective-permute-done.16
  138.1 0.5 fusion
  138.6 0.6 slice_add_fusion.2
  139.2 0.8 add_convert_fusion
  (74 shorter events, 1.7 us)
Async XLA Ops:
  0.6 7.8 %copy-start.16 = (bf16[256,512]{1,0:T(8,128)(2,1)S(1)}, bf16[256,512]{1,0:T(8,128)(2,1)}, u32[]{:S(2)}) copy-start(bf16[256,512]{1,0:T(8,128)(2,1)} %refs_1_.1) | copy-start | bytes 786436
  0.6 12.6 %copy-start.14 = (f32[256,2]{0,1:T(2,128)S(1)}, f32[256,2]{0,1:T(2,128)}, u32[]{:S(2)}) copy-start(f32[256,2]{0,1:T(2,128)} %param.9) | copy-start | bytes 6148
  0.7 12.6 %copy-start.15 = (f32[256,2]{0,1:T(2,128)S(1)}, f32[256,2]{0,1:T(2,128)}, u32[]{:S(2)}) copy-start(f32[256,2]{0,1:T(2,128)} %param.8) | copy-start | bytes 6148
  2.4 25.9 %all-to-all-start.1 = ((bf16[8,32,1024]{2,1,0:T(8,128)(2,1)}), bf16[8,32,1024]{2,1,0:T(8,128)(2,1)S(1)}, u32[]{:S(2)}, u32[]{:S(2)}) async-start(bf16[8,32,1024]{2,1,0:T(8,128)(2,1)} %broadcast_in_dim.7), calls=%async_computation.1 | async-start | bytes 1048576 | tf_op jit(solution)/shard_map/all_to_all | solution.py:637
  8.4 6.1 %collective-permute-start.2 = (bf16[16,512]{1,0:T(8,128)(2,1)S(1)}, bf16[16,512]{1,0:T(8,128)(2,1)S(1)}, u32[]{:S(2)}, u32[]{:S(2)}) collective-permute-start(bf16[16,512]{1,0:T(8,128)(2,1)S(1)} %slice.51), channel_id=1, source_target_pairs={{1,3},{3,5},{5,7},{7,9},{9,11},{11,13},{13,15},{15,17},{17,19},{19... | collective-permute-start | bytes 49160 | tf_op jit(solution)/shard_map/ppermute | solution.py:653
  9.1 9.8 %collective-permute-start.1 = (bf16[16,512]{1,0:T(8,128)(2,1)S(1)}, bf16[16,512]{1,0:T(8,128)(2,1)S(1)}, u32[]{:S(2)}, u32[]{:S(2)}) collective-permute-start(bf16[16,512]{1,0:T(8,128)(2,1)S(1)} %slice.51), channel_id=1, source_target_pairs={{1,2},{3,4},{5,6},{7,8},{9,10},{11,12},{13,14},{15,16},{17,18},{19... | collective-permute-start | bytes 49160 | tf_op jit(solution)/shard_map/ppermute | solution.py:652
  10.4 8.5 %collective-permute-start = (bf16[256,512]{1,0:T(8,128)(2,1)S(1)}, bf16[256,512]{1,0:T(8,128)(2,1)S(1)}, u32[]{:S(2)}, u32[]{:S(2)}) collective-permute-start(bf16[256,512]{1,0:T(8,128)(2,1)S(1)} %copy-done.16), channel_id=1, source_target_pairs={{0,1},{1,0},{2,3},{3,2},{4,5},{5,4},{6,7},{7,6},{8,9},{9,8},{10,11... | collective-permute-start | bytes 786440 | tf_op jit(solution)/shard_map/ppermute | solution.py:654
  13.3 5.6 %copy-start.13 = (f32[8,256]{1,0:T(8,128)}, f32[8,256]{1,0:T(8,128)S(1)}, u32[]{:S(2)}) copy-start(f32[8,256]{1,0:T(8,128)S(1)} %maximum_maximum_fusion.refs_5_) | copy-start | bytes 24580
  13.3 1.2 collective-permute-start.3
  14.5 4.4 %copy-start.23 = (f32[8,256]{1,0:T(8,128)}, f32[8,256]{1,0:T(8,128)S(1)}, u32[]{:S(2)}) copy-start(f32[8,256]{1,0:T(8,128)S(1)} %collective-permute-done.3.refs_6_) | copy-start | bytes 24580
  14.5 4.4 %copy-start.21 = (bf16[16,512]{1,0:T(8,128)(2,1)}, bf16[16,512]{1,0:T(8,128)(2,1)S(1)}, u32[]{:S(2)}) copy-start(bf16[16,512]{1,0:T(8,128)(2,1)S(1)} %collective-permute-done.2.refs_4_) | copy-start | bytes 49156
  18.9 0.6 copy-start.22
  19.5 0.7 copy-start.19
  28.4 7.8 %copy-start.6 = (bf16[8,32,1024]{2,1,0:T(8,128)(2,1)}, bf16[8,32,1024]{2,1,0:T(8,128)(2,1)S(1)}, u32[]{:S(2)}) copy-start(bf16[8,32,1024]{2,1,0:T(8,128)(2,1)S(1)} %all-to-all-done.1) | copy-start | bytes 1572868
  28.4 22.0 %all-to-all-start = ((bf16[8,272,128]{2,1,0:T(8,128)(2,1)}), bf16[8,272,128]{2,1,0:T(8,128)(2,1)S(1)}, u32[]{:S(2)}, u32[]{:S(2)}) async-start(bf16[8,272,128]{2,1,0:T(8,128)(2,1)} %get-tuple-element.50), calls=%async_computation | async-start | bytes 1114112 | tf_op jit(solution)/shard_map/all_to_all | solution.py:637
  33.3 2.8 %collective-permute-start.4 = (bf16[256,1024]{1,0:T(8,128)(2,1)S(1)}, bf16[256,1024]{1,0:T(8,128)(2,1)S(1)}, u32[]{:S(2)}, u32[]{:S(2)}) collective-permute-start(bf16[256,1024]{1,0:T(8,128)(2,1)S(1)} %bitcast.12), channel_id=1, source_target_pairs={{0,1},{1,0},{2,3},{3,2},{4,5},{5,4},{6,7},{7,6},{8,9},{9,8},{10,11... | collective-permute-start | bytes 1572872 | tf_op jit(solution)/shard_map/ppermute | solution.py:677
  36.1 22.2 %copy-start.17 = (f32[128]{0:T(128)S(1)}, f32[128]{0:T(128)}, u32[]{:S(2)}) copy-start(f32[128]{0:T(128)} %param.11) | copy-start | bytes 1540
  36.1 0.8 copy-start.7
  50.3 8.6 %copy-start = (bf16[8,272,128]{2,1,0:T(8,128)(2,1)}, bf16[8,272,128]{2,1,0:T(8,128)(2,1)S(1)}, u32[]{:S(2)}) copy-start(bf16[8,272,128]{2,1,0:T(8,128)(2,1)S(1)} %all-to-all-done.refs_0_.refs_1_) | copy-start | bytes 1671172
  50.3 0.7 copy-start.5
  52.2 6.2 %collective-permute-start.5 = (f32[128,128]{1,0:T(8,128)S(1)}, f32[128,128]{1,0:T(8,128)S(1)}, u32[]{:S(2)}, u32[]{:S(2)}) collective-permute-start(f32[128,128]{1,0:T(8,128)S(1)} %forward_total.1), channel_id=1, source_target_pairs={{0,16},{1,17},{2,18},{3,19},{4,20},{5,21},{6,22},{7,23},{8,24},{9,... | collective-permute-start | bytes 196616 | tf_op jit(solution)/shard_map/ppermute | solution.py:696
  58.3 0.6 copy-start.20
  65.0 17.9 %all-to-all-start.2 = ((bf16[8,256,128]{2,1,0:T(8,128)(2,1)}), bf16[8,256,128]{2,1,0:T(8,128)(2,1)S(1)}, u32[]{:S(2)}, u32[]{:S(2)}) async-start(bf16[8,256,128]{2,1,0:T(8,128)(2,1)} %get-tuple-element.60), calls=%async_computation.2 | async-start | bytes 1048576 | tf_op jit(solution)/shard_map/all_to_all | solution.py:637
  68.5 3.9 %collective-permute-start.6 = (bf16[256,128]{1,0:T(8,128)(2,1)}, bf16[256,128]{1,0:T(8,128)(2,1)S(1)}, u32[]{:S(2)}, u32[]{:S(2)}) collective-permute-start(bf16[256,128]{1,0:T(8,128)(2,1)} %get-tuple-element.62), channel_id=1, source_target_pairs={{0,1},{1,0},{2,3},{3,2},{4,5},{5,4},{6,7},{7,6},{8,9},{9,8},{10,11... | collective-permute-start | bytes 196616 | tf_op jit(solution)/shard_map/ppermute | solution.py:714
  68.6 14.3 %copy-start.1 = (bf16[8,272,128]{2,1,0:T(8,128)(2,1)S(1)}, bf16[8,272,128]{2,1,0:T(8,128)(2,1)}, u32[]{:S(2)}) copy-start(bf16[8,272,128]{2,1,0:T(8,128)(2,1)} %copy-done) | copy-start | bytes 1671172
  68.6 14.3 %copy-start.3 = (s32[3]{0:T(128)S(1)}, s32[3]{0:T(128)}, u32[]{:S(2)}) copy-start(s32[3]{0:T(128)} %pad_add_fusion.1.refs_0_) | copy-start | bytes 40
  72.3 0.6 copy-start.10
  82.9 16.5 %copy-start.2 = (bf16[8,256,128]{2,1,0:T(8,128)(2,1)}, bf16[8,256,128]{2,1,0:T(8,128)(2,1)S(1)}, u32[]{:S(2)}) copy-start(bf16[8,256,128]{2,1,0:T(8,128)(2,1)S(1)} %all-to-all-done.2.refs_2_) | copy-start | bytes 1572868
  82.9 0.7 copy-start.4
  85.5 7.1 %collective-permute-start.7 = (f32[128,128]{1,0:T(8,128)S(1)}, f32[128,128]{1,0:T(8,128)S(1)}, u32[]{:S(2)}, u32[]{:S(2)}) collective-permute-start(f32[128,128]{1,0:T(8,128)S(1)} %get-tuple-element.70), channel_id=1, source_target_pairs={{16,0},{17,1},{18,2},{19,3},{20,4},{21,5},{22,6},{23,7},{24,8},{25... | collective-permute-start | bytes 196616 | tf_op jit(solution)/shard_map/ppermute | solution.py:745
  87.4 5.2 %collective-permute-start.8 = (f32[8,1024]{1,0:T(8,128)S(1)}, f32[8,1024]{1,0:T(8,128)S(1)}, u32[]{:S(2)}, u32[]{:S(2)}) collective-permute-start(f32[8,1024]{1,0:T(8,128)S(1)} %get-tuple-element.72), channel_id=1, source_target_pairs={{0,0},{1,16},{2,1},{3,17},{4,2},{5,18},{6,3},{7,19},{8,4},{9,20},{... | collective-permute-start | bytes 98312 | tf_op jit(solution)/shard_map/ppermute | solution.py:754
  89.3 3.3 %collective-permute-start.9 = (f32[8,1024]{1,0:T(8,128)S(1)}, f32[8,1024]{1,0:T(8,128)S(1)}, u32[]{:S(2)}, u32[]{:S(2)}) collective-permute-start(f32[8,1024]{1,0:T(8,128)S(1)} %get-tuple-element.73), channel_id=1, source_target_pairs={{0,8},{1,24},{2,9},{3,25},{4,10},{5,26},{6,11},{7,27},{8,12},{9,28... | collective-permute-start | bytes 98312 | tf_op jit(solution)/shard_map/ppermute | solution.py:755
  92.6 6.8 %copy-start.9 = (f32[128,128]{1,0:T(8,128)}, f32[128,128]{1,0:T(8,128)S(1)}, u32[]{:S(2)}) copy-start(f32[128,128]{1,0:T(8,128)S(1)} %collective-permute-done.7.refs_3_) | copy-start | bytes 196612
  92.6 21.6 %all-to-all-start.3 = ((bf16[8,48,1024]{2,1,0:T(8,128)(2,1)}), bf16[8,48,1024]{2,1,0:T(8,128)(2,1)S(1)}, u32[]{:S(2)}, u32[]{:S(2)}) async-start(bf16[8,48,1024]{2,1,0:T(8,128)(2,1)} %get-tuple-element.74), calls=%async_computation.3 | async-start | bytes 1572864 | tf_op jit(solution)/shard_map/all_to_all | solution.py:637
  109.7 4.7 %copy-start.11 = (f32[24,512]{1,0:T(8,128)S(1)}, f32[24,512]{1,0:T(8,128)}, u32[]{:S(2)}) copy-start(f32[24,512]{1,0:T(8,128)} %get-tuple-element.85) | copy-start | bytes 147460
  109.7 21.3 %copy-start.12 = (f32[8,256]{1,0:T(8,128)S(1)}, f32[8,256]{1,0:T(8,128)}, u32[]{:S(2)}) copy-start(f32[8,256]{1,0:T(8,128)} %get-tuple-element.89) | copy-start | bytes 24580
  109.7 27.3 %copy-start.18 = (bf16[256,512]{1,0:T(8,128)(2,1)S(1)}, bf16[256,512]{1,0:T(8,128)(2,1)}, u32[]{:S(2)}) copy-start(bf16[256,512]{1,0:T(8,128)(2,1)} %get-tuple-element.87) | copy-start | bytes 786436
  109.7 29.5 %copy-start.8 = (f32[256,512]{1,0:T(8,128)S(1)}, f32[256,512]{1,0:T(8,128)}, u32[]{:S(2)}) copy-start(f32[256,512]{1,0:T(8,128)} %get-tuple-element.84) | copy-start | bytes 1572868
  114.4 1.3 collective-permute-start.10
  115.7 3.7 %collective-permute-start.13 = (f32[8,512]{1,0:T(8,128)S(1)}, f32[8,512]{1,0:T(8,128)S(1)}, u32[]{:S(2)}, u32[]{:S(2)}) collective-permute-start(f32[8,512]{1,0:T(8,128)S(1)} %get-tuple-element.90), channel_id=1, source_target_pairs={{0,2},{2,0},{4,6},{6,4},{8,10},{10,8},{12,14},{14,12},{16,18},{18,... | collective-permute-start | bytes 49160 | tf_op jit(solution)/shard_map/ppermute | solution.py:792
  119.5 5.7 %collective-permute-start.14 = (f32[8,512]{1,0:T(8,128)S(1)}, f32[8,512]{1,0:T(8,128)S(1)}, u32[]{:S(2)}, u32[]{:S(2)}) collective-permute-start(f32[8,512]{1,0:T(8,128)S(1)} %add.53), channel_id=1, source_target_pairs={{0,4},{2,6},{4,0},{6,2},{8,12},{10,14},{12,8},{14,10},{16,20},{18,... | collective-permute-start | bytes 49160 | tf_op jit(solution)/shard_map/ppermute | solution.py:792
  124.1 12.9 %collective-permute-start.12 = (f32[8,512]{1,0:T(8,128)S(1)}, f32[8,512]{1,0:T(8,128)S(1)}, u32[]{:S(2)}, u32[]{:S(2)}) collective-permute-start(f32[8,512]{1,0:T(8,128)S(1)} %get-tuple-element.88), channel_id=1, source_target_pairs={{3,1},{5,3},{7,5},{9,7},{11,9},{13,11},{15,13},{17,15},{19,17},{21... | collective-permute-start | bytes 49160 | tf_op jit(solution)/shard_map/ppermute | solution.py:788
  125.1 7.6 %collective-permute-start.15 = (f32[8,512]{1,0:T(8,128)S(1)}, f32[8,512]{1,0:T(8,128)S(1)}, u32[]{:S(2)}, u32[]{:S(2)}) collective-permute-start(f32[8,512]{1,0:T(8,128)S(1)} %add.54), channel_id=1, source_target_pairs={{0,8},{2,10},{4,12},{6,14},{8,0},{10,2},{12,4},{14,6},{16,24},{18,... | collective-permute-start | bytes 49160 | tf_op jit(solution)/shard_map/ppermute | solution.py:792
  132.8 5.3 %collective-permute-start.16 = (f32[8,512]{1,0:T(8,128)S(1)}, f32[8,512]{1,0:T(8,128)S(1)}, u32[]{:S(2)}, u32[]{:S(2)}) collective-permute-start(f32[8,512]{1,0:T(8,128)S(1)} %add.55), channel_id=1, source_target_pairs={{0,16},{2,18},{4,20},{6,22},{8,24},{10,26},{12,28},{14,30},{16,0},... | collective-permute-start | bytes 49160 | tf_op jit(solution)/shard_map/ppermute | solution.py:792
  137.0 2.2 %collective-permute-start.11 = (bf16[256,512]{1,0:T(8,128)(2,1)S(1)}, bf16[256,512]{1,0:T(8,128)(2,1)S(1)}, u32[]{:S(2)}, u32[]{:S(2)}) collective-permute-start(bf16[256,512]{1,0:T(8,128)(2,1)S(1)} %copy-done.18), channel_id=1, source_target_pairs={{0,1},{1,0},{2,3},{3,2},{4,5},{5,4},{6,7},{7,6},{8,9},{9,8},{10,11... | collective-permute-start | bytes 786440 | tf_op jit(solution)/shard_map/ppermute | solution.py:787
